TPU v7x, 32 devices: a whole 2x2x4 slice. The times are simulated.
32 devices in a mesh: ctx: 8 (over z, y), head: 4 (over x, core).
Axes of the slice: x: 2, y: 2, z: 4, core: 2. Of those that a mesh axis runs over, the one named last changes fastest.
Arguments:
- x_in: bfloat16 [4096, 8192], P('ctx', 'head'), may hold values from -6 to 6
- z_in: bfloat16 [4096, 8192], P('ctx', 'head'), may hold values from -6 to 6
- bc_in: bfloat16 [4096, 256], P('ctx', 'head'), may hold values from -6 to 6
- dt: float32 [4096, 128], P('ctx', 'head'), may hold values from 4.8828125e-05 to 0.25146484, as said below
- decay_scale: float32 [128], P('head'), may hold values from 0.5 to 2
- conv_x: bfloat16 [4, 8192], P(None, 'head'), may hold values from -3 to 3
- conv_bc: bfloat16 [4, 256], P(None, 'head'), may hold values from -3 to 3
- norm_gain: bfloat16 [8192], P('head'), may hold values from 0.25 to 1.75
- doc_start: int32 [4096], P('ctx'), may hold values from 0 to 1, as said below
Outputs:
- out: bfloat16 [4096, 8192], P('ctx', 'head')
Inputs may be any that keep to these rules, and one draw needn't show every extreme that they name: doc_start[0] = 0; going round the loop, two consecutive ones are at most 512 apart; the document that holds position 0 is exactly 512 long and begins 3 (4 - 1) or more positions before the end. `dt`: positive step sizes.
All inputs are finite; a program needn't handle non-finite values.
Results may differ from a plain program's by a relative error of at most 0.0034.
Values may be sent and summed in bfloat16 or wider, within the bound.
No kernel may reach another device: no remote copies, remote signals or barrier semaphores. Data moves between devices by JAX's collectives and lax.ppermute only.
A program may use at most 64 MiB of HBM per device.

v0:
```python
import jax
import jax.numpy as jnp
from jax import lax
from jax.sharding import PartitionSpec as P

HDIM = 64
DSTATE = 128
BLOCK = 256
CONV = 4


def shifted(value, axis, steps):
    count = lax.axis_size(axis)
    pairs = [(source, (source + steps) % count) for source in range(count)]
    return lax.ppermute(value, axis, pairs)


def causal_conv(padded, taps, same):
    rows = same.shape[1]
    total = jnp.zeros((rows, taps.shape[1]), jnp.float32)
    for offset in range(taps.shape[0]):
        piece = padded[offset : offset + rows].astype(jnp.float32) * taps[offset].astype(
            jnp.float32
        )
        total = total + jnp.where(same[offset][:, None], piece, 0.0)
    return jax.nn.silu(total)


def block_pass(state, values, bmat, cmat, steps, scale, doc_ids, doc_before):
    high = lax.Precision.HIGHEST
    log_decay = jnp.cumsum(-steps * scale[None, :], axis=0)
    scores = jnp.dot(cmat, bmat.T, precision=high)
    rows = doc_ids.shape[0]
    lower = jnp.arange(rows)[:, None] >= jnp.arange(rows)[None, :]
    keep = lower & (doc_ids[:, None] == doc_ids[None, :])
    decay_t = log_decay.T
    spread = decay_t[:, :, None] - decay_t[:, None, :]
    weights = (
        jnp.where(keep[None, :, :], jnp.exp(jnp.minimum(spread, 0.0)), 0.0) * scores[None, :, :]
    )
    output = jnp.einsum("hts,shp->htp", weights, values, precision=high)
    live = doc_ids == doc_before
    carried = jnp.einsum("tn,hpn->htp", cmat, state, precision=high)
    output = output + jnp.where(live[None, :, None], jnp.exp(decay_t)[:, :, None] * carried, 0.0)
    tail = doc_ids == doc_ids[-1]
    to_end = jnp.where(tail[:, None], jnp.exp(log_decay[-1][None, :] - log_decay), 0.0)
    fresh = jnp.einsum("sh,shp,sn->hpn", to_end, values, bmat, precision=high)
    keep_state = jnp.where(doc_ids[-1] == doc_before, jnp.exp(log_decay[-1]), 0.0)
    return (keep_state[:, None, None] * state + fresh, output)


def gated_norm(output, gate, gain):
    rows, heads, width = output.shape
    mixed = output * jax.nn.silu(gate.astype(jnp.float32)).reshape(rows, heads, width)
    factor = lax.rsqrt(jnp.mean(mixed * mixed, axis=-1, keepdims=True) + 1e-05)
    normed = mixed * factor * gain.astype(jnp.float32).reshape(heads, width)
    return normed.reshape(rows, heads * width).astype(jnp.bfloat16)


def on_device(x_in, z_in, bc_in, dt, decay_scale, conv_x, conv_bc, norm_gain, doc_start):
    high = lax.Precision.HIGHEST
    positions = x_in.shape[0]
    local_heads = dt.shape[1]
    lead = CONV - 1
    doc_ids = jnp.cumsum(doc_start)
    in_last = (doc_ids[-lead:] == doc_ids[-1])[:, None]
    tail_x = jnp.where(in_last, x_in[-lead:], jnp.zeros_like(x_in[-lead:]))
    tail_bc = jnp.where(in_last, bc_in[-lead:], jnp.zeros_like(bc_in[-lead:]))
    rim_x, rim_bc = shifted((tail_x, tail_bc), "ctx", 1)
    x_pad = jnp.concatenate([rim_x, x_in], axis=0)
    bc_pad = jnp.concatenate([rim_bc, bc_in], axis=0)
    ids_pad = jnp.concatenate([jnp.zeros((lead,), jnp.int32), doc_ids], axis=0)
    same = jnp.stack([ids_pad[offset : offset + positions] == doc_ids for offset in range(CONV)])
    x_conv = causal_conv(x_pad, conv_x, same)
    bc_local = causal_conv(bc_pad, conv_bc, same).astype(jnp.bfloat16)
    bc_whole = lax.all_gather(bc_local, "head", axis=1, tiled=True).astype(jnp.float32)
    bmat = bc_whole[:, :DSTATE]
    cmat = bc_whole[:, DSTATE:]
    blocks = positions // BLOCK
    empty = jnp.zeros((local_heads, HDIM, DSTATE), jnp.float32)
    end_state = empty
    pieces = []
    for index in range(blocks):
        low = index * BLOCK
        high_end = low + BLOCK
        before = jnp.full((), -1, jnp.int32) if index == 0 else doc_ids[low - 1]
        block_values = x_conv[low:high_end].reshape(BLOCK, local_heads, HDIM)
        end_state, block_out = block_pass(
            end_state,
            block_values,
            bmat[low:high_end],
            cmat[low:high_end],
            dt[low:high_end],
            decay_scale,
            doc_ids[low:high_end],
            before,
        )
        pieces.append(block_out)
    output = jnp.concatenate(pieces, axis=1)
    device_decay = jnp.cumsum(-dt * decay_scale[None, :], axis=0)
    through = jnp.where(doc_ids[-1] == 0, jnp.exp(device_decay[-1]), 0.0)

    def relay_turn(turn, incoming):
        return shifted(through[:, None, None] * incoming + end_state, "ctx", 1)

    state_in = lax.fori_loop(0, lax.axis_size("ctx") // 8, relay_turn, empty)
    carried = jnp.einsum("tn,hpn->htp", cmat, state_in, precision=high)
    live = (doc_ids == 0)[None, :, None]
    output = output + jnp.where(live, jnp.exp(device_decay.T)[:, :, None] * carried, 0.0)
    return gated_norm(jnp.transpose(output, (1, 0, 2)), z_in, norm_gain)


def solution(mesh):
    in_specs = (
        P("ctx", "head"),
        P("ctx", "head"),
        P("ctx", "head"),
        P("ctx", "head"),
        P("head"),
        P(None, "head"),
        P(None, "head"),
        P("head"),
        P("ctx"),
    )
    out_specs = P("ctx", "head")
    return jax.shard_map(
        on_device, mesh=mesh, in_specs=in_specs, out_specs=out_specs, check_vma=False
    )
```

profile of v0, /device:TPU:0, one launch (start us, length us, event | category | flops | bytes accessed | tf_op | source)
XLA Modules:
  0.0 98.0 jit_solution(13949360632276049648)
XLA Ops:
  0.0 1.0 %reduce-window.29 = s32[4,128]{1,0:T(4,128)S(1)} reduce-window(s32[4,128]{1,0:T(4,128)} %bitcast.145, s32[]{:T(128)} %constant.12.clone.1), window={size=1x128 pad=0_0x127_0}, to_apply=%region_0.0 | reduce-window | flops 65024 | bytes 4100 | tf_op jit(solution)/shard_map/reduce-window
  3.9 3.0 %collective-permute-start = (bf16[3,64]{0,1:T(8,128)(2,1)S(1)}, bf16[3,64]{0,1:T(8,128)(2,1)S(1)}, u32[]{:S(2)}, u32[]{:S(2)}) collective-permute-start(bf16[3,64]{0,1:T(8,128)(2,1)S(1)} %slice_select_fusion.1), channel_id=1, source_target_pairs={{0,4},{4,8},{8,12},{12,16},{16,20},{20,24},{24,28},{28,0},{1,5},{5... | collective-permute-start | bytes 1160 | tf_op jit(solution)/shard_map/ppermute | solution.py:15
  7.7 1.6 %collective-permute-start.1 = (bf16[3,2048]{1,0:T(4,128)(2,1)S(1)}, bf16[3,2048]{1,0:T(4,128)(2,1)S(1)}, u32[]{:S(2)}, u32[]{:S(2)}) collective-permute-start(bf16[3,2048]{1,0:T(4,128)(2,1)S(1)} %slice_select_fusion), channel_id=1, source_target_pairs={{0,4},{4,8},{8,12},{12,16},{16,20},{20,24},{24,28},{28,0},{1,5},{5... | collective-permute-start | bytes 36872 | tf_op jit(solution)/shard_map/ppermute | solution.py:15
  18.1 1.1 %reduce-window.39 = f32[32,4,128]{2,0,1:T(8,128)S(1)} reduce-window(f32[32,4,128]{2,0,1:T(8,128)S(1)} %copy_bitcast_fusion, f32[]{:T(128)} %constant.13.clone.1), window={size=1x1x128 pad=0_0x0_0x127_0}, to_apply=%region_6.7 | reduce-window | flops 2080768 | bytes 131076 | tf_op jit(solution)/shard_map/reduce-window.6
  21.7 2.5 %broadcast_compare_fusion.1 = (pred[256]{0:T(512)(128)(4,1)S(1)}, pred[256]{0:T(512)(128)(4,1)}, pred[256]{0:T(512)(128)(4,1)S(1)}, pred[256]{0:T(512)(128)(4,1)}) fusion(s32[]{:T(128)} %bitcast.27, s32[4,128]{1,0:T(4,128)S(1)} %get-tuple-element.16, s32[]{:T(128)} %bitcast.19, s32[]{:T(128)} %bitcast.20), kind=kLoop, calls=%fused_computation.127 | loop fusion | flops 1024 | bytes 3084 | tf_op jit(solution)/shard_map/eq | solution.py:45
  27.4 4.7 %convert_multiply_fusion = f32[512,2048]{1,0:T(8,128)} fusion(bf16[512,2048]{1,0:T(8,128)(2,1)} %param.10), kind=kLoop, calls=%fused_computation.12 | loop fusion | flops 5242880 | bytes 6291456 | tf_op jit(solution)/shard_map/jit(silu)/mul | solution.py:54
  32.8 5.5 %copy.68 = f32[512,2048]{0,1:T(8,128)} copy(f32[512,2048]{1,0:T(8,128)} %convert_multiply_fusion) | data formatting | bytes 8388608 | tf_op jit(solution)/shard_map/jit(silu)/mul | solution.py:54
  38.6 5.8 %all_gather.3 = bf16[512,256]{0,1:T(8,128)(2,1)S(1)} all-gather(bf16[512,64]{0,1:T(8,128)(2,1)S(1)} %multiply_convert_fusion.1), channel_id=1, replica_groups=mesh['ctx'=8,'head'=4] {'head'}, dimensions={1}, use_global_device_ids=true | all-gather | bytes 327680 | tf_op jit(solution)/shard_map/all_gather | solution.py:76
  44.4 0.9 fusion.59
  45.3 2.3 %fusion.48 = f32[32,64,256]{2,1,0:T(8,128)} fusion(bf16[512,256]{0,1:T(8,128)(2,1)S(1)} %all_gather.3), kind=kOutput, calls=%fused_computation.49 | convolution fusion | flops 805306368 | bytes 2162688 | tf_op jit(solution)/shard_map/tn,hpn->htp/dot_general | solution.py:43
  47.6 0.9 fusion.64
  48.5 4.2 %divide_multiply_fusion = f32[512,2048]{1,0:T(8,128)S(1)} fusion(bf16[512,2048]{1,0:T(8,128)(2,1)S(1)} %copy-done.3, bf16[3,2048]{1,0:T(4,128)(2,1)S(1)} %collective-permute-done.1, f32[2048]{0:T(1024)S(1)} %bitcast.143, f32[2048]{0:T(1024)S(1)} %bitcast.144, f32[2048]{0:T(1024)S(1)} %bitcast.142, f32[2048]{0:T(1024)S(1)} %bitcast.141, ...), kind=kLoop, calls=%fused_computation.25 | loop fusion | flops 28311552 | bytes 6338048 | tf_op jit(solution)/shard_map/jit(silu)/mul | solution.py:26
  52.7 2.3 %fusion.83 = (f32[256,2048]{1,0:T(8,128)}, f32[256,2048]{1,0:T(8,128)}) fusion(f32[512,2048]{1,0:T(8,128)S(1)} %divide_multiply_fusion), kind=kLoop, calls=%fused_computation.139 | loop fusion | bytes 8388608 | tf_op jit(solution)/shard_map/slice | solution.py:87
  55.0 1.9 %copy.59 = f32[256,2048]{0,1:T(8,128)S(1)} copy(f32[256,2048]{1,0:T(8,128)} %get-tuple-element.20) | data formatting | bytes 4194304 | tf_op jit(solution)/shard_map/slice | solution.py:87
  56.9 1.7 %fusion.37 = f32[32,64,128]{2,1,0:T(8,128)S(1)} fusion(f32[256,32,64]{0,2,1:T(8,128)S(1)} %bitcast.136, f32[256,32]{0,1:T(8,128)S(1)} %exponential_select_fusion.1, f32[32]{0:T(128)} %fusion.75, bf16[512,256]{0,1:T(8,128)(2,1)S(1)} %all_gather.3), kind=kOutput, calls=%fused_computation.44 | convolution fusion | flops 806092800 | bytes 3244160 | tf_op jit(solution)/shard_map/sh,shp,sn->hpn/dot_general | solution.py:47
  58.7 2.4 %fusion.55 = f32[32,64,256]{2,1,0:T(8,128)} fusion(f32[32,64,128]{2,1,0:T(8,128)S(1)} %fusion.37, bf16[512,256]{0,1:T(8,128)(2,1)S(1)} %all_gather.3), kind=kOutput, calls=%fused_computation.68 | convolution fusion | flops 805306368 | bytes 3211264 | tf_op jit(solution)/shard_map/tn,hpn->htp/dot_general | solution.py:43
  61.0 1.9 %copy.64 = f32[256,2048]{0,1:T(8,128)S(1)} copy(f32[256,2048]{1,0:T(8,128)} %get-tuple-element.18) | data formatting | bytes 4194304 | tf_op jit(solution)/shard_map/slice | solution.py:87
  63.0 1.1 %fusion.43 = f32[32,64,128]{2,1,0:T(8,128)S(1)} fusion(f32[256,32,64]{0,2,1:T(8,128)S(1)} %bitcast.134, f32[256,32]{0,1:T(8,128)S(1)} %exponential_select_fusion, f32[32,64,128]{2,1,0:T(8,128)S(1)} %fusion.37, f32[32]{0:T(128)S(1)} %copy-done.18, f32[32]{0:T(128)S(1)} %copy-done.17, bf16[512,256]{0,1:T(8,128)(2,1)S(1)} %all_gather.3), kind=kOutput, calls=%fused_computation.46 | convolution fusion | flops 806617088 | bytes 4293632 | tf_op jit(solution)/shard_map/sh,shp,sn->hpn/dot_general | solution.py:47
  64.2 1.8 %collective-permute-start.2 = (f32[32,64,128]{2,1,0:T(8,128)S(1)}, f32[32,64,128]{2,1,0:T(8,128)S(1)}, u32[]{:S(2)}, u32[]{:S(2)}) collective-permute-start(f32[32,64,128]{2,1,0:T(8,128)S(1)} %fusion.43), channel_id=1, source_target_pairs={{0,4},{4,8},{8,12},{12,16},{16,20},{20,24},{24,28},{28,0},{1,5},{5... | collective-permute-start | bytes 3145736 | tf_op jit(solution)/shard_map/while/body/eval_jaxpr/ppermute | solution.py:15
  66.0 10.0 %bitcast_add_fusion = f32[32,256,64]{1,2,0:T(8,128)S(1)} fusion(f32[32,64,256]{2,1,0:T(8,128)S(1)} %copy-done.5, f32[256,32,64]{0,2,1:T(8,128)S(1)} %bitcast.135, f32[256,256]{1,0:T(8,128)S(1)} %copy-done.7, f32[32,256]{1,0:T(8,128)S(1)} %copy-done.11, pred[256,256]{1,0:T(8,128)(4,1)S(1)} %copy-done.10, f32[32,256]{1,0:T(8,128)S(1)} %copy-done.13, ...), kind=kOutput, calls=%fused_computation.38 | convolution fusion | flops 1620574208 | bytes 6684928 | tf_op jit(solution)/shard_map/hts,shp->htp/dot_general | solution.py:41
  76.1 10.2 %bitcast_add_fusion.1 = f32[32,256,64]{1,2,0:T(8,128)S(1)} fusion(f32[32,64,256]{2,1,0:T(8,128)S(1)} %copy-done.4, f32[256,32,64]{0,2,1:T(8,128)S(1)} %bitcast.137, f32[256,256]{1,0:T(8,128)S(1)} %copy-done.6, f32[32,256]{1,0:T(8,128)S(1)} %copy-done.12, pred[256,256]{1,0:T(8,128)(4,1)S(1)} %copy-done.9, f32[32,256]{1,0:T(8,128)S(1)} %copy-done.14, ...), kind=kOutput, calls=%fused_computation.39 | convolution fusion | flops 1620574208 | bytes 6684928 | tf_op jit(solution)/shard_map/hts,shp->htp/dot_general | solution.py:41
  86.3 6.2 %collective-permute-done.2 = f32[32,64,128]{2,1,0:T(8,128)S(1)} collective-permute-done((f32[32,64,128]{2,1,0:T(8,128)S(1)}, f32[32,64,128]{2,1,0:T(8,128)S(1)}, u32[]{:S(2)}, u32[]{:S(2)}) %collective-permute-start.2) | collective-permute-done | bytes 1048608 | tf_op jit(solution)/shard_map/while/body/eval_jaxpr/ppermute | solution.py:15
  92.5 2.5 %multiply_reduce_fusion = (f32[512,32]{0,1:T(8,128)S(1)}, f32[512,32,64]{0,2,1:T(8,128)S(1)}) fusion(f32[512,32,64]{0,2,1:T(8,128)S(1)} %bitcast.132, f32[32,64,128]{2,1,0:T(8,128)S(1)} %collective-permute-done.2, bf16[512,256]{0,1:T(8,128)(2,1)S(1)} %all_gather.3, f32[32,512]{1,0:T(8,128)S(1)} %bitcast_exponential_fusion, ...), kind=kOutput, calls=%fused_computation.21 | convolution fusion | flops 1617936384 | bytes 13894144 | tf_op jit(solution)/shard_map/tn,hpn->htp/dot_general | solution.py:107
  95.6 2.4 %copy.69 = bf16[512,2048]{1,0:T(8,128)(2,1)} copy(bf16[512,2048]{0,1:T(8,128)(2,1)S(1)} %bitcast.133) | data formatting | bytes 4194304 | tf_op jit(solution)/shard_map/convert_element_type | solution.py:57
  (90 shorter events, 17.3 us)
Async XLA Ops:
  3.9 34.5 %collective-permute-start = (bf16[3,64]{0,1:T(8,128)(2,1)S(1)}, bf16[3,64]{0,1:T(8,128)(2,1)S(1)}, u32[]{:S(2)}, u32[]{:S(2)}) collective-permute-start(bf16[3,64]{0,1:T(8,128)(2,1)S(1)} %slice_select_fusion.1), channel_id=1, source_target_pairs={{0,4},{4,8},{8,12},{12,16},{16,20},{20,24},{24,28},{28,0},{1,5},{5... | collective-permute-start | bytes 1160 | tf_op jit(solution)/shard_map/ppermute | solution.py:15
  7.7 40.8 %collective-permute-start.1 = (bf16[3,2048]{1,0:T(4,128)(2,1)S(1)}, bf16[3,2048]{1,0:T(4,128)(2,1)S(1)}, u32[]{:S(2)}, u32[]{:S(2)}) collective-permute-start(bf16[3,2048]{1,0:T(4,128)(2,1)S(1)} %slice_select_fusion), channel_id=1, source_target_pairs={{0,4},{4,8},{8,12},{12,16},{16,20},{20,24},{24,28},{28,0},{1,5},{5... | collective-permute-start | bytes 36872 | tf_op jit(solution)/shard_map/ppermute | solution.py:15
  32.8 5.5 %copy-start.15 = (bf16[2048]{0:T(1024)(128)(2,1)S(1)}, bf16[2048]{0:T(1024)(128)(2,1)}, u32[]{:S(2)}) copy-start(bf16[2048]{0:T(1024)(128)(2,1)} %param.16) | copy-start | bytes 12292
  32.8 5.6 %copy-start.8 = (bf16[512,64]{0,1:T(8,128)(2,1)S(1)}, bf16[512,64]{0,1:T(8,128)(2,1)}, u32[]{:S(2)}) copy-start(bf16[512,64]{0,1:T(8,128)(2,1)} %param.11) | copy-start | bytes 196612
  32.8 15.7 %copy-start.3 = (bf16[512,2048]{1,0:T(8,128)(2,1)S(1)}, bf16[512,2048]{1,0:T(8,128)(2,1)}, u32[]{:S(2)}) copy-start(bf16[512,2048]{1,0:T(8,128)(2,1)} %param.9) | copy-start | bytes 6291460
  56.9 4.1 %copy-start.1 = (f32[256,2048]{0,1:T(8,128)}, f32[256,2048]{0,1:T(8,128)S(1)}, u32[]{:S(2)}) copy-start(f32[256,2048]{0,1:T(8,128)S(1)} %copy.59) | copy-start | bytes 6291460
  58.6 4.4 %copy-start.17 = (f32[32]{0:T(128)S(1)}, f32[32]{0:T(128)}, u32[]{:S(2)}) copy-start(f32[32]{0:T(128)} %fusion.71) | copy-start | bytes 388
  58.7 4.4 %copy-start.18 = (f32[32]{0:T(128)S(1)}, f32[32]{0:T(128)}, u32[]{:S(2)}) copy-start(f32[32]{0:T(128)} %broadcast_select_fusion) | copy-start | bytes 388
  63.0 3.0 %copy-start.5 = (f32[32,64,256]{2,1,0:T(8,128)S(1)}, f32[32,64,256]{2,1,0:T(8,128)}, u32[]{:S(2)}) copy-start(f32[32,64,256]{2,1,0:T(8,128)} %fusion.55) | copy-start | bytes 6291460
  63.0 3.0 %copy-start.7 = (f32[256,256]{1,0:T(8,128)S(1)}, f32[256,256]{1,0:T(8,128)}, u32[]{:S(2)}) copy-start(f32[256,256]{1,0:T(8,128)} %fusion.59) | copy-start | bytes 786436
  63.0 2.9 %copy-start.10 = (pred[256,256]{1,0:T(8,128)(4,1)S(1)}, pred[256,256]{1,0:T(8,128)(4,1)}, u32[]{:S(2)}) copy-start(pred[256,256]{1,0:T(8,128)(4,1)} %get-tuple-element.50) | copy-start | bytes 196612
  63.0 2.9 %copy-start.11 = (f32[32,256]{1,0:T(8,128)S(1)}, f32[32,256]{1,0:T(8,128)}, u32[]{:S(2)}) copy-start(f32[32,256]{1,0:T(8,128)} %get-tuple-element.24) | copy-start | bytes 98308
  63.0 2.9 %copy-start.13 = (f32[32,256]{1,0:T(8,128)S(1)}, f32[32,256]{1,0:T(8,128)}, u32[]{:S(2)}) copy-start(f32[32,256]{1,0:T(8,128)} %fusion.81) | copy-start | bytes 98308
  63.0 2.9 %copy-start.20 = (pred[256]{0:T(512)(128)(4,1)S(1)}, pred[256]{0:T(512)(128)(4,1)}, u32[]{:S(2)}) copy-start(pred[256]{0:T(512)(128)(4,1)} %get-tuple-element.32) | copy-start | bytes 772
  64.2 28.3 %collective-permute-start.2 = (f32[32,64,128]{2,1,0:T(8,128)S(1)}, f32[32,64,128]{2,1,0:T(8,128)S(1)}, u32[]{:S(2)}, u32[]{:S(2)}) collective-permute-start(f32[32,64,128]{2,1,0:T(8,128)S(1)} %fusion.43), channel_id=1, source_target_pairs={{0,4},{4,8},{8,12},{12,16},{16,20},{20,24},{24,28},{28,0},{1,5},{5... | collective-permute-start | bytes 3145736 | tf_op jit(solution)/shard_map/while/body/eval_jaxpr/ppermute | solution.py:15
  66.0 10.0 %copy-start.2 = (f32[256,2048]{0,1:T(8,128)S(1)}, f32[256,2048]{0,1:T(8,128)}, u32[]{:S(2)}) copy-start(f32[256,2048]{0,1:T(8,128)} %copy-done.1) | copy-start | bytes 6291460
  66.0 10.0 %copy-start.4 = (f32[32,64,256]{2,1,0:T(8,128)S(1)}, f32[32,64,256]{2,1,0:T(8,128)}, u32[]{:S(2)}) copy-start(f32[32,64,256]{2,1,0:T(8,128)} %fusion.48) | copy-start | bytes 6291460
  66.0 10.0 %copy-start.6 = (f32[256,256]{1,0:T(8,128)S(1)}, f32[256,256]{1,0:T(8,128)}, u32[]{:S(2)}) copy-start(f32[256,256]{1,0:T(8,128)} %fusion.64) | copy-start | bytes 786436
  66.0 10.0 %copy-start.9 = (pred[256,256]{1,0:T(8,128)(4,1)S(1)}, pred[256,256]{1,0:T(8,128)(4,1)}, u32[]{:S(2)}) copy-start(pred[256,256]{1,0:T(8,128)(4,1)} %get-tuple-element.51) | copy-start | bytes 196612
  66.0 10.0 %copy-start.12 = (f32[32,256]{1,0:T(8,128)S(1)}, f32[32,256]{1,0:T(8,128)}, u32[]{:S(2)}) copy-start(f32[32,256]{1,0:T(8,128)} %get-tuple-element.25) | copy-start | bytes 98308
  66.0 10.0 %copy-start.14 = (f32[32,256]{1,0:T(8,128)S(1)}, f32[32,256]{1,0:T(8,128)}, u32[]{:S(2)}) copy-start(f32[32,256]{1,0:T(8,128)} %fusion.79) | copy-start | bytes 98308
  66.0 10.0 %copy-start.19 = (pred[256]{0:T(512)(128)(4,1)S(1)}, pred[256]{0:T(512)(128)(4,1)}, u32[]{:S(2)}) copy-start(pred[256]{0:T(512)(128)(4,1)} %get-tuple-element.34) | copy-start | bytes 772
  76.1 16.5 %copy-start = (f32[512,2048]{0,1:T(8,128)S(1)}, f32[512,2048]{0,1:T(8,128)}, u32[]{:S(2)}) copy-start(f32[512,2048]{0,1:T(8,128)} %copy.68) | copy-start | bytes 12582916
  76.1 16.5 %copy-start.16 = (pred[512]{0:T(512)(128)(4,1)S(1)}, pred[512]{0:T(512)(128)(4,1)}, u32[]{:S(2)}) copy-start(pred[512]{0:T(512)(128)(4,1)} %get-tuple-element.11) | copy-start | bytes 1540
where the time goes:
time: 98.6 us; the launch traced here: 98 us
  matrix products  32 us (32%)
  other arithmetic  27.6 us (28%)
  local copies, waits for them, and re-layouts  17.1 us (17%)
  starting transfers between devices  6.29 us (6%)
  waiting for transfers between devices  6.22 us (6%)
  blocking collectives  5.79 us (6%)
  between operations  2.89 us (3%)
    dot_general x2, matrix products, block_pass(): output = jnp.einsum('hts,shp->htp', weights, values, precision=high)  20.2 us
    ppermute x3, starting transfers between devices, shifted(): return lax.ppermute(value, axis, pairs)  6.29 us
    ppermute x3, waiting for transfers between devices, shifted(): return lax.ppermute(value, axis, pairs)  6.22 us
    slice x3, local copies, waits for them, and re-layouts, on_device(): block_values = x_conv[low:high_end].reshape(BLOCK, local_heads, HDIM)  6.14 us
    another operation x12, other arithmetic  5.84 us
    all_gather x1, blocking collectives, on_device(): lax.all_gather(bc_local, 'head', axis=1, tiled=True).astype(jnp.float32)  5.79 us
    mul x1, local copies, waits for them, and re-layouts, gated_norm(): jax.nn.silu(gate.astype(jnp.float32)).reshape(rows, heads, width)  5.5 us
    dot_general x2, matrix products, block_pass(): carried = jnp.einsum('tn,hpn->htp', cmat, state, precision=high)  4.66 us
  transfers between devices with their start and end apart: 3, of which 1 were waited for; matrix products, arithmetic and copies ran while one was open for 53% of the time, Pallas kernels for 0%

commit v1 on v0

v1 whole, which is shorter than its diff:
```python
import functools

import jax
import jax.numpy as jnp
from jax import lax
from jax.experimental import pallas as pl
from jax.experimental.pallas import tpu as pltpu
from jax.sharding import PartitionSpec as P

HDIM = 64
DSTATE = 128
CONV = 4
CHUNK = 256
WIDE = 256
GROUPS = 2
F32 = jnp.float32
BF16 = jnp.bfloat16


def shifted(value, axis, steps):
    count = lax.axis_size(axis)
    pairs = [(source, (source + steps) % count) for source in range(count)]
    return lax.ppermute(value, axis, pairs)


def crossed(value, axis, mask):
    count = lax.axis_size(axis)
    return lax.ppermute(value, axis, [(source, source ^ mask) for source in range(count)])


def iota(shape, dim):
    return lax.broadcasted_iota(jnp.int32, shape, dim)


def mm(a, b):
    return jnp.dot(a, b, preferred_element_type=F32)


def parts(value, count):
    pieces = []
    for _ in range(count):
        piece = value.astype(BF16)
        pieces.append(piece)
        value = value - piece.astype(F32)
    return jnp.concatenate(pieces, axis=1)


def spread_matrix(copies, heads, low, width):
    shape = (copies * heads, width)
    head = lax.rem(iota(shape, 0), heads)
    return jnp.where(head == (iota(shape, 1) + low) // HDIM, 1.0, 0.0).astype(BF16)


def vmem_call(kernel, outs, scratch=(), limit=24):
    spec = pl.BlockSpec(memory_space=pltpu.VMEM)
    many = isinstance(outs, (list, tuple))
    return pl.pallas_call(
        kernel,
        out_shape=outs,
        out_specs=[spec] * len(outs) if many else spec,
        scratch_shapes=list(scratch),
        compiler_params=pltpu.CompilerParams(vmem_limit_bytes=limit << 20),
    )


def tail_kernel(start_ref, x_ref, bc_ref, out_ref):
    rows = start_ref.shape[1]
    last = start_ref[0, rows - 1]
    before = start_ref[0, rows - 2]
    width = x_ref.shape[1]

    def masked(value):
        row = iota(value.shape, 0)
        low = jnp.where(last == 1, 7, jnp.where(before == 1, 6, 5))
        return jnp.where(row >= low, value.astype(F32), 0.0).astype(BF16)

    out_ref[:, :width] = masked(x_ref[...])
    bc = masked(bc_ref[...])
    out_ref[:, width:] = jnp.concatenate([bc] * (128 // bc.shape[1]), axis=1)


def prep_kernel(dt_ref, scale_ref, start_ref, fac_ref, eps_ref, rows_ref, idc_ref, idr_ref):
    heads = dt_ref.shape[1]
    square = (CHUNK, CHUNK)
    lower = jnp.where(iota(square, 0) >= iota(square, 1), 1.0, 0.0).astype(BF16)
    upper = jnp.where(iota(square, 0) <= iota(square, 1), 1.0, 0.0).astype(BF16)
    mids = []
    offset = jnp.zeros((8, 1), F32)
    for j in range(2):
        span = slice(j * CHUNK, (j + 1) * CHUNK)
        steps = parts(-dt_ref[span, :] * scale_ref[...], 3)
        sums = mm(lower, steps)
        log_decay = sums[:, :heads] + sums[:, heads : 2 * heads] + sums[:, 2 * heads :]
        mid = 0.5 * log_decay[CHUNK - 1 : CHUNK, :]
        mids.append(mid)
        fac_ref[span, :] = parts(jnp.exp(mid - log_decay), 2)
        eps_ref[span, :] = parts(jnp.exp(log_decay - mid), 2)
        starts = start_ref[:, span].astype(F32).astype(BF16)
        by_row = mm(jnp.broadcast_to(starts, (8, CHUNK)), upper) + offset
        by_col = lax.dot_general(
            lower,
            jnp.broadcast_to(starts, (128, CHUNK)),
            (((1,), (1,)), ((), ())),
            preferred_element_type=F32,
        )
        idr_ref[:, span] = by_row
        idc_ref[span, :] = by_col + offset[:1, :]
        offset = by_row[:, CHUNK - 1 : CHUNK]
    middle = idr_ref[:1, CHUNK - 1 : CHUNK]
    final = idr_ref[:1, 2 * CHUNK - 1 : 2 * CHUNK]
    keep = jnp.where(middle == final, 1.0, 0.0)
    whole = jnp.where(final == 0.0, 1.0, 0.0)
    first, second = mids
    table = jnp.concatenate(
        [
            jnp.exp(first + second),
            jnp.exp(first + 2.0 * second) * keep,
            jnp.exp(second),
            jnp.exp(first),
            jnp.exp(2.0 * first + second),
            jnp.exp(2.0 * (first + second)) * whole,
            first,
            second,
        ],
        axis=0,
    )
    rows_ref[...] = mm(parts(table, 3), spread_matrix(3, heads, 0, rows_ref.shape[1]))


def bc_kernel(bc_ref, tail_ref, taps_ref, idc_ref, out_ref, pad_ref, ids_ref):
    rows, width = bc_ref.shape
    low = tail_ref.shape[1] - 128
    pad_ref[:8, :] = tail_ref[:, low : low + width].astype(F32)
    pad_ref[8:, :] = bc_ref[...].astype(F32)
    ids_ref[:8, :] = jnp.zeros((8, 128), F32)
    ids_ref[8:, :] = idc_ref[...]
    ids = idc_ref[:, :width]
    taps = taps_ref[...].astype(F32)
    total = pad_ref[8:, :] * taps[CONV - 1 : CONV, :]
    for back in range(1, CONV):
        same = ids_ref[pl.ds(8 - back, rows), :width] == ids
        piece = pad_ref[pl.ds(8 - back, rows), :] * taps[CONV - 1 - back : CONV - back, :]
        total = total + jnp.where(same, piece, 0.0)
    value = total / (1.0 + jnp.exp(-total))
    out_ref[...] = value.T.astype(BF16)


def conv_kernel(x_ref, tail_ref, taps_ref, fac_ref, idc_ref, out_ref, pad_ref, ids_ref, mask_ref):
    rows, columns = x_ref.shape
    heads = fac_ref.shape[1] // 2
    ids_ref[:8, :] = jnp.zeros((8, 128), F32)
    ids_ref[8:, :] = idc_ref[...]
    for back in range(1, CONV):
        same = ids_ref[pl.ds(8 - back, rows), :] == idc_ref[...]
        mask_ref[back - 1] = jnp.where(same, 1.0, 0.0)

    def column_block(block, _):
        low = pl.multiple_of(block * WIDE, WIDE)
        cols = pl.ds(low, WIDE)
        spread = spread_matrix(2, heads, low, WIDE)
        taps = 0.5 * taps_ref[:, cols].astype(F32)
        pad_ref[:8, :] = tail_ref[:, cols].astype(F32)
        pad_ref[8:, :] = x_ref[:, cols].astype(F32)
        size = 128
        for low_row in range(0, rows, size):
            span = slice(low_row, low_row + size)
            half = pad_ref[pl.ds(8 + low_row, size), :] * taps[CONV - 1 : CONV, :]
            for back in range(1, CONV):
                mask = mask_ref[back - 1, span, :]
                mask = jnp.concatenate([mask] * (WIDE // 128), axis=1)
                piece = pad_ref[pl.ds(8 + low_row - back, size), :] * mask
                half = half + piece * taps[CONV - 1 - back : CONV - back, :]
            value = half + half * jnp.tanh(half)
            out_ref[span, cols] = (value * mm(fac_ref[span, :], spread)).astype(BF16)
        return 0

    lax.fori_loop(0, columns // WIDE, column_block, 0)


def pick(flag, refs):
    half = len(refs) // 2
    near = jnp.concatenate([ref[...] for ref in refs[:half]], axis=0).astype(F32)
    far = jnp.concatenate([ref[...] for ref in refs[half:]], axis=0).astype(F32)
    first = flag == 1
    return jnp.where(first, near, far), jnp.where(first, far, near)


def state_kernel(split, flag_ref, *refs):
    b_rows, _ = pick(flag_ref[0, 0], refs[:split])
    xs_ref, rows_ref, idr_ref, mid_ref, *outs = refs[split:]
    groups = len(outs)
    group_width = outs[0].shape[1]
    pieces = []
    for j in range(2):
        span = slice(j * CHUNK, (j + 1) * CHUNK)
        ids = idr_ref[:1, span]
        end = idr_ref[:1, (j + 1) * CHUNK - 1 : (j + 1) * CHUNK]
        pieces.append(jnp.where(ids == end, b_rows[:, span], 0.0).astype(BF16))
    for group in range(groups):

        def column_block(block, _):
            low = pl.multiple_of(group * group_width + block * WIDE, WIDE)
            cols = pl.ds(low, WIDE)
            first = mm(pieces[0], xs_ref[:CHUNK, cols])
            second = mm(pieces[1], xs_ref[CHUNK:, cols])
            mid_ref[:, cols] = (first * rows_ref[0:1, cols]).astype(BF16)
            end = first * rows_ref[1:2, cols] + second * rows_ref[2:3, cols]
            here = pl.ds(pl.multiple_of(block * WIDE, WIDE), WIDE)
            outs[group][:, here] = end.astype(outs[group].dtype)
            return 0

        lax.fori_loop(0, group_width // WIDE, column_block, 0)


def local_kernel(split, flag_ref, *refs):
    b_rows, c_rows = pick(flag_ref[0, 0], refs[:split])
    xs_ref, mid_ref, idc_ref, idr_ref, y_ref, live_ref, g_ref = refs[split:]
    columns = xs_ref.shape[1]
    b_rows = b_rows.astype(BF16)
    c_cols = c_rows.T
    for j in range(2):
        span = slice(j * CHUNK, (j + 1) * CHUNK)
        ids = idc_ref[span, :]
        live_ref[span, :] = jnp.where(ids == 0.0, c_cols[span, :], 0.0).astype(BF16)
        scores = mm(c_cols[span, :].astype(BF16), b_rows[:, span])
        square = (CHUNK, CHUNK)
        wide = jnp.concatenate([ids] * (CHUNK // 128), axis=1)
        keep = (iota(square, 0) >= iota(square, 1)) & (wide == idr_ref[:1, span])
        g_ref[j] = jnp.where(keep, scores, 0.0).astype(BF16)
    ids = idc_ref[CHUNK:, :]
    before = idr_ref[:1, CHUNK - 1 : CHUNK]
    carried = jnp.where(ids == before, c_cols[CHUNK:, :], 0.0).astype(BF16)

    def column_block(block, _):
        cols = pl.ds(pl.multiple_of(block * WIDE, WIDE), WIDE)
        y_ref[:CHUNK, cols] = mm(g_ref[0], xs_ref[:CHUNK, cols])
        y_ref[CHUNK:, cols] = mm(g_ref[1], xs_ref[CHUNK:, cols]) + mm(carried, mid_ref[:, cols])
        return 0

    lax.fori_loop(0, columns // WIDE, column_block, 0)


def final_kernel(group, width, *refs):
    state_ref, y_ref, live_ref, eps_ref, rows_ref, z_ref, gain_ref = refs[:7]
    out_ref = refs[-1]
    heads = eps_ref.shape[1] // 2
    square = (WIDE, WIDE)
    mean_matrix = jnp.where(
        iota(square, 0) // HDIM == iota(square, 1) // HDIM, 1.0 / HDIM, 0.0
    ).astype(BF16)

    def column_block(block, _):
        here = pl.ds(pl.multiple_of(block * WIDE, WIDE), WIDE)
        low = pl.multiple_of(group * width + block * WIDE, WIDE)
        cols = pl.ds(low, WIDE)
        spread = spread_matrix(2, heads, low, WIDE)
        gain = gain_ref[:, cols].astype(F32)
        state = state_ref[:, here]
        size = 128
        for low_row in range(0, y_ref.shape[0], size):
            span = slice(low_row, low_row + size)
            scale = rows_ref[3:4, cols] if low_row < CHUNK else rows_ref[4:5, cols]
            total = y_ref[span, cols] + mm(live_ref[span, :], state) * scale
            half = 0.5 * z_ref[span, cols].astype(F32)
            gate = half + half * jnp.tanh(half)
            mixed = total * mm(eps_ref[span, :], spread) * gate
            mean = mm((mixed * mixed).astype(BF16), mean_matrix)
            out_ref[span, cols] = (mixed * lax.rsqrt(mean + 1e-05) * gain).astype(BF16)
        return 0

    lax.fori_loop(0, width // WIDE, column_block, 0)


def on_device(x_in, z_in, bc_in, dt, decay_scale, conv_x, conv_bc, norm_gain, doc_start):
    rows, columns = x_in.shape
    heads = dt.shape[1]
    bc_width = bc_in.shape[1]
    turns = lax.axis_size("ctx") // 8
    starts = doc_start.reshape(1, rows)
    whole = lambda *_: (0, 0)
    tail = pl.pallas_call(
        tail_kernel,
        grid=(1,),
        in_specs=[
            pl.BlockSpec((1, rows), whole, memory_space=pltpu.SMEM),
            pl.BlockSpec((8, columns), lambda i: (rows // 8 - 1, 0)),
            pl.BlockSpec((8, bc_width), lambda i: (rows // 8 - 1, 0)),
        ],
        out_specs=pl.BlockSpec((8, columns + 128), whole),
        out_shape=jax.ShapeDtypeStruct((8, columns + 128), BF16),
        compiler_params=pltpu.CompilerParams(vmem_limit_bytes=4 << 20),
    )(starts, x_in, bc_in)
    rim = shifted(tail, "ctx", 1)
    fac, eps, row_table, ids_col, ids_row = vmem_call(
        prep_kernel,
        [
            jax.ShapeDtypeStruct((rows, 2 * heads), BF16),
            jax.ShapeDtypeStruct((rows, 2 * heads), BF16),
            jax.ShapeDtypeStruct((8, columns), F32),
            jax.ShapeDtypeStruct((rows, 128), F32),
            jax.ShapeDtypeStruct((8, rows), F32),
        ],
    )(dt, decay_scale.reshape(1, heads), starts)
    own = vmem_call(
        bc_kernel,
        jax.ShapeDtypeStruct((bc_width, rows), BF16),
        [pltpu.VMEM((rows + 8, bc_width), F32), pltpu.VMEM((rows + 8, 128), F32)],
    )(bc_in, rim, conv_bc, ids_col)
    split = lax.axis_size("head")
    shares = [own] + [crossed(own, "head", mask) for mask in range(1, split)]
    values = vmem_call(
        conv_kernel,
        jax.ShapeDtypeStruct((rows, columns), BF16),
        [
            pltpu.VMEM((rows + 8, WIDE), F32),
            pltpu.VMEM((rows + 8, 128), F32),
            pltpu.VMEM((CONV - 1, rows, 128), F32),
        ],
    )(x_in, rim, conv_x, fac, ids_col)
    flag = (lax.axis_index("head") < split // 2).astype(jnp.int32).reshape(1, 1)
    spec = pl.BlockSpec(memory_space=pltpu.VMEM)
    smem = pl.BlockSpec(memory_space=pltpu.SMEM)
    width = columns // GROUPS
    state_type = BF16 if turns == 1 else F32
    out_shapes = [jax.ShapeDtypeStruct((DSTATE, columns), BF16)]
    out_shapes += [jax.ShapeDtypeStruct((DSTATE, width), state_type)] * GROUPS
    middle, *ends = pl.pallas_call(
        functools.partial(state_kernel, split),
        out_shape=out_shapes,
        in_specs=[smem] + [spec] * (split + 3),
        out_specs=[spec] * (1 + GROUPS),
        compiler_params=pltpu.CompilerParams(vmem_limit_bytes=16 << 20),
    )(flag, *shares, values, row_table, ids_row)

    def relay(group, end):
        if turns == 1:
            return shifted(end, "ctx", 1)
        through = row_table[5:6, group * width : (group + 1) * width]
        turn = lambda _, incoming: shifted(through * incoming + end, "ctx", 1)
        return lax.fori_loop(0, turns, turn, jnp.zeros_like(end)).astype(BF16)

    incoming = [relay(group, end) for group, end in enumerate(ends)]
    local, live = pl.pallas_call(
        functools.partial(local_kernel, split),
        out_shape=[
            jax.ShapeDtypeStruct((rows, columns), F32),
            jax.ShapeDtypeStruct((rows, DSTATE), BF16),
        ],
        in_specs=[smem] + [spec] * (split + 4),
        out_specs=[spec] * 2,
        scratch_shapes=[pltpu.VMEM((2, CHUNK, CHUNK), BF16)],
        compiler_params=pltpu.CompilerParams(vmem_limit_bytes=16 << 20),
    )(flag, *shares, values, middle, ids_col, ids_row)
    gain = norm_gain.reshape(1, columns)
    outs = []
    for group in range(GROUPS):
        kernel = lambda *refs, g=group: final_kernel(g, width, *refs)
        args = [incoming[group], local, live, eps, row_table, z_in, gain]
        in_specs = [spec] * 7
        alias = {}
        if group > 0:
            args.append(out)
            in_specs.append(pl.BlockSpec(memory_space=pl.ANY))
            alias = {7: 0}
        out = pl.pallas_call(
            kernel,
            out_shape=jax.ShapeDtypeStruct((rows, columns), BF16),
            in_specs=in_specs,
            out_specs=spec,
            input_output_aliases=alias,
            compiler_params=pltpu.CompilerParams(vmem_limit_bytes=16 << 20),
        )(*args)
    return out


def solution(mesh):
    in_specs = (
        P("ctx", "head"),
        P("ctx", "head"),
        P("ctx", "head"),
        P("ctx", "head"),
        P("head"),
        P(None, "head"),
        P(None, "head"),
        P("head"),
        P("ctx"),
    )
    out_specs = P("ctx", "head")
    return jax.shard_map(
        on_device, mesh=mesh, in_specs=in_specs, out_specs=out_specs, check_vma=False
    )
```

time: 98.6 us -> 42.2 us (0.43)
  matrix products: 32 us -> 0 us
  other arithmetic: 27.6 us -> 0 us
  Pallas kernels: 0 us -> 19.5 us
  local copies, waits for them, and re-layouts: 17.1 us -> 3.42 us
  waiting for transfers between devices: 6.22 us -> 12.6 us
  blocking collectives: 5.79 us -> 0 us
  between operations: 2.89 us -> 0.14 us
    dot_general x9 -> x0, matrix products: 32 us -> none  [the longest x2 20.2 us: block_pass(): output = jnp.einsum('hts,shp->htp', weights, values, precision=high)]
    pallas_call x0 -> x8, Pallas kernels: none -> 19.5 us  [the longest x2 9.03 us: on_device(): pl.pallas_call(kernel, out_shape=jax.ShapeDtypeStruct((rows, columns), BF...]
    mul x6 -> x0, other arithmetic: 11.8 us -> none  [the longest x1 4.66 us: gated_norm(): jax.nn.silu(gate.astype(jnp.float32)).reshape(rows, heads, width)]
    slice x9 -> x0, local copies, waits for them, and re-layouts: 8.43 us -> none  [the longest x3 6.14 us: on_device(): block_values = x_conv[low:high_end].reshape(BLOCK, local_heads, HDIM)]
    ppermute x3, waiting for transfers between devices: 6.22 us -> 12.6 us  [shifted(): return lax.ppermute(value, axis, pairs)]
    another operation x12 -> x0, other arithmetic: 5.84 us -> none
    all_gather x1 -> x0, blocking collectives: 5.79 us -> none  [on_device(): lax.all_gather(bc_local, 'head', axis=1, tiled=True).astype(jnp.float32)]
    mul x2 -> x0, local copies, waits for them, and re-layouts: 5.58 us -> none  [the longest x1 5.5 us: gated_norm(): jax.nn.silu(gate.astype(jnp.float32)).reshape(rows, heads, width)]
  transfers between devices with their start and end apart: 3 -> 6, of which waited for: 1 -> 3; matrix products, arithmetic and copies ran while one was open for 53% -> 0% of each run, Pallas kernels for 0% -> 29%
where the time goes in v1:
time: 42.2 us; the launch traced here: 42 us
  Pallas kernels  19.5 us (46%)
  waiting for transfers between devices  12.6 us (30%)
  starting transfers between devices  6.36 us (15%)
  local copies, waits for them, and re-layouts  3.42 us (8%)
    ppermute x3, waiting for transfers between devices, shifted(): return lax.ppermute(value, axis, pairs)  12.6 us
    pallas_call x2, Pallas kernels, on_device(): pl.pallas_call(kernel, out_shape=jax.ShapeDtypeStruct((rows, columns), BF...  9.03 us
    pallas_call x1, Pallas kernels, on_device(): vmem_call(conv_kernel, jax.ShapeDtypeStruct((rows, columns), BF16), [pltp...  4.65 us
    ppermute x3, starting transfers between devices, shifted(): return lax.ppermute(value, axis, pairs)  4.41 us
    unnamed x22, local copies, waits for them, and re-layouts  3.41 us
    pallas_call x1, Pallas kernels, on_device(): pl.pallas_call(functools.partial(local_kernel, split), out_shape=[jax.Sha...  2.34 us
    ppermute x3, starting transfers between devices, crossed(): lax.ppermute(value, axis, [(source, source ^ mask) for source in range(co...  1.95 us
    pallas_call x1, Pallas kernels, on_device(): pl.pallas_call(functools.partial(state_kernel, split), out_shape=out_shap...  1.68 us
  transfers between devices with their start and end apart: 6, of which 3 were waited for; matrix products, arithmetic and copies ran while one was open for 0% of the time, Pallas kernels for 29%

profile of v1, /device:TPU:0, one launch (start us, length us, event | category | flops | bytes accessed | tf_op | source)
XLA Modules:
  0.0 42.0 jit_solution(17164467601584201454)
XLA Ops:
  0.0 1.0 %copy.13.bc_ref = bf16[512,64]{1,0:T(8,128)(2,1)S(1)} copy(bf16[512,64]{0,1:T(8,128)(2,1)} %param.11) | data formatting | bytes 131072 | tf_op args[2]
  1.0 0.0 copy-start
  1.0 1.6 %copy-done = bf16[512,2048]{1,0:T(8,128)(2,1)S(1)} copy-done((bf16[512,2048]{1,0:T(8,128)(2,1)S(1)}, bf16[512,2048]{1,0:T(8,128)(2,1)}, u32[]{:S(2)}) %copy-start) | copy-done | bytes 2097176
  2.6 0.7 %copy-done.4 = s32[512]{0:T(512)S(1)} copy-done((s32[512]{0:T(512)S(1)}, s32[512]{0:T(512)}, u32[]{:S(2)}) %copy-start.4) | copy-done | bytes 2072
  3.3 0.6 %shard_map.91 = bf16[8,2176]{1,0:T(8,128)(2,1)S(1)} custom-call(s32[1,512]{1,0:T(1,128)S(1)} %bitcast.3, bf16[512,2048]{1,0:T(8,128)(2,1)S(1)} %copy-done, bf16[512,64]{1,0:T(8,128)(2,1)S(1)} %copy.13.bc_ref), custom_call_target="tpu_custom_call" | custom-call | tf_op jit(solution)/shard_map/pallas_call | solution.py:281
  3.9 3.0 %collective-permute-start = (bf16[8,2176]{1,0:T(8,128)(2,1)S(1)}, bf16[8,2176]{1,0:T(8,128)(2,1)S(1)}, u32[]{:S(2)}, u32[]{:S(2)}) collective-permute-start(bf16[8,2176]{1,0:T(8,128)(2,1)S(1)} %shard_map.91), channel_id=1, source_target_pairs={{0,4},{4,8},{8,12},{12,16},{16,20},{20,24},{24,28},{28,0},{1,5},{5... | collective-permute-start | bytes 104456 | tf_op jit(solution)/shard_map/ppermute | solution.py:23
  6.9 0.1 copy.12.dt_ref
  7.1 0.9 %shard_map.92 = (bf16[512,64]{1,0:T(8,128)(2,1)S(1)}, bf16[512,64]{1,0:T(8,128)(2,1)S(1)}, f32[8,2048]{1,0:T(8,128)S(1)}, f32[512,128]{1,0:T(8,128)S(1)}, f32[8,512]{1,0:T(8,128)S(1)}) custom-call(f32[512,32]{1,0:T(8,128)S(1)} %copy.12.dt_ref, f32[1,32]{1,0:T(1,128)S(1)} %bitcast.5, s32[1,512]{1,0:T(1,128)S(1)} %bitcast.4), custom_call_target="tpu_custom_call" | custom-call | tf_op jit(solution)/shard_map/pallas_call | solution.py:294
  7.9 3.9 %collective-permute-done.tail_ref = bf16[8,2176]{1,0:T(8,128)(2,1)S(1)} collective-permute-done((bf16[8,2176]{1,0:T(8,128)(2,1)S(1)}, bf16[8,2176]{1,0:T(8,128)(2,1)S(1)}, u32[]{:S(2)}, u32[]{:S(2)}) %collective-permute-start) | collective-permute-done | bytes 34848 | tf_op jit(solution)/shard_map/ppermute | solution.py:23
  11.9 0.3 shard_map.93.refs_0_
  12.2 0.1 collective-permute-start.3
  12.3 1.7 %collective-permute-start.2 = (bf16[64,512]{1,0:T(8,128)(2,1)S(1)}, bf16[64,512]{1,0:T(8,128)(2,1)S(1)}, u32[]{:S(2)}, u32[]{:S(2)}) collective-permute-start(bf16[64,512]{1,0:T(8,128)(2,1)S(1)} %shard_map.93.refs_0_), channel_id=1, source_target_pairs={{0,2},{1,3},{2,0},{3,1},{4,6},{5,7},{6,4},{7,5},{8,10},{9,11},{10,... | collective-permute-start | bytes 196616 | tf_op jit(solution)/shard_map/ppermute | solution.py:28
  14.0 0.1 collective-permute-start.1
  14.1 4.6 %shard_map.94.refs_4_ = bf16[512,2048]{1,0:T(8,128)(2,1)S(1)} custom-call(bf16[512,2048]{1,0:T(8,128)(2,1)S(1)} %copy-done.1, bf16[8,2176]{1,0:T(8,128)(2,1)S(1)} %collective-permute-done.tail_ref, bf16[4,2048]{1,0:T(4,128)(2,1)S(1)} %copy-done.3, bf16[512,64]{1,0:T(8,128)(2,1)S(1)} %get-tuple-element.16.fac_ref, ...), custom_call_target="tpu_custom_call" | custom-call | tf_op jit(solution)/shard_map/pallas_call | solution.py:311
  18.8 0.0 copy-start.9
  18.8 1.7 %shard_map.95 = (bf16[128,2048]{1,0:T(8,128)(2,1)S(1)}, bf16[128,1024]{1,0:T(8,128)(2,1)S(1)}, bf16[128,1024]{1,0:T(8,128)(2,1)S(1)}) custom-call(s32[1,1]{1,0:T(1,128)} %bitcast.flag_ref, bf16[64,512]{1,0:T(8,128)(2,1)S(1)} %shard_map.93.refs_0_, bf16[64,512]{1,0:T(8,128)(2,1)S(1)} %collective-permute-done.1.refs_1_, ...), custom_call_target="tpu_custom_call" | custom-call | tf_op jit(solution)/shard_map/pallas_call | solution.py:327
  20.5 0.0 copy-start.2
  20.5 0.1 collective-permute-start.5
  20.6 1.4 %collective-permute-start.4 = (bf16[128,1024]{1,0:T(8,128)(2,1)S(1)}, bf16[128,1024]{1,0:T(8,128)(2,1)S(1)}, u32[]{:S(2)}, u32[]{:S(2)}) collective-permute-start(bf16[128,1024]{1,0:T(8,128)(2,1)S(1)} %get-tuple-element.19), channel_id=1, source_target_pairs={{0,4},{4,8},{8,12},{12,16},{16,20},{20,24},{24,28},{28,0},{1,5},{5... | collective-permute-start | bytes 786440 | tf_op jit(solution)/shard_map/ppermute | solution.py:23
  22.0 2.3 %shard_map.96 = (f32[512,2048]{1,0:T(8,128)S(1)}, bf16[512,128]{1,0:T(8,128)(2,1)S(1)}) custom-call(s32[1,1]{1,0:T(1,128)} %bitcast.flag_ref, bf16[64,512]{1,0:T(8,128)(2,1)S(1)} %shard_map.93.refs_0_, bf16[64,512]{1,0:T(8,128)(2,1)S(1)} %collective-permute-done.1.refs_1_, bf16[64,512]{1,0:T(8,128)(2,1)S(1)} %collective-permute-done.2.refs_2_, ...), custom_call_target="tpu_custom_call" | custom-call | tf_op jit(solution)/shard_map/pallas_call | solution.py:343
  24.3 8.1 %collective-permute-done.5.refs_0_ = bf16[128,1024]{1,0:T(8,128)(2,1)S(1)} collective-permute-done((bf16[128,1024]{1,0:T(8,128)(2,1)S(1)}, bf16[128,1024]{1,0:T(8,128)(2,1)S(1)}, u32[]{:S(2)}, u32[]{:S(2)}) %collective-permute-start.5) | collective-permute-done | bytes 262176 | tf_op jit(solution)/shard_map/ppermute | solution.py:23
  32.4 4.5 %shard_map.97.refs_7_ = bf16[512,2048]{1,0:T(8,128)(2,1)} custom-call(bf16[128,1024]{1,0:T(8,128)(2,1)S(1)} %collective-permute-done.5.refs_0_, f32[512,2048]{1,0:T(8,128)S(1)} %get-tuple-element.21.refs_1_, bf16[512,128]{1,0:T(8,128)(2,1)S(1)} %get-tuple-element.22.refs_2_, bf16[512,64]{1,0:T(8,128)(2,1)S(1)} %get-tuple-element.23.refs_3_, ...), custom_call_target="tpu_custom_call" | custom-call | tf_op jit(solution)/shard_map/pallas_call | solution.py:365
  36.9 0.5 %collective-permute-done.4.refs_0_ = bf16[128,1024]{1,0:T(8,128)(2,1)S(1)} collective-permute-done((bf16[128,1024]{1,0:T(8,128)(2,1)S(1)}, bf16[128,1024]{1,0:T(8,128)(2,1)S(1)}, u32[]{:S(2)}, u32[]{:S(2)}) %collective-permute-start.4) | collective-permute-done | bytes 262176 | tf_op jit(solution)/shard_map/ppermute | solution.py:23
  37.4 4.5 %shard_map.98 = bf16[512,2048]{1,0:T(8,128)(2,1)} custom-call(bf16[128,1024]{1,0:T(8,128)(2,1)S(1)} %collective-permute-done.4.refs_0_, f32[512,2048]{1,0:T(8,128)S(1)} %get-tuple-element.21.refs_1_, bf16[512,128]{1,0:T(8,128)(2,1)S(1)} %get-tuple-element.22.refs_2_, bf16[512,64]{1,0:T(8,128)(2,1)S(1)} %get-tuple-element.23.refs_3_, ...), custom_call_target="tpu_custom_call", output_to_operand_aliasing={{}: (7, {})} | custom-call | tf_op jit(solution)/shard_map/pallas_call | solution.py:365
  (19 shorter events, 0.0 us)
Async XLA Ops:
  0.0 7.0 %copy-start.5 = (s32[512]{0:T(512)S(1)}, s32[512]{0:T(512)}, u32[]{:S(2)}) copy-start(s32[512]{0:T(512)} %param.17) | copy-start | bytes 6148
  0.0 6.9 %copy-start.8 = (f32[512,32]{0,1:T(8,128)S(1)}, f32[512,32]{0,1:T(8,128)}, u32[]{:S(2)}) copy-start(f32[512,32]{0,1:T(8,128)} %param.12) | copy-start | bytes 196612
  0.0 7.1 %copy-start.7 = (f32[32]{0:T(128)S(1)}, f32[32]{0:T(128)}, u32[]{:S(2)}) copy-start(f32[32]{0:T(128)} %param.13) | copy-start | bytes 388
  0.0 11.9 %copy-start.6 = (bf16[4,64]{1,0:T(4,128)(2,1)S(1)}, bf16[4,64]{1,0:T(4,128)(2,1)}, u32[]{:S(2)}) copy-start(bf16[4,64]{1,0:T(4,128)(2,1)} %taps_ref.2) | copy-start | bytes 1540
  0.0 14.1 %copy-start.3 = (bf16[4,2048]{1,0:T(4,128)(2,1)S(1)}, bf16[4,2048]{1,0:T(4,128)(2,1)}, u32[]{:S(2)}) copy-start(bf16[4,2048]{1,0:T(4,128)(2,1)} %taps_ref.3) | copy-start | bytes 49156
  1.0 1.6 %copy-start = (bf16[512,2048]{1,0:T(8,128)(2,1)S(1)}, bf16[512,2048]{1,0:T(8,128)(2,1)}, u32[]{:S(2)}) copy-start(bf16[512,2048]{1,0:T(8,128)(2,1)} %x_ref.3) | copy-start | bytes 6291460
  2.6 0.7 %copy-start.4 = (s32[512]{0:T(512)S(1)}, s32[512]{0:T(512)}, u32[]{:S(2)}) copy-start(s32[512]{0:T(512)} %param.17) | copy-start | bytes 6148
  3.3 10.8 %copy-start.1 = (bf16[512,2048]{1,0:T(8,128)(2,1)S(1)}, bf16[512,2048]{1,0:T(8,128)(2,1)}, u32[]{:S(2)}) copy-start(bf16[512,2048]{1,0:T(8,128)(2,1)} %x_ref.3) | copy-start | bytes 6291460
  3.9 7.9 %collective-permute-start = (bf16[8,2176]{1,0:T(8,128)(2,1)S(1)}, bf16[8,2176]{1,0:T(8,128)(2,1)S(1)}, u32[]{:S(2)}, u32[]{:S(2)}) collective-permute-start(bf16[8,2176]{1,0:T(8,128)(2,1)S(1)} %shard_map.91), channel_id=1, source_target_pairs={{0,4},{4,8},{8,12},{12,16},{16,20},{20,24},{24,28},{28,0},{1,5},{5... | collective-permute-start | bytes 104456 | tf_op jit(solution)/shard_map/ppermute | solution.py:23
  12.2 6.6 %collective-permute-start.3 = (bf16[64,512]{1,0:T(8,128)(2,1)S(1)}, bf16[64,512]{1,0:T(8,128)(2,1)S(1)}, u32[]{:S(2)}, u32[]{:S(2)}) collective-permute-start(bf16[64,512]{1,0:T(8,128)(2,1)S(1)} %shard_map.93.refs_0_), channel_id=1, source_target_pairs={{0,3},{1,2},{2,1},{3,0},{4,7},{5,6},{6,5},{7,4},{8,11},{9,10},{10,... | collective-permute-start | bytes 196616 | tf_op jit(solution)/shard_map/ppermute | solution.py:28
  12.3 6.5 %collective-permute-start.2 = (bf16[64,512]{1,0:T(8,128)(2,1)S(1)}, bf16[64,512]{1,0:T(8,128)(2,1)S(1)}, u32[]{:S(2)}, u32[]{:S(2)}) collective-permute-start(bf16[64,512]{1,0:T(8,128)(2,1)S(1)} %shard_map.93.refs_0_), channel_id=1, source_target_pairs={{0,2},{1,3},{2,0},{3,1},{4,6},{5,7},{6,4},{7,5},{8,10},{9,11},{10,... | collective-permute-start | bytes 196616 | tf_op jit(solution)/shard_map/ppermute | solution.py:28
  14.0 4.8 %collective-permute-start.1 = (bf16[64,512]{1,0:T(8,128)(2,1)S(1)}, bf16[64,512]{1,0:T(8,128)(2,1)S(1)}, u32[]{:S(2)}, u32[]{:S(2)}) collective-permute-start(bf16[64,512]{1,0:T(8,128)(2,1)S(1)} %shard_map.93.refs_0_), channel_id=1, source_target_pairs={{0,1},{1,0},{2,3},{3,2},{4,5},{5,4},{6,7},{7,6},{8,9},{9,8},{10,11... | collective-permute-start | bytes 196616 | tf_op jit(solution)/shard_map/ppermute | solution.py:28
  18.8 3.2 %copy-start.9 = (bf16[2048]{0:T(1024)(128)(2,1)S(1)}, bf16[2048]{0:T(1024)(128)(2,1)}, u32[]{:S(2)}) copy-start(bf16[2048]{0:T(1024)(128)(2,1)} %param.16) | copy-start | bytes 12292
  20.5 11.9 %copy-start.2 = (bf16[512,2048]{1,0:T(8,128)(2,1)S(1)}, bf16[512,2048]{1,0:T(8,128)(2,1)}, u32[]{:S(2)}) copy-start(bf16[512,2048]{1,0:T(8,128)(2,1)} %refs_5_.3) | copy-start | bytes 6291460
  20.5 11.9 %collective-permute-start.5 = (bf16[128,1024]{1,0:T(8,128)(2,1)S(1)}, bf16[128,1024]{1,0:T(8,128)(2,1)S(1)}, u32[]{:S(2)}, u32[]{:S(2)}) collective-permute-start(bf16[128,1024]{1,0:T(8,128)(2,1)S(1)} %get-tuple-element.24), channel_id=1, source_target_pairs={{0,4},{4,8},{8,12},{12,16},{16,20},{20,24},{24,28},{28,0},{1,5},{5... | collective-permute-start | bytes 786440 | tf_op jit(solution)/shard_map/ppermute | solution.py:23
  20.6 16.9 %collective-permute-start.4 = (bf16[128,1024]{1,0:T(8,128)(2,1)S(1)}, bf16[128,1024]{1,0:T(8,128)(2,1)S(1)}, u32[]{:S(2)}, u32[]{:S(2)}) collective-permute-start(bf16[128,1024]{1,0:T(8,128)(2,1)S(1)} %get-tuple-element.19), channel_id=1, source_target_pairs={{0,4},{4,8},{8,12},{12,16},{16,20},{20,24},{24,28},{28,0},{1,5},{5... | collective-permute-start | bytes 786440 | tf_op jit(solution)/shard_map/ppermute | solution.py:23

commit v2 on v1

v2 whole, which is shorter than its diff:
```python
import functools

import jax
import jax.numpy as jnp
from jax import lax
from jax.experimental import pallas as pl
from jax.experimental.pallas import tpu as pltpu
from jax.sharding import PartitionSpec as P

HDIM = 64
DSTATE = 128
CONV = 4
CHUNK = 256
WIDE = 256
SHARES = (4, 2, 2)
F32 = jnp.float32
BF16 = jnp.bfloat16


def shifted(value, axis, steps):
    count = lax.axis_size(axis)
    pairs = [(source, (source + steps) % count) for source in range(count)]
    return lax.ppermute(value, axis, pairs)


def crossed(value, axis, mask):
    count = lax.axis_size(axis)
    return lax.ppermute(value, axis, [(source, source ^ mask) for source in range(count)])


def iota(shape, dim):
    return lax.broadcasted_iota(jnp.int32, shape, dim)


def mm(a, b):
    return jnp.dot(a, b, preferred_element_type=F32)


def mm_t(a, b):
    return lax.dot_general(a, b, (((1,), (1,)), ((), ())), preferred_element_type=F32)


def parts(value, count, axis=1):
    pieces = []
    for _ in range(count):
        piece = value.astype(BF16)
        pieces.append(piece)
        value = value - piece.astype(F32)
    return jnp.concatenate(pieces, axis=axis)


def spread_matrix(copies, heads, low, width):
    shape = (copies * heads, width)
    head = lax.rem(iota(shape, 0), heads)
    return jnp.where(head == (iota(shape, 1) + low) // HDIM, 1.0, 0.0).astype(BF16)


def call(kernel, in_specs, outs, scratch, name, out_spec=None, alias=None, limit=12):
    spec = out_spec or pl.BlockSpec(memory_space=pltpu.VMEM)
    return pl.pallas_call(
        kernel,
        out_shape=outs,
        in_specs=in_specs,
        out_specs=[spec] * len(outs) if isinstance(outs, list) else spec,
        scratch_shapes=list(scratch),
        input_output_aliases=alias or {},
        compiler_params=pltpu.CompilerParams(vmem_limit_bytes=limit << 20),
        name=name,
    )


def tail_kernel(start_ref, x_ref, bc_ref, out_ref, buffer, sem):
    rows, width = x_ref.shape
    copy = pltpu.make_async_copy(x_ref.at[pl.ds(rows - 8, 8), :], buffer, sem)
    copy.start()
    starts = start_ref[:, rows - 128 :].astype(F32)
    last = starts[:, 127:128]
    before = jnp.maximum(last, starts[:, 126:127])
    row = iota((8, 128), 0)
    kept = jnp.where(row == 5, 1.0 - before, jnp.where(row == 6, 1.0 - last, 1.0))
    kept = jnp.where(row >= 5, kept, 0.0)
    bc = bc_ref[:, rows - 128 :].astype(F32).T[120:, :]
    bc = jnp.concatenate([bc] * (128 // bc.shape[1]), axis=1)
    out_ref[:, width:] = (bc * kept).astype(BF16)
    copy.wait()
    kept = jnp.concatenate([kept] * (width // 128), axis=1)
    out_ref[:, :width] = (buffer[...].astype(F32) * kept).astype(BF16)


def prep_kernel(dt_ref, scale_ref, start_ref, fac_ref, eps_ref, rows_ref, idc_ref, idr_ref):
    heads = dt_ref.shape[0]
    square = (CHUNK, CHUNK)
    lower = jnp.where(iota(square, 0) >= iota(square, 1), 1.0, 0.0).astype(BF16)
    upper = jnp.where(iota(square, 0) <= iota(square, 1), 1.0, 0.0).astype(BF16)
    mids = []
    offset = jnp.zeros((8, 1), F32)
    for j in range(2):
        span = slice(j * CHUNK, (j + 1) * CHUNK)
        sums = mm_t(lower, parts(dt_ref[:, span], 3, 0))
        sums = sums[:, :heads] + sums[:, heads : 2 * heads] + sums[:, 2 * heads :]
        log_decay = -(sums * scale_ref[...])
        mid = 0.5 * log_decay[CHUNK - 1 : CHUNK, :]
        mids.append(mid)
        fac_ref[span, :] = parts(jnp.exp(mid - log_decay), 2)
        eps_ref[span, :] = parts(jnp.exp(log_decay - mid), 2)
        starts = start_ref[:, span].astype(F32).astype(BF16)
        by_row = mm(jnp.broadcast_to(starts, (8, CHUNK)), upper) + offset
        by_col = mm_t(lower, jnp.broadcast_to(starts, (128, CHUNK)))
        idr_ref[:, span] = by_row
        idc_ref[span, :] = by_col + offset[:1, :]
        offset = by_row[:, CHUNK - 1 : CHUNK]
    middle = idr_ref[:1, CHUNK - 1 : CHUNK]
    final = idr_ref[:1, 2 * CHUNK - 1 : 2 * CHUNK]
    keep = jnp.where(middle == final, 1.0, 0.0)
    whole = jnp.where(final == 0.0, 1.0, 0.0)
    first, second = mids
    table = jnp.concatenate(
        [
            jnp.exp(first + second),
            jnp.exp(first + 2.0 * second) * keep,
            jnp.exp(second),
            jnp.exp(first),
            jnp.exp(2.0 * first + second),
            jnp.exp(2.0 * (first + second)) * whole,
            first,
            second,
        ],
        axis=0,
    )
    rows_ref[...] = mm(parts(table, 3), spread_matrix(3, heads, 0, rows_ref.shape[1]))


def bc_kernel(bc_ref, tail_ref, taps_ref, idr_ref, out_ref):
    width, rows = bc_ref.shape
    low = tail_ref.shape[1] - 128
    tail = tail_ref[:, low : low + width].astype(F32)
    tail = jnp.concatenate([jnp.zeros((120, width), F32), tail], axis=0).T
    values = jnp.concatenate([tail, bc_ref[...].astype(F32)], axis=1)
    ids = jnp.concatenate([jnp.zeros((8, 128), F32), idr_ref[...]], axis=1)
    taps = jnp.concatenate([taps_ref[...].astype(F32)] * 2, axis=0).T
    total = values[:, 128:] * taps[:, CONV - 1 : CONV]
    for back in range(1, CONV):
        same = pltpu.roll(ids, back, 1)[:1, 128:] == ids[:1, 128:]
        kept = jnp.where(same, 1.0, 0.0)
        piece = pltpu.roll(values, back, 1)[:, 128:] * kept
        total = total + piece * taps[:, CONV - 1 - back : CONV - back]
    out_ref[...] = (total / (1.0 + jnp.exp(-total))).astype(BF16)


def conv_kernel(low, x_ref, tail_ref, taps_ref, fac_ref, idc_ref, out_ref, ids_ref, mask_ref):
    rows = x_ref.shape[0]
    heads = fac_ref.shape[1] // 2
    ids_ref[:8, :] = jnp.zeros((8, 128), F32)
    ids_ref[8:, :] = idc_ref[...]
    for back in range(1, CONV):
        same = ids_ref[pl.ds(8 - back, rows), :] == idc_ref[...]
        mask_ref[back - 1] = jnp.where(same, 1.0, 0.0)
    for block in range(out_ref.shape[1] // WIDE):
        start = low + block * WIDE
        cols = slice(start, start + WIDE)
        spread = spread_matrix(2, heads, start, WIDE)
        taps = 0.5 * taps_ref[:, cols].astype(F32)
        factor = mm(fac_ref[...], spread)
        size = 128
        for row in range(0, rows, size):
            span = slice(row, row + size)
            above = tail_ref[:, cols] if row == 0 else x_ref[row - 8 : row, cols]
            here = x_ref[span, cols].astype(F32)
            padded = jnp.concatenate([above.astype(F32), here], axis=0)
            half = here * taps[CONV - 1 : CONV, :]
            for back in range(1, CONV):
                mask = jnp.concatenate([mask_ref[back - 1, span, :]] * (WIDE // 128), axis=1)
                piece = pltpu.roll(padded, back, 0)[8:] * mask
                half = half + piece * taps[CONV - 1 - back : CONV - back, :]
            value = half + half * jnp.tanh(half)
            out_ref[span, block * WIDE : (block + 1) * WIDE] = (value * factor[span]).astype(BF16)


def pick(flag, refs):
    half = len(refs) // 2
    near = jnp.concatenate([ref[...] for ref in refs[:half]], axis=0).astype(F32)
    far = jnp.concatenate([ref[...] for ref in refs[half:]], axis=0).astype(F32)
    first = flag == 1
    return jnp.where(first, near, far), jnp.where(first, far, near)


def state_kernel(low, split, flag_ref, *refs):
    b_rows, _ = pick(flag_ref[0, 0], refs[:split])
    xs_ref, rows_ref, idr_ref, mid_ref, end_ref = refs[split:]
    pieces = []
    for j in range(2):
        span = slice(j * CHUNK, (j + 1) * CHUNK)
        ids = idr_ref[:1, span]
        end = idr_ref[:1, (j + 1) * CHUNK - 1 : (j + 1) * CHUNK]
        pieces.append(jnp.where(ids == end, b_rows[:, span], 0.0).astype(BF16))
    for block in range(xs_ref.shape[1] // WIDE):
        here = slice(block * WIDE, (block + 1) * WIDE)
        cols = slice(low + block * WIDE, low + (block + 1) * WIDE)
        first = mm(pieces[0], xs_ref[:CHUNK, here])
        second = mm(pieces[1], xs_ref[CHUNK:, here])
        mid_ref[:, here] = (first * rows_ref[0:1, cols]).astype(BF16)
        end = first * rows_ref[1:2, cols] + second * rows_ref[2:3, cols]
        end_ref[:, here] = end.astype(end_ref.dtype)


def score_kernel(split, flag_ref, *refs):
    b_rows, c_rows = pick(flag_ref[0, 0], refs[:split])
    idc_ref, idr_ref, g_ref, live_ref, carried_ref = refs[split:]
    b_rows = b_rows.astype(BF16)
    c_cols = c_rows.T
    for j in range(2):
        span = slice(j * CHUNK, (j + 1) * CHUNK)
        ids = idc_ref[span, :]
        live_ref[span, :] = jnp.where(ids == 0.0, c_cols[span, :], 0.0).astype(BF16)
        scores = mm(c_cols[span, :].astype(BF16), b_rows[:, span])
        square = (CHUNK, CHUNK)
        wide = jnp.concatenate([ids] * (CHUNK // 128), axis=1)
        keep = (iota(square, 0) >= iota(square, 1)) & (wide == idr_ref[:1, span])
        g_ref[j] = jnp.where(keep, scores, 0.0).astype(BF16)
    before = idr_ref[:1, CHUNK - 1 : CHUNK]
    ids = idc_ref[CHUNK:, :]
    carried_ref[...] = jnp.where(ids == before, c_cols[CHUNK:, :], 0.0).astype(BF16)


def local_kernel(low, xs_ref, mid_ref, g_ref, carried_ref, eps_ref, rows_ref, z_ref, y_ref, dec_ref):
    heads = eps_ref.shape[1] // 2
    for block in range(xs_ref.shape[1] // WIDE):
        start = low + block * WIDE
        here = slice(block * WIDE, (block + 1) * WIDE)
        cols = slice(start, start + WIDE)
        spread = spread_matrix(2, heads, start, WIDE)
        for j in range(2):
            span = slice(j * CHUNK, (j + 1) * CHUNK)
            y = mm(g_ref[j], xs_ref[span, here])
            if j == 1:
                y = y + mm(carried_ref[...], mid_ref[:, here])
            half = 0.5 * z_ref[span, cols].astype(F32)
            gate = (half + half * jnp.tanh(half)) * mm(eps_ref[span, :], spread)
            y_ref[span, here] = y * gate
            dec_ref[span, here] = rows_ref[3 + j : 4 + j, cols] * gate


def final_kernel(low, state_ref, y_ref, dec_ref, live_ref, gain_ref, *refs):
    out_ref, buffer, sem = refs[-3:]
    square = (WIDE, WIDE)
    same = iota(square, 0) // HDIM == iota(square, 1) // HDIM
    mean_matrix = jnp.where(same, 1.0 / HDIM, 0.0).astype(BF16)
    copies = []
    for block in range(y_ref.shape[1] // WIDE):
        here = slice(block * WIDE, (block + 1) * WIDE)
        cols = slice(low + block * WIDE, low + (block + 1) * WIDE)
        gain = gain_ref[:, cols].astype(F32)
        for j in range(2):
            span = slice(j * CHUNK, (j + 1) * CHUNK)
            mixed = y_ref[span, here] + mm(live_ref[span, :], state_ref[:, here]) * dec_ref[span, here]
            mean = mm((mixed * mixed).astype(BF16), mean_matrix)
            buffer[block, span, :] = (mixed * lax.rsqrt(mean + 1e-05) * gain).astype(BF16)
        copy = pltpu.make_async_copy(buffer.at[block], out_ref.at[:, cols], sem.at[block])
        copy.start()
        copies.append(copy)
    for copy in copies:
        copy.wait()


def on_device(x_in, z_in, bc_in, dt, decay_scale, conv_x, conv_bc, norm_gain, doc_start):
    rows, columns = x_in.shape
    heads = dt.shape[1]
    bc_width = bc_in.shape[1]
    turns = lax.axis_size("ctx") // 8
    split = lax.axis_size("head")
    starts = doc_start.reshape(1, rows)
    spec = pl.BlockSpec(memory_space=pltpu.VMEM)
    smem = pl.BlockSpec(memory_space=pltpu.SMEM)
    hbm = pl.BlockSpec(memory_space=pltpu.HBM)
    shape = jax.ShapeDtypeStruct
    bc_rows = bc_in.T
    tail = call(
        tail_kernel,
        [spec, hbm, spec],
        shape((8, columns + 128), BF16),
        [pltpu.VMEM((8, columns), BF16), pltpu.SemaphoreType.DMA],
        "tail",
    )(starts, x_in, bc_rows)
    rim = shifted(tail, "ctx", 1)
    fac, eps, table, ids_col, ids_row = call(
        prep_kernel,
        [spec] * 3,
        [
            shape((rows, 2 * heads), BF16),
            shape((rows, 2 * heads), BF16),
            shape((8, columns), F32),
            shape((rows, 128), F32),
            shape((8, rows), F32),
        ],
        (),
        "prep",
    )(dt.T, decay_scale.reshape(1, heads), starts)
    own = call(bc_kernel, [spec] * 4, shape((bc_width, rows), BF16), (), "bc")(
        bc_rows, rim, conv_bc, ids_row
    )
    shares = [own] + [crossed(own, "head", mask) for mask in range(1, split)]
    flag = (lax.axis_index("head") < split // 2).astype(jnp.int32).reshape(1, 1)
    total = sum(SHARES)
    widths = [columns * share // total for share in SHARES]
    lows = [sum(widths[:group]) for group in range(len(widths))]
    state_type = BF16 if turns == 1 else F32
    gain = norm_gain.reshape(1, columns)

    def relay(low, width, end):
        if turns == 1:
            return shifted(end, "ctx", 1)
        through = table[5:6, low : low + width]
        turn = lambda _, incoming: shifted(through * incoming + end, "ctx", 1)
        return lax.fori_loop(0, turns, turn, jnp.zeros_like(end)).astype(BF16)

    values, middles, incoming = [], [], []
    for low, width in zip(lows, widths):
        part = call(
            functools.partial(conv_kernel, low),
            [spec] * 5,
            shape((rows, width), BF16),
            [pltpu.VMEM((rows + 8, 128), F32), pltpu.VMEM((CONV - 1, rows, 128), F32)],
            f"conv{low}",
        )(x_in, rim, conv_x, fac, ids_col)
        middle, end = call(
            functools.partial(state_kernel, low, split),
            [smem] + [spec] * (split + 3),
            [shape((DSTATE, width), BF16), shape((DSTATE, width), state_type)],
            (),
            f"state{low}",
        )(flag, *shares, part, table, ids_row)
        values.append(part)
        middles.append(middle)
        incoming.append(relay(low, width, end))
    scores, live, carried = call(
        functools.partial(score_kernel, split),
        [smem] + [spec] * (split + 2),
        [shape((2, CHUNK, CHUNK), BF16), shape((rows, DSTATE), BF16), shape((CHUNK, DSTATE), BF16)],
        (),
        "score",
    )(flag, *shares, ids_col, ids_row)
    out = None
    for group, (low, width) in enumerate(zip(lows, widths)):
        mixed, decay = call(
            functools.partial(local_kernel, low),
            [spec] * 7,
            [shape((rows, width), F32)] * 2,
            (),
            f"local{low}",
        )(values[group], middles[group], scores, carried, eps, table, z_in)
        blocks = width // WIDE
        args = [incoming[group], mixed, decay, live, gain]
        in_specs = [spec] * 5
        if group > 0:
            args.append(out)
            in_specs.append(hbm)
        out = call(
            functools.partial(final_kernel, low),
            in_specs,
            shape((rows, columns), BF16),
            [pltpu.VMEM((blocks, rows, WIDE), BF16), pltpu.SemaphoreType.DMA((blocks,))],
            f"final{low}",
            hbm,
            {5: 0} if group > 0 else {},
        )(*args)
    return out


def solution(mesh):
    in_specs = (
        P("ctx", "head"),
        P("ctx", "head"),
        P("ctx", "head"),
        P("ctx", "head"),
        P("head"),
        P(None, "head"),
        P(None, "head"),
        P("head"),
        P("ctx"),
    )
    out_specs = P("ctx", "head")
    return jax.shard_map(
        on_device, mesh=mesh, in_specs=in_specs, out_specs=out_specs, check_vma=False
    )
```

time: 42.2 us -> 36.1 us (0.86)
  Pallas kernels: 19.5 us -> 12.2 us
  waiting for transfers between devices: 12.6 us -> 13.4 us
  starting transfers between devices: 6.36 us -> 6.96 us
    pallas_call x8 -> x16, Pallas kernels: 19.5 us -> 12.2 us  [the longest x3 4.15 us: on_device(): call(functools.partial(final_kernel, low), in_specs, shape((rows, columns...]
    ppermute x3, waiting for transfers between devices: 0.01 us -> 2.1 us  [crossed(): lax.ppermute(value, axis, [(source, source ^ mask) for source in range(co...]
    ppermute x3 -> x4, waiting for transfers between devices: 12.6 us -> 11.3 us  [shifted(): return lax.ppermute(value, axis, pairs)]
    ppermute x3 -> x4, starting transfers between devices: 4.41 us -> 5.02 us  [shifted(): return lax.ppermute(value, axis, pairs)]
    unnamed x22 -> x20, local copies, waits for them, and re-layouts: 3.41 us -> 3.17 us
  transfers between devices with their start and end apart: 6 -> 7, of which waited for: 3 -> 6; matrix products, arithmetic and copies ran while one was open for 0% -> 0% of each run, Pallas kernels for 29% -> 28%
where the time goes in v2:
time: 36.1 us; the launch traced here: 35.9 us
  waiting for transfers between devices  13.4 us (37%)
  Pallas kernels  12.2 us (34%)
  starting transfers between devices  6.96 us (19%)
  local copies, waits for them, and re-layouts  3.18 us (9%)
    ppermute x4, waiting for transfers between devices, shifted(): return lax.ppermute(value, axis, pairs)  11.3 us
    ppermute x4, starting transfers between devices, shifted(): return lax.ppermute(value, axis, pairs)  5.02 us
    pallas_call x3, Pallas kernels, on_device(): call(functools.partial(final_kernel, low), in_specs, shape((rows, columns...  4.15 us
    pallas_call x3, Pallas kernels, on_device(): call(functools.partial(conv_kernel, low), [spec] * 5, shape((rows, width)...  3.71 us
    unnamed x20, local copies, waits for them, and re-layouts  3.17 us
    ppermute x3, waiting for transfers between devices, crossed(): lax.ppermute(value, axis, [(source, source ^ mask) for source in range(co...  2.1 us
    ppermute x3, starting transfers between devices, crossed(): lax.ppermute(value, axis, [(source, source ^ mask) for source in range(co...  1.93 us
    pallas_call x3, Pallas kernels, on_device(): call(functools.partial(local_kernel, low), [spec] * 7, [shape((rows, widt...  1.84 us
  transfers between devices with their start and end apart: 7, of which 6 were waited for; matrix products, arithmetic and copies ran while one was open for 0% of the time, Pallas kernels for 28%

profile of v2, /device:TPU:0, one launch (start us, length us, event | category | flops | bytes accessed | tf_op | source)
XLA Modules:
  0.0 35.9 jit_solution(9747253258846850996)
XLA Ops:
  0.0 1.6 %copy-done = bf16[512,2048]{1,0:T(8,128)(2,1)S(1)} copy-done((bf16[512,2048]{1,0:T(8,128)(2,1)S(1)}, bf16[512,2048]{1,0:T(8,128)(2,1)}, u32[]{:S(2)}) %copy-start) | copy-done | bytes 2097176
  1.6 0.8 %copy-done.3 = bf16[512,64]{0,1:T(8,128)(2,1)S(1)} copy-done((bf16[512,64]{0,1:T(8,128)(2,1)S(1)}, bf16[512,64]{0,1:T(8,128)(2,1)}, u32[]{:S(2)}) %copy-start.3) | copy-done | bytes 65560
  2.5 0.7 %copy-done.6 = s32[512]{0:T(512)S(1)} copy-done((s32[512]{0:T(512)S(1)}, s32[512]{0:T(512)}, u32[]{:S(2)}) %copy-start.6) | copy-done | bytes 2072
  3.4 3.0 %collective-permute-start = (bf16[8,2176]{1,0:T(8,128)(2,1)S(1)}, bf16[8,2176]{1,0:T(8,128)(2,1)S(1)}, u32[]{:S(2)}, u32[]{:S(2)}) collective-permute-start(bf16[8,2176]{1,0:T(8,128)(2,1)S(1)} %tail.1), channel_id=1, source_target_pairs={{0,4},{4,8},{8,12},{12,16},{16,20},{20,24},{24,28},{28,0},{1,5},{5... | collective-permute-start | bytes 104456 | tf_op jit(solution)/shard_map/ppermute | solution.py:23
  6.4 0.8 %prep.1 = (bf16[512,64]{1,0:T(8,128)(2,1)S(1)}, bf16[512,64]{1,0:T(8,128)(2,1)S(1)}, f32[8,2048]{1,0:T(8,128)S(1)}, f32[512,128]{1,0:T(8,128)S(1)}, f32[8,512]{1,0:T(8,128)S(1)}) custom-call(f32[32,512]{1,0:T(8,128)S(1)} %bitcast.7, f32[1,32]{1,0:T(1,128)S(1)} %bitcast.10, s32[1,512]{1,0:T(1,128)S(1)} %bitcast.9), custom_call_target="tpu_custom_call" | custom-call | tf_op jit(solution)/shard_map/prep/pallas_call | solution.py:285
  7.2 4.2 %collective-permute-done.tail_ref = bf16[8,2176]{1,0:T(8,128)(2,1)S(1)} collective-permute-done((bf16[8,2176]{1,0:T(8,128)(2,1)S(1)}, bf16[8,2176]{1,0:T(8,128)(2,1)S(1)}, u32[]{:S(2)}, u32[]{:S(2)}) %collective-permute-start) | collective-permute-done | bytes 34848 | tf_op jit(solution)/shard_map/ppermute | solution.py:23
  11.8 1.7 %collective-permute-start.2 = (bf16[64,512]{1,0:T(8,128)(2,1)S(1)}, bf16[64,512]{1,0:T(8,128)(2,1)S(1)}, u32[]{:S(2)}, u32[]{:S(2)}) collective-permute-start(bf16[64,512]{1,0:T(8,128)(2,1)S(1)} %bc.1.refs_0_), channel_id=1, source_target_pairs={{0,2},{1,3},{2,0},{3,1},{4,6},{5,7},{6,4},{7,5},{8,10},{9,11},{10,... | collective-permute-start | bytes 196616 | tf_op jit(solution)/shard_map/ppermute | solution.py:28
  13.6 1.8 %conv0.1.refs_4_.xs_ref = bf16[512,1024]{1,0:T(8,128)(2,1)S(1)} custom-call(bf16[512,2048]{1,0:T(8,128)(2,1)S(1)} %copy-done.1, bf16[8,2176]{1,0:T(8,128)(2,1)S(1)} %collective-permute-done.tail_ref, bf16[4,2048]{1,0:T(4,128)(2,1)S(1)} %copy-done.4, bf16[512,64]{1,0:T(8,128)(2,1)S(1)} %get-tuple-element.26.fac_ref, ...), custom_call_target="tpu_custom_call" | custom-call | tf_op jit(solution)/shard_map/conv0/pallas_call | solution.py:318
  15.4 0.8 %collective-permute-done.2.refs_2_ = bf16[64,512]{1,0:T(8,128)(2,1)S(1)} collective-permute-done((bf16[64,512]{1,0:T(8,128)(2,1)S(1)}, bf16[64,512]{1,0:T(8,128)(2,1)S(1)}, u32[]{:S(2)}, u32[]{:S(2)}) %collective-permute-start.2) | collective-permute-done | bytes 65568 | tf_op jit(solution)/shard_map/ppermute | solution.py:28
  16.3 1.3 %collective-permute-done.3.refs_3_ = bf16[64,512]{1,0:T(8,128)(2,1)S(1)} collective-permute-done((bf16[64,512]{1,0:T(8,128)(2,1)S(1)}, bf16[64,512]{1,0:T(8,128)(2,1)S(1)}, u32[]{:S(2)}, u32[]{:S(2)}) %collective-permute-start.3) | collective-permute-done | bytes 65568 | tf_op jit(solution)/shard_map/ppermute | solution.py:28
  17.5 0.4 state0.1
  18.0 1.0 %conv1024.1.refs_4_.xs_ref = bf16[512,512]{1,0:T(8,128)(2,1)S(1)} custom-call(bf16[512,2048]{1,0:T(8,128)(2,1)S(1)} %copy-done.1, bf16[8,2176]{1,0:T(8,128)(2,1)S(1)} %collective-permute-done.tail_ref, bf16[4,2048]{1,0:T(4,128)(2,1)S(1)} %copy-done.4, bf16[512,64]{1,0:T(8,128)(2,1)S(1)} %get-tuple-element.26.fac_ref, ...), custom_call_target="tpu_custom_call" | custom-call | tf_op jit(solution)/shard_map/conv1024/pallas_call | solution.py:318
  19.2 1.3 %collective-permute-start.5 = (bf16[128,512]{1,0:T(8,128)(2,1)S(1)}, bf16[128,512]{1,0:T(8,128)(2,1)S(1)}, u32[]{:S(2)}, u32[]{:S(2)}) collective-permute-start(bf16[128,512]{1,0:T(8,128)(2,1)S(1)} %get-tuple-element.37), channel_id=1, source_target_pairs={{0,4},{4,8},{8,12},{12,16},{16,20},{20,24},{24,28},{28,0},{1,5},{5... | collective-permute-start | bytes 393224 | tf_op jit(solution)/shard_map/ppermute | solution.py:23
  20.5 1.0 %conv1536.1.refs_4_.xs_ref = bf16[512,512]{1,0:T(8,128)(2,1)S(1)} custom-call(bf16[512,2048]{1,0:T(8,128)(2,1)S(1)} %copy-done.1, bf16[8,2176]{1,0:T(8,128)(2,1)S(1)} %collective-permute-done.tail_ref, bf16[4,2048]{1,0:T(4,128)(2,1)S(1)} %copy-done.4, bf16[512,64]{1,0:T(8,128)(2,1)S(1)} %get-tuple-element.26.fac_ref, ...), custom_call_target="tpu_custom_call" | custom-call | tf_op jit(solution)/shard_map/conv1536/pallas_call | solution.py:318
  21.8 0.7 %collective-permute-start.4 = (bf16[128,512]{1,0:T(8,128)(2,1)S(1)}, bf16[128,512]{1,0:T(8,128)(2,1)S(1)}, u32[]{:S(2)}, u32[]{:S(2)}) collective-permute-start(bf16[128,512]{1,0:T(8,128)(2,1)S(1)} %get-tuple-element.29), channel_id=1, source_target_pairs={{0,4},{4,8},{8,12},{12,16},{16,20},{20,24},{24,28},{28,0},{1,5},{5... | collective-permute-start | bytes 393224 | tf_op jit(solution)/shard_map/ppermute | solution.py:23
  22.7 0.9 %local0.1 = (f32[512,1024]{1,0:T(8,128)S(1)}, f32[512,1024]{1,0:T(8,128)S(1)}) custom-call(bf16[512,1024]{1,0:T(8,128)(2,1)S(1)} %conv0.1.refs_4_.xs_ref, bf16[128,1024]{1,0:T(8,128)(2,1)S(1)} %get-tuple-element.42.mid_ref, bf16[2,256,256]{2,1,0:T(8,128)(2,1)S(1)} %get-tuple-element.31.g_ref, bf16[256,128]{1,0:T(8,128)(2,1)S(1)} %get-tuple-element.32.carried_ref, ...), custom_call_target="tpu_custom_call" | custom-call | tf_op jit(solution)/shard_map/local0/pallas_call | solution.py:344
  23.6 0.5 %local1024.1 = (f32[512,512]{1,0:T(8,128)S(1)}, f32[512,512]{1,0:T(8,128)S(1)}) custom-call(bf16[512,512]{1,0:T(8,128)(2,1)S(1)} %conv1024.1.refs_4_.xs_ref, bf16[128,512]{1,0:T(8,128)(2,1)S(1)} %get-tuple-element.38.mid_ref, bf16[2,256,256]{2,1,0:T(8,128)(2,1)S(1)} %get-tuple-element.31.g_ref, bf16[256,128]{1,0:T(8,128)(2,1)S(1)} %get-tuple-element.32.carried_ref, ...), custom_call_target="tpu_custom_call" | custom-call | tf_op jit(solution)/shard_map/local1024/pallas_call | solution.py:344
  24.1 0.5 %local1536.1 = (f32[512,512]{1,0:T(8,128)S(1)}, f32[512,512]{1,0:T(8,128)S(1)}) custom-call(bf16[512,512]{1,0:T(8,128)(2,1)S(1)} %conv1536.1.refs_4_.xs_ref, bf16[128,512]{1,0:T(8,128)(2,1)S(1)} %get-tuple-element.30.mid_ref, bf16[2,256,256]{2,1,0:T(8,128)(2,1)S(1)} %get-tuple-element.31.g_ref, bf16[256,128]{1,0:T(8,128)(2,1)S(1)} %get-tuple-element.32.carried_ref, ...), custom_call_target="tpu_custom_call" | custom-call | tf_op jit(solution)/shard_map/local1536/pallas_call | solution.py:344
  24.6 5.2 %collective-permute-done.6.state_ref = bf16[128,1024]{1,0:T(8,128)(2,1)S(1)} collective-permute-done((bf16[128,1024]{1,0:T(8,128)(2,1)S(1)}, bf16[128,1024]{1,0:T(8,128)(2,1)S(1)}, u32[]{:S(2)}, u32[]{:S(2)}) %collective-permute-start.6) | collective-permute-done | bytes 262176 | tf_op jit(solution)/shard_map/ppermute | solution.py:23
  29.8 1.6 %final0.1.refs_0_ = bf16[512,2048]{1,0:T(8,128)(2,1)} custom-call(bf16[128,1024]{1,0:T(8,128)(2,1)S(1)} %collective-permute-done.6.state_ref, f32[512,1024]{1,0:T(8,128)S(1)} %get-tuple-element.43.y_ref, f32[512,1024]{1,0:T(8,128)S(1)} %get-tuple-element.44.dec_ref, bf16[512,128]{1,0:T(8,128)(2,1)S(1)} %get-tuple-element.36.live_ref, ...), custom_call_target="tpu_custom_call" | custom-call | tf_op jit(solution)/shard_map/final0/pallas_call | solution.py:357
  31.4 1.2 %collective-permute-done.5.state_ref = bf16[128,512]{1,0:T(8,128)(2,1)S(1)} collective-permute-done((bf16[128,512]{1,0:T(8,128)(2,1)S(1)}, bf16[128,512]{1,0:T(8,128)(2,1)S(1)}, u32[]{:S(2)}, u32[]{:S(2)}) %collective-permute-start.5) | collective-permute-done | bytes 131104 | tf_op jit(solution)/shard_map/ppermute | solution.py:23
  32.6 1.3 %final1024.1.refs_0_ = bf16[512,2048]{1,0:T(8,128)(2,1)} custom-call(bf16[128,512]{1,0:T(8,128)(2,1)S(1)} %collective-permute-done.5.state_ref, f32[512,512]{1,0:T(8,128)S(1)} %get-tuple-element.39.y_ref, f32[512,512]{1,0:T(8,128)S(1)} %get-tuple-element.40.dec_ref, bf16[512,128]{1,0:T(8,128)(2,1)S(1)} %get-tuple-element.36.live_ref, ...), custom_call_target="tpu_custom_call", output_to_operand_aliasing={{}: (5, {})} | custom-call | tf_op jit(solution)/shard_map/final1024/pallas_call | solution.py:357
  33.9 0.8 %collective-permute-done.4.state_ref = bf16[128,512]{1,0:T(8,128)(2,1)S(1)} collective-permute-done((bf16[128,512]{1,0:T(8,128)(2,1)S(1)}, bf16[128,512]{1,0:T(8,128)(2,1)S(1)}, u32[]{:S(2)}, u32[]{:S(2)}) %collective-permute-start.4) | collective-permute-done | bytes 131104 | tf_op jit(solution)/shard_map/ppermute | solution.py:23
  34.6 1.3 %final1536.1 = bf16[512,2048]{1,0:T(8,128)(2,1)} custom-call(bf16[128,512]{1,0:T(8,128)(2,1)S(1)} %collective-permute-done.4.state_ref, f32[512,512]{1,0:T(8,128)S(1)} %get-tuple-element.34.y_ref, f32[512,512]{1,0:T(8,128)S(1)} %get-tuple-element.35.dec_ref, bf16[512,128]{1,0:T(8,128)(2,1)S(1)} %get-tuple-element.36.live_ref, ...), custom_call_target="tpu_custom_call", output_to_operand_aliasing={{}: (5, {})} | custom-call | tf_op jit(solution)/shard_map/final1536/pallas_call | solution.py:357
  (27 shorter events, 1.7 us)
Async XLA Ops:
  0.0 6.4 %copy-start.8 = (f32[32]{0:T(128)S(1)}, f32[32]{0:T(128)}, u32[]{:S(2)}) copy-start(f32[32]{0:T(128)} %param.13) | copy-start | bytes 388
  0.0 11.4 %copy-start.7 = (bf16[4,64]{1,0:T(4,128)(2,1)S(1)}, bf16[4,64]{1,0:T(4,128)(2,1)}, u32[]{:S(2)}) copy-start(bf16[4,64]{1,0:T(4,128)(2,1)} %taps_ref.4) | copy-start | bytes 1540
  0.0 1.6 %copy-start = (bf16[512,2048]{1,0:T(8,128)(2,1)S(1)}, bf16[512,2048]{1,0:T(8,128)(2,1)}, u32[]{:S(2)}) copy-start(bf16[512,2048]{1,0:T(8,128)(2,1)} %x_ref.7) | copy-start | bytes 6291460
  1.6 0.8 %copy-start.3 = (bf16[512,64]{0,1:T(8,128)(2,1)S(1)}, bf16[512,64]{0,1:T(8,128)(2,1)}, u32[]{:S(2)}) copy-start(bf16[512,64]{0,1:T(8,128)(2,1)} %param.11) | copy-start | bytes 196612
  2.5 0.7 %copy-start.6 = (s32[512]{0:T(512)S(1)}, s32[512]{0:T(512)}, u32[]{:S(2)}) copy-start(s32[512]{0:T(512)} %param.17) | copy-start | bytes 6148
  3.1 3.3 %copy-start.5 = (f32[512,32]{0,1:T(8,128)S(1)}, f32[512,32]{0,1:T(8,128)}, u32[]{:S(2)}) copy-start(f32[512,32]{0,1:T(8,128)} %param.12) | copy-start | bytes 196612
  3.1 10.5 %copy-start.1 = (bf16[512,2048]{1,0:T(8,128)(2,1)S(1)}, bf16[512,2048]{1,0:T(8,128)(2,1)}, u32[]{:S(2)}) copy-start(bf16[512,2048]{1,0:T(8,128)(2,1)} %x_ref.7) | copy-start | bytes 6291460
  3.1 10.5 %copy-start.4 = (bf16[4,2048]{1,0:T(4,128)(2,1)S(1)}, bf16[4,2048]{1,0:T(4,128)(2,1)}, u32[]{:S(2)}) copy-start(bf16[4,2048]{1,0:T(4,128)(2,1)} %taps_ref.7) | copy-start | bytes 49156
  3.4 8.0 %collective-permute-start = (bf16[8,2176]{1,0:T(8,128)(2,1)S(1)}, bf16[8,2176]{1,0:T(8,128)(2,1)S(1)}, u32[]{:S(2)}, u32[]{:S(2)}) collective-permute-start(bf16[8,2176]{1,0:T(8,128)(2,1)S(1)} %tail.1), channel_id=1, source_target_pairs={{0,4},{4,8},{8,12},{12,16},{16,20},{20,24},{24,28},{28,0},{1,5},{5... | collective-permute-start | bytes 104456 | tf_op jit(solution)/shard_map/ppermute | solution.py:23
  11.7 3.7 %collective-permute-start.1 = (bf16[64,512]{1,0:T(8,128)(2,1)S(1)}, bf16[64,512]{1,0:T(8,128)(2,1)S(1)}, u32[]{:S(2)}, u32[]{:S(2)}) collective-permute-start(bf16[64,512]{1,0:T(8,128)(2,1)S(1)} %bc.1.refs_0_), channel_id=1, source_target_pairs={{0,1},{1,0},{2,3},{3,2},{4,5},{5,4},{6,7},{7,6},{8,9},{9,8},{10,11... | collective-permute-start | bytes 196616 | tf_op jit(solution)/shard_map/ppermute | solution.py:28
  11.8 4.5 %collective-permute-start.2 = (bf16[64,512]{1,0:T(8,128)(2,1)S(1)}, bf16[64,512]{1,0:T(8,128)(2,1)S(1)}, u32[]{:S(2)}, u32[]{:S(2)}) collective-permute-start(bf16[64,512]{1,0:T(8,128)(2,1)S(1)} %bc.1.refs_0_), channel_id=1, source_target_pairs={{0,2},{1,3},{2,0},{3,1},{4,6},{5,7},{6,4},{7,5},{8,10},{9,11},{10,... | collective-permute-start | bytes 196616 | tf_op jit(solution)/shard_map/ppermute | solution.py:28
  13.5 4.0 %collective-permute-start.3 = (bf16[64,512]{1,0:T(8,128)(2,1)S(1)}, bf16[64,512]{1,0:T(8,128)(2,1)S(1)}, u32[]{:S(2)}, u32[]{:S(2)}) collective-permute-start(bf16[64,512]{1,0:T(8,128)(2,1)S(1)} %bc.1.refs_0_), channel_id=1, source_target_pairs={{0,3},{1,2},{2,1},{3,0},{4,7},{5,6},{6,5},{7,4},{8,11},{9,10},{10,... | collective-permute-start | bytes 196616 | tf_op jit(solution)/shard_map/ppermute | solution.py:28
  17.9 11.9 %collective-permute-start.6 = (bf16[128,1024]{1,0:T(8,128)(2,1)S(1)}, bf16[128,1024]{1,0:T(8,128)(2,1)S(1)}, u32[]{:S(2)}, u32[]{:S(2)}) collective-permute-start(bf16[128,1024]{1,0:T(8,128)(2,1)S(1)} %get-tuple-element.41), channel_id=1, source_target_pairs={{0,4},{4,8},{8,12},{12,16},{16,20},{20,24},{24,28},{28,0},{1,5},{5... | collective-permute-start | bytes 786440 | tf_op jit(solution)/shard_map/ppermute | solution.py:23
  19.2 3.2 %copy-start.9 = (bf16[2048]{0:T(1024)(128)(2,1)S(1)}, bf16[2048]{0:T(1024)(128)(2,1)}, u32[]{:S(2)}) copy-start(bf16[2048]{0:T(1024)(128)(2,1)} %param.16) | copy-start | bytes 12292
  19.2 3.5 %copy-start.2 = (bf16[512,2048]{1,0:T(8,128)(2,1)S(1)}, bf16[512,2048]{1,0:T(8,128)(2,1)}, u32[]{:S(2)}) copy-start(bf16[512,2048]{1,0:T(8,128)(2,1)} %z_ref.5) | copy-start | bytes 6291460
  19.2 13.4 %collective-permute-start.5 = (bf16[128,512]{1,0:T(8,128)(2,1)S(1)}, bf16[128,512]{1,0:T(8,128)(2,1)S(1)}, u32[]{:S(2)}, u32[]{:S(2)}) collective-permute-start(bf16[128,512]{1,0:T(8,128)(2,1)S(1)} %get-tuple-element.37), channel_id=1, source_target_pairs={{0,4},{4,8},{8,12},{12,16},{16,20},{20,24},{24,28},{28,0},{1,5},{5... | collective-permute-start | bytes 393224 | tf_op jit(solution)/shard_map/ppermute | solution.py:23
  21.8 12.9 %collective-permute-start.4 = (bf16[128,512]{1,0:T(8,128)(2,1)S(1)}, bf16[128,512]{1,0:T(8,128)(2,1)S(1)}, u32[]{:S(2)}, u32[]{:S(2)}) collective-permute-start(bf16[128,512]{1,0:T(8,128)(2,1)S(1)} %get-tuple-element.29), channel_id=1, source_target_pairs={{0,4},{4,8},{8,12},{12,16},{16,20},{20,24},{24,28},{28,0},{1,5},{5... | collective-permute-start | bytes 393224 | tf_op jit(solution)/shard_map/ppermute | solution.py:23

commit v3 on v2

--- a/solution.py
+++ b/solution.py
@@ -12,7 +12,8 @@
 CONV = 4
 CHUNK = 256
 WIDE = 256
-SHARES = (4, 2, 2)
+SHARES = (2, 4, 2)
+EDGE = 16
 F32 = jnp.float32
 BF16 = jnp.bfloat16
 
@@ -69,25 +70,48 @@
     )
 
 
-def tail_kernel(start_ref, x_ref, bc_ref, out_ref, buffer, sem):
-    rows, width = x_ref.shape
-    copy = pltpu.make_async_copy(x_ref.at[pl.ds(rows - 8, 8), :], buffer, sem)
-    copy.start()
+def rim_rows(columns, split, width):
+    return -(-3 * (columns + 128 * split) // width // 16) * 16
+
+
+def rim_block(x_ref, start_ref, shares, width):
+    rows, columns = x_ref.shape
+    total = rim_rows(columns, len(shares), width)
     starts = start_ref[:, rows - 128 :].astype(F32)
     last = starts[:, 127:128]
     before = jnp.maximum(last, starts[:, 126:127])
     row = iota((8, 128), 0)
     kept = jnp.where(row == 5, 1.0 - before, jnp.where(row == 6, 1.0 - last, 1.0))
     kept = jnp.where(row >= 5, kept, 0.0)
-    bc = bc_ref[:, rows - 128 :].astype(F32).T[120:, :]
-    bc = jnp.concatenate([bc] * (128 // bc.shape[1]), axis=1)
-    out_ref[:, width:] = (bc * kept).astype(BF16)
-    copy.wait()
     kept = jnp.concatenate([kept] * (width // 128), axis=1)
-    out_ref[:, :width] = (buffer[...].astype(F32) * kept).astype(BF16)
-
-
-def prep_kernel(dt_ref, scale_ref, start_ref, fac_ref, eps_ref, rows_ref, idc_ref, idr_ref):
+    row = iota((8, width), 0)
+    block = jnp.zeros((total, width), F32)
+    below = jnp.zeros((total - 8, width), F32)
+    slot = 0
+    for low in range(0, columns, width):
+        piece = x_ref[rows - 8 :, low : low + width].astype(F32) * kept
+        piece = jnp.concatenate([piece, below], axis=0)
+        block = block + pltpu.roll(piece, (slot - 5) % total, 0)
+        slot += 3
+    count = width // 128
+    for index in range(0, len(shares), count):
+        piece = [share[share.shape[0] - 8 :, :128] for share in shares[index : index + count]]
+        piece = jnp.concatenate(piece, axis=1).astype(F32)
+        piece = jnp.where((row >= 3) & (row < 6), piece, 0.0)
+        piece = jnp.concatenate([piece, below], axis=0)
+        block = block + pltpu.roll(piece, (slot - 3) % total, 0)
+        slot += 3
+    return block.astype(BF16)
+
+
+def tail_kernel(x_ref, start_ref, *refs):
+    refs[-1][...] = rim_block(x_ref, start_ref, refs[:-1], refs[-1].shape[1])
+
+
+def prep_kernel(dt_ref, scale_ref, start_ref, x_hbm, *refs):
+    fac_ref, eps_ref, rows_ref, idc_ref, idr_ref, x_ref, sem = refs
+    copy = pltpu.make_async_copy(x_hbm, x_ref, sem)
+    copy.start()
     heads = dt_ref.shape[0]
     square = (CHUNK, CHUNK)
     lower = jnp.where(iota(square, 0) >= iota(square, 1), 1.0, 0.0).astype(BF16)
@@ -128,26 +152,97 @@
         axis=0,
     )
     rows_ref[...] = mm(parts(table, 3), spread_matrix(3, heads, 0, rows_ref.shape[1]))
-
-
-def bc_kernel(bc_ref, tail_ref, taps_ref, idr_ref, out_ref):
+    copy.wait()
+
+
+def bc_kernel(*refs):
+    sources, (out_ref, *copied), (bc_ref, taps_ref, sems) = refs[:6], refs[6:11], refs[11:]
     width, rows = bc_ref.shape
-    low = tail_ref.shape[1] - 128
-    tail = tail_ref[:, low : low + width].astype(F32)
-    tail = jnp.concatenate([jnp.zeros((120, width), F32), tail], axis=0).T
-    values = jnp.concatenate([tail, bc_ref[...].astype(F32)], axis=1)
-    ids = jnp.concatenate([jnp.zeros((8, 128), F32), idr_ref[...]], axis=1)
+    start_ref = copied[0]
+    copies = [
+        pltpu.make_async_copy(source, target, sems.at[index])
+        for index, (source, target) in enumerate(zip(sources, [bc_ref, taps_ref, *copied]))
+    ]
+    for copy in copies:
+        copy.start()
+    for copy in copies[:3]:
+        copy.wait()
+    values = jnp.concatenate([jnp.zeros((width, 128), F32), bc_ref[...].astype(F32)], axis=1)
+    starts = jnp.broadcast_to(start_ref[...].astype(F32), (8, rows))
+    open_ = jnp.concatenate([jnp.ones((8, 128), F32), 1.0 - starts], axis=1)
     taps = jnp.concatenate([taps_ref[...].astype(F32)] * 2, axis=0).T
     total = values[:, 128:] * taps[:, CONV - 1 : CONV]
+    kept = open_
     for back in range(1, CONV):
-        same = pltpu.roll(ids, back, 1)[:1, 128:] == ids[:1, 128:]
-        kept = jnp.where(same, 1.0, 0.0)
-        piece = pltpu.roll(values, back, 1)[:, 128:] * kept
+        if back > 1:
+            kept = kept * pltpu.roll(open_, back - 1, 1)
+        piece = pltpu.roll(values, back, 1)[:, 128:] * kept[:1, 128:]
         total = total + piece * taps[:, CONV - 1 - back : CONV - back]
-    out_ref[...] = (total / (1.0 + jnp.exp(-total))).astype(BF16)
-
-
-def conv_kernel(low, x_ref, tail_ref, taps_ref, fac_ref, idc_ref, out_ref, ids_ref, mask_ref):
+    out_ref[:width, :] = (total / (1.0 + jnp.exp(-total))).astype(BF16)
+    lane = iota((1, 128), 1)
+    last = open_[:1, rows:]
+    near, far = last[:, 127:128], last[:, 126:127]
+    kept = jnp.where(lane == 125, near * far, jnp.where(lane == 126, near, 1.0))
+    ends = jnp.where(lane >= 125, kept, 0.0) * values[:, rows:]
+    after = jnp.zeros((width, 128), F32)
+    for back in range(1, CONV):
+        after = after + pltpu.roll(ends, back, 1) * taps[:, CONV - 1 - back : CONV - back]
+    table = jnp.where(lane < 3, total[:, :128], pltpu.roll(after, 3, 1))
+    table = jnp.where(lane < 6, table, 0.0).T[:8, :]
+    high = table.astype(BF16)
+    low = (table - high.astype(F32)).astype(BF16)
+    gap = [jnp.zeros((8, 64 - width), BF16)] if width < 64 else []
+    out_ref[width:, :128] = jnp.concatenate([high, *gap, low, *gap], axis=1)
+    out_ref[width:, 128:] = jnp.zeros((8, rows - 128), BF16)
+    for copy in copies[3:]:
+        copy.wait()
+
+
+def fix_kernel(x_ref, rim_ref, taps_ref, fac_ref, idc_ref, *refs):
+    shares, bc_ref, xs_ref = refs[:-2], refs[-2], refs[-1]
+    columns = x_ref.shape[1]
+    depth = rim_rows(columns, len(shares), rim_ref.shape[1])
+    base = rim_ref.shape[0] - depth
+
+    def rim(low, size, row):
+        slot, lane = low // rim_ref.shape[1], low % rim_ref.shape[1]
+        block = rim_ref[base:, lane : lane + size].astype(F32)
+        return pltpu.roll(block, (row - 3 * slot) % depth, 0)[:8]
+
+    heads = fac_ref.shape[1] // 2
+    width = shares[0].shape[0] - 8
+    live = idc_ref[:8, :] == 0.0
+    lane = iota((width, 128), 1)
+    for index, share in enumerate(shares):
+        low = columns + index * 128
+        own = share[width:, :128].astype(F32)
+        after = jnp.where(live, rim(low, 128, 0), 0.0)
+        total = own + after
+        total = total + pltpu.roll(total, 64, 1)
+        value = total / (1.0 + jnp.exp(-total))
+        value = jnp.concatenate([value, jnp.zeros((120, 128), F32)], axis=0).T[:width, :]
+        first = jnp.where(lane < 3, value, share[:width, :128].astype(F32))
+        bc_ref[index * width : (index + 1) * width, :] = first.astype(BF16)
+    ids = jnp.concatenate([jnp.zeros((8, 128), F32), idc_ref[:EDGE, :]], axis=0)
+    masks = []
+    for back in range(1, CONV):
+        same = pltpu.roll(ids, back, 0)[8:] == ids[8:]
+        masks.append(jnp.concatenate([jnp.where(same, 1.0, 0.0)] * (WIDE // 128), axis=1))
+    for low in range(0, columns, WIDE):
+        cols = slice(low, low + WIDE)
+        taps = 0.5 * taps_ref[:, cols].astype(F32)
+        above = rim(low, WIDE, 5)
+        padded = jnp.concatenate([above, x_ref[:EDGE, cols].astype(F32)], axis=0)
+        half = padded[8:] * taps[CONV - 1 : CONV, :]
+        for back in range(1, CONV):
+            piece = pltpu.roll(padded, back, 0)[8:] * masks[back - 1]
+            half = half + piece * taps[CONV - 1 - back : CONV - back, :]
+        value = half + half * jnp.tanh(half)
+        factor = mm(fac_ref[:EDGE, :], spread_matrix(2, heads, low, WIDE))
+        xs_ref[:, cols] = (value * factor).astype(BF16)
+
+
+def conv_kernel(low, x_ref, taps_ref, fac_ref, idc_ref, out_ref, ids_ref, mask_ref):
     rows = x_ref.shape[0]
     heads = fac_ref.shape[1] // 2
     ids_ref[:8, :] = jnp.zeros((8, 128), F32)
@@ -164,9 +259,12 @@
         size = 128
         for row in range(0, rows, size):
             span = slice(row, row + size)
-            above = tail_ref[:, cols] if row == 0 else x_ref[row - 8 : row, cols]
             here = x_ref[span, cols].astype(F32)
-            padded = jnp.concatenate([above.astype(F32), here], axis=0)
+            if row == 0:
+                above = jnp.zeros((8, WIDE), F32)
+            else:
+                above = x_ref[row - 8 : row, cols].astype(F32)
+            padded = jnp.concatenate([above, here], axis=0)
             half = here * taps[CONV - 1 : CONV, :]
             for back in range(1, CONV):
                 mask = jnp.concatenate([mask_ref[back - 1, span, :]] * (WIDE // 128), axis=1)
@@ -176,36 +274,51 @@
             out_ref[span, block * WIDE : (block + 1) * WIDE] = (value * factor[span]).astype(BF16)
 
 
-def pick(flag, refs):
+def pick(flag, refs, first=None):
     half = len(refs) // 2
-    near = jnp.concatenate([ref[...] for ref in refs[:half]], axis=0).astype(F32)
-    far = jnp.concatenate([ref[...] for ref in refs[half:]], axis=0).astype(F32)
-    first = flag == 1
-    return jnp.where(first, near, far), jnp.where(first, far, near)
-
-
-def state_kernel(low, split, flag_ref, *refs):
-    b_rows, _ = pick(flag_ref[0, 0], refs[:split])
-    xs_ref, rows_ref, idr_ref, mid_ref, end_ref = refs[split:]
-    pieces = []
-    for j in range(2):
-        span = slice(j * CHUNK, (j + 1) * CHUNK)
-        ids = idr_ref[:1, span]
-        end = idr_ref[:1, (j + 1) * CHUNK - 1 : (j + 1) * CHUNK]
-        pieces.append(jnp.where(ids == end, b_rows[:, span], 0.0).astype(BF16))
+    width = refs[0].shape[0] - 8
+    near = jnp.concatenate([ref[:width, :] for ref in refs[:half]], axis=0).astype(F32)
+    far = jnp.concatenate([ref[:width, :] for ref in refs[half:]], axis=0).astype(F32)
+    if first is not None:
+        edge = first[...].astype(F32)
+        near = jnp.concatenate([edge[:DSTATE], near[:, 128:]], axis=1)
+        far = jnp.concatenate([edge[DSTATE:], far[:, 128:]], axis=1)
+    own = flag == 1
+    return jnp.where(own, near, far), jnp.where(own, far, near)
+
+
+def ending(b_rows, idr_ref, j):
+    span = slice(j * CHUNK, (j + 1) * CHUNK)
+    end = idr_ref[:1, (j + 1) * CHUNK - 1 : (j + 1) * CHUNK]
+    return jnp.where(idr_ref[:1, span] == end, b_rows[:, span], 0.0).astype(BF16)
+
+
+def opening(xs_ref, edge_ref, here, cols):
+    return jnp.concatenate([edge_ref[:, cols], xs_ref[EDGE:CHUNK, here]], axis=0)
+
+
+def state_kernel(low, split, carries, flag_ref, *refs):
+    xs_ref, rows_ref, idr_ref, *edges, end_ref = refs[split:]
+    if carries:
+        x_ref, start_ref = edges
+        edges = []
+        end_ref[DSTATE:, :] = rim_block(x_ref, start_ref, refs[:split], end_ref.shape[1])
+    b_rows, _ = pick(flag_ref[0, 0], refs[:split], edges[0] if edges else None)
+    pieces = [ending(b_rows, idr_ref, j) for j in range(2)]
     for block in range(xs_ref.shape[1] // WIDE):
         here = slice(block * WIDE, (block + 1) * WIDE)
         cols = slice(low + block * WIDE, low + (block + 1) * WIDE)
-        first = mm(pieces[0], xs_ref[:CHUNK, here])
+        values = opening(xs_ref, edges[1], here, cols) if edges else xs_ref[:CHUNK, here]
+        first = mm(pieces[0], values)
         second = mm(pieces[1], xs_ref[CHUNK:, here])
-        mid_ref[:, here] = (first * rows_ref[0:1, cols]).astype(BF16)
         end = first * rows_ref[1:2, cols] + second * rows_ref[2:3, cols]
-        end_ref[:, here] = end.astype(end_ref.dtype)
+        end_ref[:DSTATE, here] = end.astype(end_ref.dtype)
 
 
 def score_kernel(split, flag_ref, *refs):
-    b_rows, c_rows = pick(flag_ref[0, 0], refs[:split])
-    idc_ref, idr_ref, g_ref, live_ref, carried_ref = refs[split:]
+    edge_ref, idc_ref, idr_ref, g_ref, live_ref, carried_ref, ending_ref = refs[split:]
+    b_rows, c_rows = pick(flag_ref[0, 0], refs[:split], edge_ref)
+    ending_ref[...] = ending(b_rows, idr_ref, 0)
     b_rows = b_rows.astype(BF16)
     c_cols = c_rows.T
     for j in range(2):
@@ -222,18 +335,21 @@
     carried_ref[...] = jnp.where(ids == before, c_cols[CHUNK:, :], 0.0).astype(BF16)
 
 
-def local_kernel(low, xs_ref, mid_ref, g_ref, carried_ref, eps_ref, rows_ref, z_ref, y_ref, dec_ref):
+def local_kernel(low, xs_ref, edge_ref, g_ref, carried_ref, ending_ref, eps_ref, rows_ref, z_ref, y_ref, dec_ref):
     heads = eps_ref.shape[1] // 2
     for block in range(xs_ref.shape[1] // WIDE):
         start = low + block * WIDE
         here = slice(block * WIDE, (block + 1) * WIDE)
         cols = slice(start, start + WIDE)
         spread = spread_matrix(2, heads, start, WIDE)
+        values = opening(xs_ref, edge_ref, here, cols)
+        middle = (mm(ending_ref[...], values) * rows_ref[0:1, cols]).astype(BF16)
         for j in range(2):
             span = slice(j * CHUNK, (j + 1) * CHUNK)
-            y = mm(g_ref[j], xs_ref[span, here])
-            if j == 1:
-                y = y + mm(carried_ref[...], mid_ref[:, here])
+            if j == 0:
+                y = mm(g_ref[0], values)
+            else:
+                y = mm(g_ref[1], xs_ref[span, here]) + mm(carried_ref[...], middle)
             half = 0.5 * z_ref[span, cols].astype(F32)
             gate = (half + half * jnp.tanh(half)) * mm(eps_ref[span, :], spread)
             y_ref[span, here] = y * gate
@@ -252,7 +368,7 @@
         gain = gain_ref[:, cols].astype(F32)
         for j in range(2):
             span = slice(j * CHUNK, (j + 1) * CHUNK)
-            mixed = y_ref[span, here] + mm(live_ref[span, :], state_ref[:, here]) * dec_ref[span, here]
+            mixed = y_ref[span, here] + mm(live_ref[span, :], state_ref[:DSTATE, here]) * dec_ref[span, here]
             mean = mm((mixed * mixed).astype(BF16), mean_matrix)
             buffer[block, span, :] = (mixed * lax.rsqrt(mean + 1e-05) * gain).astype(BF16)
         copy = pltpu.make_async_copy(buffer.at[block], out_ref.at[:, cols], sem.at[block])
@@ -273,38 +389,67 @@
     smem = pl.BlockSpec(memory_space=pltpu.SMEM)
     hbm = pl.BlockSpec(memory_space=pltpu.HBM)
     shape = jax.ShapeDtypeStruct
-    bc_rows = bc_in.T
-    tail = call(
-        tail_kernel,
-        [spec, hbm, spec],
-        shape((8, columns + 128), BF16),
-        [pltpu.VMEM((8, columns), BF16), pltpu.SemaphoreType.DMA],
-        "tail",
-    )(starts, x_in, bc_rows)
-    rim = shifted(tail, "ctx", 1)
-    fac, eps, table, ids_col, ids_row = call(
+    in_hbm = lambda value: pltpu.with_memory_space_constraint(value, pltpu.HBM)
+    own, starts, steps, scale, taps = call(
+        bc_kernel,
+        [hbm] * 6,
+        [
+            shape((bc_width + 8, rows), BF16),
+            shape((1, rows), jnp.int32),
+            shape((heads, rows), F32),
+            shape((1, heads), F32),
+            shape((CONV, columns), BF16),
+        ],
+        [
+            pltpu.VMEM((bc_width, rows), BF16),
+            pltpu.VMEM((CONV, bc_width), BF16),
+            pltpu.SemaphoreType.DMA((6,)),
+        ],
+        "bc",
+    )(
+        in_hbm(bc_in.T),
+        in_hbm(conv_bc),
+        in_hbm(starts),
+        in_hbm(dt.T),
+        in_hbm(decay_scale.reshape(1, heads)),
+        in_hbm(conv_x),
+    )
+    shares = [own] + [crossed(own, "head", mask) for mask in range(1, split)]
+    fac, eps, table, ids_col, ids_row, x_near = call(
         prep_kernel,
-        [spec] * 3,
+        [spec] * 3 + [hbm],
         [
             shape((rows, 2 * heads), BF16),
             shape((rows, 2 * heads), BF16),
             shape((8, columns), F32),
             shape((rows, 128), F32),
             shape((8, rows), F32),
+            shape((rows, columns), BF16),
         ],
-        (),
+        [pltpu.SemaphoreType.DMA],
         "prep",
-    )(dt.T, decay_scale.reshape(1, heads), starts)
-    own = call(bc_kernel, [spec] * 4, shape((bc_width, rows), BF16), (), "bc")(
-        bc_rows, rim, conv_bc, ids_row
-    )
-    shares = [own] + [crossed(own, "head", mask) for mask in range(1, split)]
+    )(steps, scale, starts, in_hbm(x_in))
     flag = (lax.axis_index("head") < split // 2).astype(jnp.int32).reshape(1, 1)
     total = sum(SHARES)
     widths = [columns * share // total for share in SHARES]
     lows = [sum(widths[:group]) for group in range(len(widths))]
     state_type = BF16 if turns == 1 else F32
     gain = norm_gain.reshape(1, columns)
+    extra = rim_rows(columns, split, widths[0])
+
+    def fixed(rim):
+        return call(
+            fix_kernel,
+            [spec] * (5 + split),
+            [shape((2 * DSTATE, 128), BF16), shape((EDGE, columns), BF16)],
+            (),
+            "fix",
+        )(x_near, rim, taps, fac, ids_col, *shares)
+
+    edges = []
+    if turns > 1:
+        tail = call(tail_kernel, [spec] * (2 + split), shape((extra, widths[0]), BF16), (), "tail")
+        edges = fixed(shifted(tail(x_near, starts, *shares), "ctx", 1))
 
     def relay(low, width, end):
         if turns == 1:
@@ -313,41 +458,48 @@
         turn = lambda _, incoming: shifted(through * incoming + end, "ctx", 1)
         return lax.fori_loop(0, turns, turn, jnp.zeros_like(end)).astype(BF16)
 
-    values, middles, incoming = [], [], []
+    values, incoming = [], []
     for low, width in zip(lows, widths):
         part = call(
             functools.partial(conv_kernel, low),
-            [spec] * 5,
+            [spec] * 4,
             shape((rows, width), BF16),
             [pltpu.VMEM((rows + 8, 128), F32), pltpu.VMEM((CONV - 1, rows, 128), F32)],
             f"conv{low}",
-        )(x_in, rim, conv_x, fac, ids_col)
-        middle, end = call(
-            functools.partial(state_kernel, low, split),
-            [smem] + [spec] * (split + 3),
-            [shape((DSTATE, width), BF16), shape((DSTATE, width), state_type)],
+        )(x_near, taps, fac, ids_col)
+        carries = turns == 1 and low == 0
+        others = [x_near, starts] if carries else edges
+        end = call(
+            functools.partial(state_kernel, low, split, carries),
+            [smem] + [spec] * (split + 3 + len(others)),
+            shape((DSTATE + extra if carries else DSTATE, width), state_type),
             (),
             f"state{low}",
-        )(flag, *shares, part, table, ids_row)
+        )(flag, *shares, part, table, ids_row, *others)
         values.append(part)
-        middles.append(middle)
         incoming.append(relay(low, width, end))
-    scores, live, carried = call(
+    edge_bc, edge_x = edges or fixed(incoming[0])
+    scores, live, carried, ended = call(
         functools.partial(score_kernel, split),
-        [smem] + [spec] * (split + 2),
-        [shape((2, CHUNK, CHUNK), BF16), shape((rows, DSTATE), BF16), shape((CHUNK, DSTATE), BF16)],
+        [smem] + [spec] * (split + 3),
+        [
+            shape((2, CHUNK, CHUNK), BF16),
+            shape((rows, DSTATE), BF16),
+            shape((CHUNK, DSTATE), BF16),
+            shape((DSTATE, CHUNK), BF16),
+        ],
         (),
         "score",
-    )(flag, *shares, ids_col, ids_row)
+    )(flag, *shares, edge_bc, ids_col, ids_row)
     out = None
     for group, (low, width) in enumerate(zip(lows, widths)):
         mixed, decay = call(
             functools.partial(local_kernel, low),
-            [spec] * 7,
+            [spec] * 8,
             [shape((rows, width), F32)] * 2,
             (),
             f"local{low}",
-        )(values[group], middles[group], scores, carried, eps, table, z_in)
+        )(values[group], edge_x, scores, carried, ended, eps, table, z_in)
         blocks = width // WIDE
         args = [incoming[group], mixed, decay, live, gain]
         in_specs = [spec] * 5

time: 36.1 us -> 31.9 us (0.88)
  waiting for transfers between devices: 13.4 us -> 8.42 us
  local copies, waits for them, and re-layouts: 3.18 us -> 0.02 us
  Pallas kernels: 12.2 us -> 15 us
  starting transfers between devices: 6.96 us -> 8.19 us
    ppermute x4 -> x3, waiting for transfers between devices: 11.3 us -> 7.66 us  [shifted(): return lax.ppermute(value, axis, pairs)]
    unnamed x20 -> x4, local copies, waits for them, and re-layouts: 3.17 us -> 0.01 us
    pallas_call x13, Pallas kernels: 8.07 us -> 10.8 us  [the longest x3 3.68 us: on_device(): call(functools.partial(conv_kernel, low), [spec] * 4, shape((rows, width)...]
    ppermute x3, waiting for transfers between devices: 2.1 us -> 0.76 us  [crossed(): lax.ppermute(value, axis, [(source, source ^ mask) for source in range(co...]
    ppermute x3, starting transfers between devices: 1.93 us -> 3.12 us  [crossed(): lax.ppermute(value, axis, [(source, source ^ mask) for source in range(co...]
    ppermute x4 -> x3, starting transfers between devices: 5.02 us -> 5.07 us  [shifted(): return lax.ppermute(value, axis, pairs)]
  transfers between devices with their start and end apart: 7 -> 6, of which waited for: 6 -> 2; matrix products, arithmetic and copies ran while one was open for 0% -> 0% of each run, Pallas kernels for 28% -> 38%
where the time goes in v3:
time: 31.9 us; the launch traced here: 31.7 us
  Pallas kernels  15 us (47%)
  waiting for transfers between devices  8.42 us (26%)
  starting transfers between devices  8.19 us (26%)
    ppermute x3, waiting for transfers between devices, shifted(): return lax.ppermute(value, axis, pairs)  7.66 us
    ppermute x3, starting transfers between devices, shifted(): return lax.ppermute(value, axis, pairs)  5.07 us
    pallas_call x3, Pallas kernels, on_device(): call(functools.partial(final_kernel, low), in_specs, shape((rows, columns...  4.19 us
    pallas_call x3, Pallas kernels, on_device(): call(functools.partial(conv_kernel, low), [spec] * 4, shape((rows, width)...  3.68 us
    ppermute x3, starting transfers between devices, crossed(): lax.ppermute(value, axis, [(source, source ^ mask) for source in range(co...  3.12 us
    pallas_call x3, Pallas kernels, on_device(): call(functools.partial(local_kernel, low), [spec] * 8, [shape((rows, widt...  2.64 us
    pallas_call x1, Pallas kernels, on_device(): call(prep_kernel, [spec] * 3 + [hbm], [shape((rows, 2 * heads), BF16), sh...  1.6 us
    pallas_call x1, Pallas kernels, on_device(): call(bc_kernel, [hbm] * 6, [shape((bc_width + 8, rows), BF16), shape((1,...  1.37 us
  transfers between devices with their start and end apart: 6, of which 2 were waited for; matrix products, arithmetic and copies ran while one was open for 0% of the time, Pallas kernels for 38%

profile of v3, /device:TPU:0, one launch (start us, length us, event | category | flops | bytes accessed | tf_op | source)
XLA Modules:
  0.0 31.7 jit_solution(18175280321440881259)
XLA Ops:
  0.0 1.4 %bc.1 = (bf16[72,512]{1,0:T(8,128)(2,1)S(1)}, s32[1,512]{1,0:T(1,128)S(1)}, f32[32,512]{1,0:T(8,128)S(1)}, f32[1,32]{1,0:T(1,128)S(1)}, bf16[4,2048]{1,0:T(4,128)(2,1)S(1)}) custom-call(bf16[64,512]{1,0:T(8,128)(2,1)} %bitcast.5, bf16[4,64]{1,0:T(4,128)(2,1)} %refs_1_.1, s32[1,512]{1,0:T(1,128)} %bitcast.7, f32[32,512]{1,0:T(8,128)} %bitcast.6, ...), custom_call_target="tpu_custom_call" | custom-call | tf_op jit(solution)/shard_map/bc/pallas_call | solution.py:393
  1.4 2.4 %collective-permute-start.2 = (bf16[72,512]{1,0:T(8,128)(2,1)S(1)}, bf16[72,512]{1,0:T(8,128)(2,1)S(1)}, u32[]{:S(2)}, u32[]{:S(2)}) collective-permute-start(bf16[72,512]{1,0:T(8,128)(2,1)S(1)} %get-tuple-element.28.refs_0_), channel_id=1, source_target_pairs={{0,3},{1,2},{2,1},{3,0},{4,7},{5,6},{6,5},{7,4},{8,11},{9,10},{10,... | collective-permute-start | bytes 221192 | tf_op jit(solution)/shard_map/ppermute | solution.py:29
  3.8 0.6 %collective-permute-start.1 = (bf16[72,512]{1,0:T(8,128)(2,1)S(1)}, bf16[72,512]{1,0:T(8,128)(2,1)S(1)}, u32[]{:S(2)}, u32[]{:S(2)}) collective-permute-start(bf16[72,512]{1,0:T(8,128)(2,1)S(1)} %get-tuple-element.28.refs_0_), channel_id=1, source_target_pairs={{0,2},{1,3},{2,0},{3,1},{4,6},{5,7},{6,4},{7,5},{8,10},{9,11},{10,... | collective-permute-start | bytes 221192 | tf_op jit(solution)/shard_map/ppermute | solution.py:29
  4.5 0.0 collective-permute-start
  4.5 1.6 %prep.1 = (bf16[512,64]{1,0:T(8,128)(2,1)S(1)}, bf16[512,64]{1,0:T(8,128)(2,1)S(1)}, f32[8,2048]{1,0:T(8,128)S(1)}, f32[512,128]{1,0:T(8,128)S(1)}, f32[8,512]{1,0:T(8,128)S(1)}, /*index=5*/bf16[512,2048]{1,0:T(8,128)(2,1)S(1)}) custom-call(f32[32,512]{1,0:T(8,128)S(1)} %get-tuple-element.29.dt_ref, f32[1,32]{1,0:T(1,128)S(1)} %get-tuple-element.30.scale_ref, ...), custom_call_target="tpu_custom_call" | custom-call | tf_op jit(solution)/shard_map/prep/pallas_call | solution.py:418
  6.1 1.8 %conv512.1.refs_4_.xs_ref = bf16[512,1024]{1,0:T(8,128)(2,1)S(1)} custom-call(bf16[512,2048]{1,0:T(8,128)(2,1)S(1)} %get-tuple-element.32.x_ref.refs_7_, bf16[4,2048]{1,0:T(4,128)(2,1)S(1)} %get-tuple-element.33.taps_ref, bf16[512,64]{1,0:T(8,128)(2,1)S(1)} %get-tuple-element.34.fac_ref, f32[512,128]{1,0:T(8,128)S(1)} %get-tuple-element.35.idc_ref.refs_5_), custom_call_target="tpu_custom_call" | custom-call | tf_op jit(solution)/shard_map/conv512/pallas_call | solution.py:463
  7.9 0.8 %collective-permute-done.1.refs_2_ = bf16[72,512]{1,0:T(8,128)(2,1)S(1)} collective-permute-done((bf16[72,512]{1,0:T(8,128)(2,1)S(1)}, bf16[72,512]{1,0:T(8,128)(2,1)S(1)}, u32[]{:S(2)}, u32[]{:S(2)}) %collective-permute-start.1) | collective-permute-done | bytes 73760 | tf_op jit(solution)/shard_map/ppermute | solution.py:29
  8.7 0.4 %state512.1 = bf16[128,1024]{1,0:T(8,128)(2,1)S(1)} custom-call(s32[1,1]{1,0:T(1,128)} %bitcast.flag_ref, bf16[72,512]{1,0:T(8,128)(2,1)S(1)} %get-tuple-element.28.refs_0_, bf16[72,512]{1,0:T(8,128)(2,1)S(1)} %collective-permute-done.refs_1_, bf16[72,512]{1,0:T(8,128)(2,1)S(1)} %collective-permute-done.1.refs_2_, ...), custom_call_target="tpu_custom_call" | custom-call | tf_op jit(solution)/shard_map/state512/pallas_call | solution.py:472
  9.0 1.9 %collective-permute-start.5 = (bf16[128,1024]{1,0:T(8,128)(2,1)S(1)}, bf16[128,1024]{1,0:T(8,128)(2,1)S(1)}, u32[]{:S(2)}, u32[]{:S(2)}) collective-permute-start(bf16[128,1024]{1,0:T(8,128)(2,1)S(1)} %state512.1), channel_id=1, source_target_pairs={{0,4},{4,8},{8,12},{12,16},{16,20},{20,24},{24,28},{28,0},{1,5},{5... | collective-permute-start | bytes 786440 | tf_op jit(solution)/shard_map/ppermute | solution.py:24
  11.0 0.9 %conv0.1.refs_4_.xs_ref = bf16[512,512]{1,0:T(8,128)(2,1)S(1)} custom-call(bf16[512,2048]{1,0:T(8,128)(2,1)S(1)} %get-tuple-element.32.x_ref.refs_7_, bf16[4,2048]{1,0:T(4,128)(2,1)S(1)} %get-tuple-element.33.taps_ref, bf16[512,64]{1,0:T(8,128)(2,1)S(1)} %get-tuple-element.34.fac_ref, f32[512,128]{1,0:T(8,128)S(1)} %get-tuple-element.35.idc_ref.refs_5_), custom_call_target="tpu_custom_call" | custom-call | tf_op jit(solution)/shard_map/conv0/pallas_call | solution.py:463
  11.9 0.3 state0.1
  12.2 1.6 %collective-permute-start.4 = (bf16[144,512]{1,0:T(8,128)(2,1)S(1)}, bf16[144,512]{1,0:T(8,128)(2,1)S(1)}, u32[]{:S(2)}, u32[]{:S(2)}) collective-permute-start(bf16[144,512]{1,0:T(8,128)(2,1)S(1)} %state0.1), channel_id=1, source_target_pairs={{0,4},{4,8},{8,12},{12,16},{16,20},{20,24},{24,28},{28,0},{1,5},{5... | collective-permute-start | bytes 442376 | tf_op jit(solution)/shard_map/ppermute | solution.py:24
  13.8 0.9 %conv1536.1.refs_4_.xs_ref = bf16[512,512]{1,0:T(8,128)(2,1)S(1)} custom-call(bf16[512,2048]{1,0:T(8,128)(2,1)S(1)} %get-tuple-element.32.x_ref.refs_7_, bf16[4,2048]{1,0:T(4,128)(2,1)S(1)} %get-tuple-element.33.taps_ref, bf16[512,64]{1,0:T(8,128)(2,1)S(1)} %get-tuple-element.34.fac_ref, f32[512,128]{1,0:T(8,128)S(1)} %get-tuple-element.35.idc_ref.refs_5_), custom_call_target="tpu_custom_call" | custom-call | tf_op jit(solution)/shard_map/conv1536/pallas_call | solution.py:463
  14.8 0.3 state1536.1
  15.0 1.6 %collective-permute-start.3 = (bf16[128,512]{1,0:T(8,128)(2,1)S(1)}, bf16[128,512]{1,0:T(8,128)(2,1)S(1)}, u32[]{:S(2)}, u32[]{:S(2)}) collective-permute-start(bf16[128,512]{1,0:T(8,128)(2,1)S(1)} %state1536.1), channel_id=1, source_target_pairs={{0,4},{4,8},{8,12},{12,16},{16,20},{20,24},{24,28},{28,0},{1,5},{5... | collective-permute-start | bytes 393224 | tf_op jit(solution)/shard_map/ppermute | solution.py:24
  16.6 7.7 %collective-permute-done.4.rim_ref.state_ref = bf16[144,512]{1,0:T(8,128)(2,1)S(1)} collective-permute-done((bf16[144,512]{1,0:T(8,128)(2,1)S(1)}, bf16[144,512]{1,0:T(8,128)(2,1)S(1)}, u32[]{:S(2)}, u32[]{:S(2)}) %collective-permute-start.4) | collective-permute-done | bytes 147488 | tf_op jit(solution)/shard_map/ppermute | solution.py:24
  24.3 0.2 fix.1
  24.5 0.3 score.1
  24.8 0.7 %local1536.1 = (f32[512,512]{1,0:T(8,128)S(1)}, f32[512,512]{1,0:T(8,128)S(1)}) custom-call(bf16[512,512]{1,0:T(8,128)(2,1)S(1)} %conv1536.1.refs_4_.xs_ref, bf16[16,2048]{1,0:T(8,128)(2,1)S(1)} %get-tuple-element.38.edge_ref, bf16[2,256,256]{2,1,0:T(8,128)(2,1)S(1)} %get-tuple-element.40.g_ref, bf16[256,128]{1,0:T(8,128)(2,1)S(1)} %get-tuple-element.41.carried_ref, ...), custom_call_target="tpu_custom_call" | custom-call | tf_op jit(solution)/shard_map/local1536/pallas_call | solution.py:496
  25.6 0.7 %local0.1 = (f32[512,512]{1,0:T(8,128)S(1)}, f32[512,512]{1,0:T(8,128)S(1)}) custom-call(bf16[512,512]{1,0:T(8,128)(2,1)S(1)} %conv0.1.refs_4_.xs_ref, bf16[16,2048]{1,0:T(8,128)(2,1)S(1)} %get-tuple-element.38.edge_ref, bf16[2,256,256]{2,1,0:T(8,128)(2,1)S(1)} %get-tuple-element.40.g_ref, bf16[256,128]{1,0:T(8,128)(2,1)S(1)} %get-tuple-element.41.carried_ref, ...), custom_call_target="tpu_custom_call" | custom-call | tf_op jit(solution)/shard_map/local0/pallas_call | solution.py:496
  26.3 1.2 %local512.1 = (f32[512,1024]{1,0:T(8,128)S(1)}, f32[512,1024]{1,0:T(8,128)S(1)}) custom-call(bf16[512,1024]{1,0:T(8,128)(2,1)S(1)} %conv512.1.refs_4_.xs_ref, bf16[16,2048]{1,0:T(8,128)(2,1)S(1)} %get-tuple-element.38.edge_ref, bf16[2,256,256]{2,1,0:T(8,128)(2,1)S(1)} %get-tuple-element.40.g_ref, bf16[256,128]{1,0:T(8,128)(2,1)S(1)} %get-tuple-element.41.carried_ref, ...), custom_call_target="tpu_custom_call" | custom-call | tf_op jit(solution)/shard_map/local512/pallas_call | solution.py:496
  27.5 1.3 %final0.1.refs_0_ = bf16[512,2048]{1,0:T(8,128)(2,1)} custom-call(bf16[144,512]{1,0:T(8,128)(2,1)S(1)} %collective-permute-done.4.rim_ref.state_ref, f32[512,512]{1,0:T(8,128)S(1)} %get-tuple-element.49.y_ref, f32[512,512]{1,0:T(8,128)S(1)} %get-tuple-element.50.dec_ref, bf16[512,128]{1,0:T(8,128)(2,1)S(1)} %get-tuple-element.46.live_ref, ...), custom_call_target="tpu_custom_call" | custom-call | tf_op jit(solution)/shard_map/final0/pallas_call | solution.py:509
  28.8 1.6 %final512.1.refs_0_ = bf16[512,2048]{1,0:T(8,128)(2,1)} custom-call(bf16[128,1024]{1,0:T(8,128)(2,1)S(1)} %collective-permute-done.5.state_ref, f32[512,1024]{1,0:T(8,128)S(1)} %get-tuple-element.47.y_ref, f32[512,1024]{1,0:T(8,128)S(1)} %get-tuple-element.48.dec_ref, ...), custom_call_target="tpu_custom_call", output_to_operand_aliasing={{}: (5, {})} | custom-call | tf_op jit(solution)/shard_map/final512/pallas_call | solution.py:509
  30.4 1.3 %final1536.1 = bf16[512,2048]{1,0:T(8,128)(2,1)} custom-call(bf16[128,512]{1,0:T(8,128)(2,1)S(1)} %collective-permute-done.3.state_ref, f32[512,512]{1,0:T(8,128)S(1)} %get-tuple-element.44.y_ref, f32[512,512]{1,0:T(8,128)S(1)} %get-tuple-element.45.dec_ref, bf16[512,128]{1,0:T(8,128)(2,1)S(1)} %get-tuple-element.46.live_ref, ...), custom_call_target="tpu_custom_call", output_to_operand_aliasing={{}: (5, {})} | custom-call | tf_op jit(solution)/shard_map/final1536/pallas_call | solution.py:509
  (9 shorter events, 0.0 us)
Async XLA Ops:
  1.4 6.5 %collective-permute-start.2 = (bf16[72,512]{1,0:T(8,128)(2,1)S(1)}, bf16[72,512]{1,0:T(8,128)(2,1)S(1)}, u32[]{:S(2)}, u32[]{:S(2)}) collective-permute-start(bf16[72,512]{1,0:T(8,128)(2,1)S(1)} %get-tuple-element.28.refs_0_), channel_id=1, source_target_pairs={{0,3},{1,2},{2,1},{3,0},{4,7},{5,6},{6,5},{7,4},{8,11},{9,10},{10,... | collective-permute-start | bytes 221192 | tf_op jit(solution)/shard_map/ppermute | solution.py:29
  3.8 4.8 %collective-permute-start.1 = (bf16[72,512]{1,0:T(8,128)(2,1)S(1)}, bf16[72,512]{1,0:T(8,128)(2,1)S(1)}, u32[]{:S(2)}, u32[]{:S(2)}) collective-permute-start(bf16[72,512]{1,0:T(8,128)(2,1)S(1)} %get-tuple-element.28.refs_0_), channel_id=1, source_target_pairs={{0,2},{1,3},{2,0},{3,1},{4,6},{5,7},{6,4},{7,5},{8,10},{9,11},{10,... | collective-permute-start | bytes 221192 | tf_op jit(solution)/shard_map/ppermute | solution.py:29
  4.5 4.2 %collective-permute-start = (bf16[72,512]{1,0:T(8,128)(2,1)S(1)}, bf16[72,512]{1,0:T(8,128)(2,1)S(1)}, u32[]{:S(2)}, u32[]{:S(2)}) collective-permute-start(bf16[72,512]{1,0:T(8,128)(2,1)S(1)} %get-tuple-element.28.refs_0_), channel_id=1, source_target_pairs={{0,1},{1,0},{2,3},{3,2},{4,5},{5,4},{6,7},{7,6},{8,9},{9,8},{10,11... | collective-permute-start | bytes 221192 | tf_op jit(solution)/shard_map/ppermute | solution.py:29
  9.0 19.8 %collective-permute-start.5 = (bf16[128,1024]{1,0:T(8,128)(2,1)S(1)}, bf16[128,1024]{1,0:T(8,128)(2,1)S(1)}, u32[]{:S(2)}, u32[]{:S(2)}) collective-permute-start(bf16[128,1024]{1,0:T(8,128)(2,1)S(1)} %state512.1), channel_id=1, source_target_pairs={{0,4},{4,8},{8,12},{12,16},{16,20},{20,24},{24,28},{28,0},{1,5},{5... | collective-permute-start | bytes 786440 | tf_op jit(solution)/shard_map/ppermute | solution.py:24
  12.2 4.4 %copy-start.1 = (bf16[2048]{0:T(1024)(128)(2,1)S(1)}, bf16[2048]{0:T(1024)(128)(2,1)}, u32[]{:S(2)}) copy-start(bf16[2048]{0:T(1024)(128)(2,1)} %param.16) | copy-start | bytes 12292
  12.2 12.1 %collective-permute-start.4 = (bf16[144,512]{1,0:T(8,128)(2,1)S(1)}, bf16[144,512]{1,0:T(8,128)(2,1)S(1)}, u32[]{:S(2)}, u32[]{:S(2)}) collective-permute-start(bf16[144,512]{1,0:T(8,128)(2,1)S(1)} %state0.1), channel_id=1, source_target_pairs={{0,4},{4,8},{8,12},{12,16},{16,20},{20,24},{24,28},{28,0},{1,5},{5... | collective-permute-start | bytes 442376 | tf_op jit(solution)/shard_map/ppermute | solution.py:24
  14.7 10.1 %copy-start = (bf16[512,2048]{1,0:T(8,128)(2,1)S(1)}, bf16[512,2048]{1,0:T(8,128)(2,1)}, u32[]{:S(2)}) copy-start(bf16[512,2048]{1,0:T(8,128)(2,1)} %z_ref.5) | copy-start | bytes 6291460
  15.0 15.4 %collective-permute-start.3 = (bf16[128,512]{1,0:T(8,128)(2,1)S(1)}, bf16[128,512]{1,0:T(8,128)(2,1)S(1)}, u32[]{:S(2)}, u32[]{:S(2)}) collective-permute-start(bf16[128,512]{1,0:T(8,128)(2,1)S(1)} %state1536.1), channel_id=1, source_target_pairs={{0,4},{4,8},{8,12},{12,16},{16,20},{20,24},{24,28},{28,0},{1,5},{5... | collective-permute-start | bytes 393224 | tf_op jit(solution)/shard_map/ppermute | solution.py:24

commit v4 on v3

--- a/solution.py
+++ b/solution.py
@@ -12,7 +12,7 @@
 CONV = 4
 CHUNK = 256
 WIDE = 256
-SHARES = (2, 4, 2)
+SHARES = (4, 2, 2)
 EDGE = 16
 F32 = jnp.float32
 BF16 = jnp.bfloat16
@@ -71,7 +71,8 @@
 
 
 def rim_rows(columns, split, width):
-    return -(-3 * (columns + 128 * split) // width // 16) * 16
+    slots = columns // width + -(-128 * split // width)
+    return -(-3 * slots // 16) * 16
 
 
 def rim_block(x_ref, start_ref, shares, width):
@@ -96,6 +97,8 @@
     count = width // 128
     for index in range(0, len(shares), count):
         piece = [share[share.shape[0] - 8 :, :128] for share in shares[index : index + count]]
+        gap = width - 128 * len(piece)
+        piece += [jnp.zeros((8, gap), BF16)] if gap else []
         piece = jnp.concatenate(piece, axis=1).astype(F32)
         piece = jnp.where((row >= 3) & (row < 6), piece, 0.0)
         piece = jnp.concatenate([piece, below], axis=0)

time: 31.9 us -> 29.3 us (0.918)
  waiting for transfers between devices: 8.42 us -> 5.92 us
    ppermute x3, waiting for transfers between devices: 7.66 us -> 5.19 us  [shifted(): return lax.ppermute(value, axis, pairs)]
  transfers between devices with their start and end apart: 6 -> 6, of which waited for: 2 -> 2; matrix products, arithmetic and copies ran while one was open for 0% -> 0% of each run, Pallas kernels for 38% -> 41%
where the time goes in v4:
time: 29.3 us; the launch traced here: 29.1 us
  Pallas kernels  14.9 us (51%)
  starting transfers between devices  8.14 us (28%)
  waiting for transfers between devices  5.92 us (20%)
    ppermute x3, waiting for transfers between devices, shifted(): return lax.ppermute(value, axis, pairs)  5.19 us
    ppermute x3, starting transfers between devices, shifted(): return lax.ppermute(value, axis, pairs)  4.99 us
    pallas_call x3, Pallas kernels, on_device(): call(functools.partial(final_kernel, low), in_specs, shape((rows, columns...  4.12 us
    pallas_call x3, Pallas kernels, on_device(): call(functools.partial(conv_kernel, low), [spec] * 4, shape((rows, width)...  3.69 us
    ppermute x3, starting transfers between devices, crossed(): lax.ppermute(value, axis, [(source, source ^ mask) for source in range(co...  3.15 us
    pallas_call x3, Pallas kernels, on_device(): call(functools.partial(local_kernel, low), [spec] * 8, [shape((rows, widt...  2.62 us
    pallas_call x1, Pallas kernels, on_device(): call(prep_kernel, [spec] * 3 + [hbm], [shape((rows, 2 * heads), BF16), sh...  1.6 us
    pallas_call x1, Pallas kernels, on_device(): call(bc_kernel, [hbm] * 6, [shape((bc_width + 8, rows), BF16), shape((1,...  1.37 us
  transfers between devices with their start and end apart: 6, of which 2 were waited for; matrix products, arithmetic and copies ran while one was open for 0% of the time, Pallas kernels for 41%

profile of v4, /device:TPU:0, one launch (start us, length us, event | category | flops | bytes accessed | tf_op | source)
XLA Modules:
  0.0 29.1 jit_solution(6349873387245121182)
XLA Ops:
  0.0 1.4 %bc.1 = (bf16[72,512]{1,0:T(8,128)(2,1)S(1)}, s32[1,512]{1,0:T(1,128)S(1)}, f32[32,512]{1,0:T(8,128)S(1)}, f32[1,32]{1,0:T(1,128)S(1)}, bf16[4,2048]{1,0:T(4,128)(2,1)S(1)}) custom-call(bf16[64,512]{1,0:T(8,128)(2,1)} %bitcast.5, bf16[4,64]{1,0:T(4,128)(2,1)} %refs_1_.1, s32[1,512]{1,0:T(1,128)} %bitcast.7, f32[32,512]{1,0:T(8,128)} %bitcast.6, ...), custom_call_target="tpu_custom_call" | custom-call | tf_op jit(solution)/shard_map/bc/pallas_call | solution.py:396
  1.4 0.5 %collective-permute-start = (bf16[72,512]{1,0:T(8,128)(2,1)S(1)}, bf16[72,512]{1,0:T(8,128)(2,1)S(1)}, u32[]{:S(2)}, u32[]{:S(2)}) collective-permute-start(bf16[72,512]{1,0:T(8,128)(2,1)S(1)} %get-tuple-element.28.refs_0_), channel_id=1, source_target_pairs={{0,1},{1,0},{2,3},{3,2},{4,5},{5,4},{6,7},{7,6},{8,9},{9,8},{10,11... | collective-permute-start | bytes 221192 | tf_op jit(solution)/shard_map/ppermute | solution.py:29
  1.9 2.6 %collective-permute-start.1 = (bf16[72,512]{1,0:T(8,128)(2,1)S(1)}, bf16[72,512]{1,0:T(8,128)(2,1)S(1)}, u32[]{:S(2)}, u32[]{:S(2)}) collective-permute-start(bf16[72,512]{1,0:T(8,128)(2,1)S(1)} %get-tuple-element.28.refs_0_), channel_id=1, source_target_pairs={{0,2},{1,3},{2,0},{3,1},{4,6},{5,7},{6,4},{7,5},{8,10},{9,11},{10,... | collective-permute-start | bytes 221192 | tf_op jit(solution)/shard_map/ppermute | solution.py:29
  4.5 0.1 collective-permute-start.2
  4.5 1.6 %prep.1 = (bf16[512,64]{1,0:T(8,128)(2,1)S(1)}, bf16[512,64]{1,0:T(8,128)(2,1)S(1)}, f32[8,2048]{1,0:T(8,128)S(1)}, f32[512,128]{1,0:T(8,128)S(1)}, f32[8,512]{1,0:T(8,128)S(1)}, /*index=5*/bf16[512,2048]{1,0:T(8,128)(2,1)S(1)}) custom-call(f32[32,512]{1,0:T(8,128)S(1)} %get-tuple-element.29.dt_ref, f32[1,32]{1,0:T(1,128)S(1)} %get-tuple-element.30.scale_ref, ...), custom_call_target="tpu_custom_call" | custom-call | tf_op jit(solution)/shard_map/prep/pallas_call | solution.py:421
  6.1 1.8 %conv0.1.refs_4_.xs_ref = bf16[512,1024]{1,0:T(8,128)(2,1)S(1)} custom-call(bf16[512,2048]{1,0:T(8,128)(2,1)S(1)} %get-tuple-element.32.x_ref.refs_7_, bf16[4,2048]{1,0:T(4,128)(2,1)S(1)} %get-tuple-element.33.taps_ref, bf16[512,64]{1,0:T(8,128)(2,1)S(1)} %get-tuple-element.34.fac_ref, f32[512,128]{1,0:T(8,128)S(1)} %get-tuple-element.35.idc_ref.refs_5_), custom_call_target="tpu_custom_call" | custom-call | tf_op jit(solution)/shard_map/conv0/pallas_call | solution.py:466
  8.0 0.7 %collective-permute-done.2.refs_3_ = bf16[72,512]{1,0:T(8,128)(2,1)S(1)} collective-permute-done((bf16[72,512]{1,0:T(8,128)(2,1)S(1)}, bf16[72,512]{1,0:T(8,128)(2,1)S(1)}, u32[]{:S(2)}, u32[]{:S(2)}) %collective-permute-start.2) | collective-permute-done | bytes 73760 | tf_op jit(solution)/shard_map/ppermute | solution.py:29
  8.7 0.4 %state0.1 = bf16[144,1024]{1,0:T(8,128)(2,1)S(1)} custom-call(s32[1,1]{1,0:T(1,128)} %bitcast.flag_ref, bf16[72,512]{1,0:T(8,128)(2,1)S(1)} %get-tuple-element.28.refs_0_, bf16[72,512]{1,0:T(8,128)(2,1)S(1)} %collective-permute-done.refs_1_, bf16[72,512]{1,0:T(8,128)(2,1)S(1)} %collective-permute-done.1.refs_2_, ...), custom_call_target="tpu_custom_call" | custom-call | tf_op jit(solution)/shard_map/state0/pallas_call | solution.py:475
  9.0 1.8 %collective-permute-start.4 = (bf16[144,1024]{1,0:T(8,128)(2,1)S(1)}, bf16[144,1024]{1,0:T(8,128)(2,1)S(1)}, u32[]{:S(2)}, u32[]{:S(2)}) collective-permute-start(bf16[144,1024]{1,0:T(8,128)(2,1)S(1)} %state0.1), channel_id=1, source_target_pairs={{0,4},{4,8},{8,12},{12,16},{16,20},{20,24},{24,28},{28,0},{1,5},{5... | collective-permute-start | bytes 884744 | tf_op jit(solution)/shard_map/ppermute | solution.py:24
  10.9 0.9 %conv1024.1.refs_4_.xs_ref = bf16[512,512]{1,0:T(8,128)(2,1)S(1)} custom-call(bf16[512,2048]{1,0:T(8,128)(2,1)S(1)} %get-tuple-element.32.x_ref.refs_7_, bf16[4,2048]{1,0:T(4,128)(2,1)S(1)} %get-tuple-element.33.taps_ref, bf16[512,64]{1,0:T(8,128)(2,1)S(1)} %get-tuple-element.34.fac_ref, f32[512,128]{1,0:T(8,128)S(1)} %get-tuple-element.35.idc_ref.refs_5_), custom_call_target="tpu_custom_call" | custom-call | tf_op jit(solution)/shard_map/conv1024/pallas_call | solution.py:466
  11.8 0.3 state1024.1
  12.1 1.6 %collective-permute-start.5 = (bf16[128,512]{1,0:T(8,128)(2,1)S(1)}, bf16[128,512]{1,0:T(8,128)(2,1)S(1)}, u32[]{:S(2)}, u32[]{:S(2)}) collective-permute-start(bf16[128,512]{1,0:T(8,128)(2,1)S(1)} %state1024.1), channel_id=1, source_target_pairs={{0,4},{4,8},{8,12},{12,16},{16,20},{20,24},{24,28},{28,0},{1,5},{5... | collective-permute-start | bytes 393224 | tf_op jit(solution)/shard_map/ppermute | solution.py:24
  13.7 0.9 %conv1536.1.refs_4_.xs_ref = bf16[512,512]{1,0:T(8,128)(2,1)S(1)} custom-call(bf16[512,2048]{1,0:T(8,128)(2,1)S(1)} %get-tuple-element.32.x_ref.refs_7_, bf16[4,2048]{1,0:T(4,128)(2,1)S(1)} %get-tuple-element.33.taps_ref, bf16[512,64]{1,0:T(8,128)(2,1)S(1)} %get-tuple-element.34.fac_ref, f32[512,128]{1,0:T(8,128)S(1)} %get-tuple-element.35.idc_ref.refs_5_), custom_call_target="tpu_custom_call" | custom-call | tf_op jit(solution)/shard_map/conv1536/pallas_call | solution.py:466
  14.7 0.3 state1536.1
  15.0 1.6 %collective-permute-start.3 = (bf16[128,512]{1,0:T(8,128)(2,1)S(1)}, bf16[128,512]{1,0:T(8,128)(2,1)S(1)}, u32[]{:S(2)}, u32[]{:S(2)}) collective-permute-start(bf16[128,512]{1,0:T(8,128)(2,1)S(1)} %state1536.1), channel_id=1, source_target_pairs={{0,4},{4,8},{8,12},{12,16},{16,20},{20,24},{24,28},{28,0},{1,5},{5... | collective-permute-start | bytes 393224 | tf_op jit(solution)/shard_map/ppermute | solution.py:24
  16.6 5.2 %collective-permute-done.4.rim_ref.state_ref = bf16[144,1024]{1,0:T(8,128)(2,1)S(1)} collective-permute-done((bf16[144,1024]{1,0:T(8,128)(2,1)S(1)}, bf16[144,1024]{1,0:T(8,128)(2,1)S(1)}, u32[]{:S(2)}, u32[]{:S(2)}) %collective-permute-start.4) | collective-permute-done | bytes 294944 | tf_op jit(solution)/shard_map/ppermute | solution.py:24
  21.7 0.2 fix.1
  22.0 0.3 %score.1 = (bf16[2,256,256]{2,1,0:T(8,128)(2,1)S(1)}, bf16[512,128]{1,0:T(8,128)(2,1)S(1)}, bf16[256,128]{1,0:T(8,128)(2,1)S(1)}, bf16[128,256]{1,0:T(8,128)(2,1)S(1)}) custom-call(s32[1,1]{1,0:T(1,128)} %bitcast.flag_ref, bf16[72,512]{1,0:T(8,128)(2,1)S(1)} %get-tuple-element.28.refs_0_, bf16[72,512]{1,0:T(8,128)(2,1)S(1)} %collective-permute-done.refs_1_, ...), custom_call_target="tpu_custom_call" | custom-call | tf_op jit(solution)/shard_map/score/pallas_call | solution.py:485
  22.3 1.2 %local0.1 = (f32[512,1024]{1,0:T(8,128)S(1)}, f32[512,1024]{1,0:T(8,128)S(1)}) custom-call(bf16[512,1024]{1,0:T(8,128)(2,1)S(1)} %conv0.1.refs_4_.xs_ref, bf16[16,2048]{1,0:T(8,128)(2,1)S(1)} %get-tuple-element.38.edge_ref, bf16[2,256,256]{2,1,0:T(8,128)(2,1)S(1)} %get-tuple-element.40.g_ref, bf16[256,128]{1,0:T(8,128)(2,1)S(1)} %get-tuple-element.41.carried_ref, ...), custom_call_target="tpu_custom_call" | custom-call | tf_op jit(solution)/shard_map/local0/pallas_call | solution.py:499
  23.5 0.7 %local1024.1 = (f32[512,512]{1,0:T(8,128)S(1)}, f32[512,512]{1,0:T(8,128)S(1)}) custom-call(bf16[512,512]{1,0:T(8,128)(2,1)S(1)} %conv1024.1.refs_4_.xs_ref, bf16[16,2048]{1,0:T(8,128)(2,1)S(1)} %get-tuple-element.38.edge_ref, bf16[2,256,256]{2,1,0:T(8,128)(2,1)S(1)} %get-tuple-element.40.g_ref, bf16[256,128]{1,0:T(8,128)(2,1)S(1)} %get-tuple-element.41.carried_ref, ...), custom_call_target="tpu_custom_call" | custom-call | tf_op jit(solution)/shard_map/local1024/pallas_call | solution.py:499
  24.2 0.7 %local1536.1 = (f32[512,512]{1,0:T(8,128)S(1)}, f32[512,512]{1,0:T(8,128)S(1)}) custom-call(bf16[512,512]{1,0:T(8,128)(2,1)S(1)} %conv1536.1.refs_4_.xs_ref, bf16[16,2048]{1,0:T(8,128)(2,1)S(1)} %get-tuple-element.38.edge_ref, bf16[2,256,256]{2,1,0:T(8,128)(2,1)S(1)} %get-tuple-element.40.g_ref, bf16[256,128]{1,0:T(8,128)(2,1)S(1)} %get-tuple-element.41.carried_ref, ...), custom_call_target="tpu_custom_call" | custom-call | tf_op jit(solution)/shard_map/local1536/pallas_call | solution.py:499
  24.9 1.6 %final0.1.refs_0_ = bf16[512,2048]{1,0:T(8,128)(2,1)} custom-call(bf16[144,1024]{1,0:T(8,128)(2,1)S(1)} %collective-permute-done.4.rim_ref.state_ref, f32[512,1024]{1,0:T(8,128)S(1)} %get-tuple-element.49.y_ref, f32[512,1024]{1,0:T(8,128)S(1)} %get-tuple-element.50.dec_ref, bf16[512,128]{1,0:T(8,128)(2,1)S(1)} %get-tuple-element.46.live_ref, ...), custom_call_target="tpu_custom_call" | custom-call | tf_op jit(solution)/shard_map/final0/pallas_call | solution.py:512
  26.5 1.3 %final1024.1.refs_0_ = bf16[512,2048]{1,0:T(8,128)(2,1)} custom-call(bf16[128,512]{1,0:T(8,128)(2,1)S(1)} %collective-permute-done.5.state_ref, f32[512,512]{1,0:T(8,128)S(1)} %get-tuple-element.47.y_ref, f32[512,512]{1,0:T(8,128)S(1)} %get-tuple-element.48.dec_ref, bf16[512,128]{1,0:T(8,128)(2,1)S(1)} %get-tuple-element.46.live_ref, ...), custom_call_target="tpu_custom_call", output_to_operand_aliasing={{}: (5, {})} | custom-call | tf_op jit(solution)/shard_map/final1024/pallas_call | solution.py:512
  27.8 1.3 %final1536.1 = bf16[512,2048]{1,0:T(8,128)(2,1)} custom-call(bf16[128,512]{1,0:T(8,128)(2,1)S(1)} %collective-permute-done.3.state_ref, f32[512,512]{1,0:T(8,128)S(1)} %get-tuple-element.44.y_ref, f32[512,512]{1,0:T(8,128)S(1)} %get-tuple-element.45.dec_ref, bf16[512,128]{1,0:T(8,128)(2,1)S(1)} %get-tuple-element.46.live_ref, ...), custom_call_target="tpu_custom_call", output_to_operand_aliasing={{}: (5, {})} | custom-call | tf_op jit(solution)/shard_map/final1536/pallas_call | solution.py:512
  (9 shorter events, 0.0 us)
Async XLA Ops:
  1.4 6.6 %collective-permute-start = (bf16[72,512]{1,0:T(8,128)(2,1)S(1)}, bf16[72,512]{1,0:T(8,128)(2,1)S(1)}, u32[]{:S(2)}, u32[]{:S(2)}) collective-permute-start(bf16[72,512]{1,0:T(8,128)(2,1)S(1)} %get-tuple-element.28.refs_0_), channel_id=1, source_target_pairs={{0,1},{1,0},{2,3},{3,2},{4,5},{5,4},{6,7},{7,6},{8,9},{9,8},{10,11... | collective-permute-start | bytes 221192 | tf_op jit(solution)/shard_map/ppermute | solution.py:29
  1.9 6.1 %collective-permute-start.1 = (bf16[72,512]{1,0:T(8,128)(2,1)S(1)}, bf16[72,512]{1,0:T(8,128)(2,1)S(1)}, u32[]{:S(2)}, u32[]{:S(2)}) collective-permute-start(bf16[72,512]{1,0:T(8,128)(2,1)S(1)} %get-tuple-element.28.refs_0_), channel_id=1, source_target_pairs={{0,2},{1,3},{2,0},{3,1},{4,6},{5,7},{6,4},{7,5},{8,10},{9,11},{10,... | collective-permute-start | bytes 221192 | tf_op jit(solution)/shard_map/ppermute | solution.py:29
  4.5 4.2 %collective-permute-start.2 = (bf16[72,512]{1,0:T(8,128)(2,1)S(1)}, bf16[72,512]{1,0:T(8,128)(2,1)S(1)}, u32[]{:S(2)}, u32[]{:S(2)}) collective-permute-start(bf16[72,512]{1,0:T(8,128)(2,1)S(1)} %get-tuple-element.28.refs_0_), channel_id=1, source_target_pairs={{0,3},{1,2},{2,1},{3,0},{4,7},{5,6},{6,5},{7,4},{8,11},{9,10},{10,... | collective-permute-start | bytes 221192 | tf_op jit(solution)/shard_map/ppermute | solution.py:29
  9.0 12.7 %collective-permute-start.4 = (bf16[144,1024]{1,0:T(8,128)(2,1)S(1)}, bf16[144,1024]{1,0:T(8,128)(2,1)S(1)}, u32[]{:S(2)}, u32[]{:S(2)}) collective-permute-start(bf16[144,1024]{1,0:T(8,128)(2,1)S(1)} %state0.1), channel_id=1, source_target_pairs={{0,4},{4,8},{8,12},{12,16},{16,20},{20,24},{24,28},{28,0},{1,5},{5... | collective-permute-start | bytes 884744 | tf_op jit(solution)/shard_map/ppermute | solution.py:24
  12.1 4.4 %copy-start.1 = (bf16[2048]{0:T(1024)(128)(2,1)S(1)}, bf16[2048]{0:T(1024)(128)(2,1)}, u32[]{:S(2)}) copy-start(bf16[2048]{0:T(1024)(128)(2,1)} %param.16) | copy-start | bytes 12292
  12.1 14.4 %collective-permute-start.5 = (bf16[128,512]{1,0:T(8,128)(2,1)S(1)}, bf16[128,512]{1,0:T(8,128)(2,1)S(1)}, u32[]{:S(2)}, u32[]{:S(2)}) collective-permute-start(bf16[128,512]{1,0:T(8,128)(2,1)S(1)} %state1024.1), channel_id=1, source_target_pairs={{0,4},{4,8},{8,12},{12,16},{16,20},{20,24},{24,28},{28,0},{1,5},{5... | collective-permute-start | bytes 393224 | tf_op jit(solution)/shard_map/ppermute | solution.py:24
  15.0 7.3 %copy-start = (bf16[512,2048]{1,0:T(8,128)(2,1)S(1)}, bf16[512,2048]{1,0:T(8,128)(2,1)}, u32[]{:S(2)}) copy-start(bf16[512,2048]{1,0:T(8,128)(2,1)} %z_ref.5) | copy-start | bytes 6291460
  15.0 12.9 %collective-permute-start.3 = (bf16[128,512]{1,0:T(8,128)(2,1)S(1)}, bf16[128,512]{1,0:T(8,128)(2,1)S(1)}, u32[]{:S(2)}, u32[]{:S(2)}) collective-permute-start(bf16[128,512]{1,0:T(8,128)(2,1)S(1)} %state1536.1), channel_id=1, source_target_pairs={{0,4},{4,8},{8,12},{12,16},{16,20},{20,24},{24,28},{28,0},{1,5},{5... | collective-permute-start | bytes 393224 | tf_op jit(solution)/shard_map/ppermute | solution.py:24

commit v5 on v4

--- a/solution.py
+++ b/solution.py
@@ -8,6 +8,7 @@
 from jax.sharding import PartitionSpec as P
 
 HDIM = 64
+HDIM_BITS = 6
 DSTATE = 128
 CONV = 4
 CHUNK = 256
@@ -52,8 +53,8 @@
 
 def spread_matrix(copies, heads, low, width):
     shape = (copies * heads, width)
-    head = lax.rem(iota(shape, 0), heads)
-    return jnp.where(head == (iota(shape, 1) + low) // HDIM, 1.0, 0.0).astype(BF16)
+    head = iota(shape, 0) & (heads - 1)
+    return jnp.where(head == (iota(shape, 1) + low) >> HDIM_BITS, 1.0, 0.0).astype(BF16)
 
 
 def call(kernel, in_specs, outs, scratch, name, out_spec=None, alias=None, limit=12):
@@ -112,7 +113,7 @@
 
 
 def prep_kernel(dt_ref, scale_ref, start_ref, x_hbm, *refs):
-    fac_ref, eps_ref, rows_ref, idc_ref, idr_ref, x_ref, sem = refs
+    fac_ref, eps_ref, inv_ref, rows_ref, idc_ref, idr_ref, x_ref, sem = refs
     copy = pltpu.make_async_copy(x_hbm, x_ref, sem)
     copy.start()
     heads = dt_ref.shape[0]
@@ -130,6 +131,8 @@
         mids.append(mid)
         fac_ref[span, :] = parts(jnp.exp(mid - log_decay), 2)
         eps_ref[span, :] = parts(jnp.exp(log_decay - mid), 2)
+        if j == 0:
+            inv_ref[...] = parts(jnp.exp(-log_decay[:EDGE, :]), 2)
         starts = start_ref[:, span].astype(F32).astype(BF16)
         by_row = mm(jnp.broadcast_to(starts, (8, CHUNK)), upper) + offset
         by_col = mm_t(lower, jnp.broadcast_to(starts, (128, CHUNK)))
@@ -201,10 +204,12 @@
         copy.wait()
 
 
-def fix_kernel(x_ref, rim_ref, taps_ref, fac_ref, idc_ref, *refs):
-    shares, bc_ref, xs_ref = refs[:-2], refs[-2], refs[-1]
-    columns = x_ref.shape[1]
-    depth = rim_rows(columns, len(shares), rim_ref.shape[1])
+def fix_kernel(split, flag_ref, x_ref, rim_ref, taps_ref, fac_ref, inv_ref, idc_ref, old_ref, *refs):
+    shares, (live_ref, xe_ref, *exact) = refs[:split], refs[split:]
+    rows, columns = x_ref.shape
+    heads = fac_ref.shape[1] // 2
+    width = shares[0].shape[0] - 8
+    depth = rim_rows(columns, split, rim_ref.shape[1])
     base = rim_ref.shape[0] - depth
 
     def rim(low, size, row):
@@ -212,20 +217,32 @@
         block = rim_ref[base:, lane : lane + size].astype(F32)
         return pltpu.roll(block, (row - 3 * slot) % depth, 0)[:8]
 
-    heads = fac_ref.shape[1] // 2
-    width = shares[0].shape[0] - 8
     live = idc_ref[:8, :] == 0.0
-    lane = iota((width, 128), 1)
+    row, lane = iota((8, 128), 0), iota((width, 128), 1)
+    firsts = []
     for index, share in enumerate(shares):
-        low = columns + index * 128
         own = share[width:, :128].astype(F32)
-        after = jnp.where(live, rim(low, 128, 0), 0.0)
-        total = own + after
+        total = own + jnp.where(live, rim(columns + index * 128, 128, 0), 0.0)
         total = total + pltpu.roll(total, 64, 1)
         value = total / (1.0 + jnp.exp(-total))
-        value = jnp.concatenate([value, jnp.zeros((120, 128), F32)], axis=0).T[:width, :]
-        first = jnp.where(lane < 3, value, share[:width, :128].astype(F32))
-        bc_ref[index * width : (index + 1) * width, :] = first.astype(BF16)
+        firsts.append(value[:, :width])
+        if exact:
+            value = jnp.concatenate([value, jnp.zeros((120, 128), F32)], axis=0).T[:width, :]
+            first = jnp.where(lane < 3, value, share[:width, :128].astype(F32))
+            exact[0][index * width : (index + 1) * width, :] = first.astype(BF16)
+    near = jnp.concatenate(firsts[: split // 2], axis=1)
+    far = jnp.concatenate(firsts[split // 2 :], axis=1)
+    own = flag_ref[0, 0] == 1
+    b_edge, c_edge = jnp.where(own, near, far), jnp.where(own, far, near)
+    b_edge = jnp.where((row < 3) & live, b_edge, 0.0)
+    b_edge = jnp.concatenate([b_edge, jnp.zeros((120, DSTATE), F32)], axis=0).astype(BF16)
+    old = old_ref[:EDGE, :].astype(F32)
+    c_edge = jnp.where(row < 3, jnp.where(live, c_edge, 0.0), old[:8])
+    c_edge = jnp.concatenate([c_edge, old[8:]], axis=0).astype(BF16)
+    c_all = jnp.concatenate([c_edge, old_ref[EDGE:, :]], axis=0)
+    live_ref[:, :DSTATE] = c_all
+    ahead = (iota((rows, 128), 0) >= iota((rows, 128), 1)) & (iota((rows, 128), 1) < 3)
+    live_ref[:, DSTATE:] = jnp.where(ahead, mm_t(c_all, b_edge), 0.0).astype(BF16)
     ids = jnp.concatenate([jnp.zeros((8, 128), F32), idc_ref[:EDGE, :]], axis=0)
     masks = []
     for back in range(1, CONV):
@@ -234,15 +251,17 @@
     for low in range(0, columns, WIDE):
         cols = slice(low, low + WIDE)
         taps = 0.5 * taps_ref[:, cols].astype(F32)
-        above = rim(low, WIDE, 5)
-        padded = jnp.concatenate([above, x_ref[:EDGE, cols].astype(F32)], axis=0)
+        padded = jnp.concatenate([rim(low, WIDE, 5), x_ref[:EDGE, cols].astype(F32)], axis=0)
         half = padded[8:] * taps[CONV - 1 : CONV, :]
         for back in range(1, CONV):
             piece = pltpu.roll(padded, back, 0)[8:] * masks[back - 1]
             half = half + piece * taps[CONV - 1 - back : CONV - back, :]
         value = half + half * jnp.tanh(half)
-        factor = mm(fac_ref[:EDGE, :], spread_matrix(2, heads, low, WIDE))
-        xs_ref[:, cols] = (value * factor).astype(BF16)
+        spread = spread_matrix(2, heads, low, WIDE)
+        edge = jnp.where(iota(value.shape, 0) < 3, value * mm(inv_ref[...], spread), 0.0)
+        xe_ref[:, cols] = edge.astype(BF16)
+        if exact:
+            exact[1][:, cols] = (value * mm(fac_ref[:EDGE, :], spread)).astype(BF16)
 
 
 def conv_kernel(low, x_ref, taps_ref, fac_ref, idc_ref, out_ref, ids_ref, mask_ref):
@@ -296,10 +315,6 @@
     return jnp.where(idr_ref[:1, span] == end, b_rows[:, span], 0.0).astype(BF16)
 
 
-def opening(xs_ref, edge_ref, here, cols):
-    return jnp.concatenate([edge_ref[:, cols], xs_ref[EDGE:CHUNK, here]], axis=0)
-
-
 def state_kernel(low, split, carries, flag_ref, *refs):
     xs_ref, rows_ref, idr_ref, *edges, end_ref = refs[split:]
     if carries:
@@ -311,7 +326,9 @@
     for block in range(xs_ref.shape[1] // WIDE):
         here = slice(block * WIDE, (block + 1) * WIDE)
         cols = slice(low + block * WIDE, low + (block + 1) * WIDE)
-        values = opening(xs_ref, edges[1], here, cols) if edges else xs_ref[:CHUNK, here]
+        values = xs_ref[:CHUNK, here]
+        if edges:
+            values = jnp.concatenate([edges[1][:, cols], values[EDGE:]], axis=0)
         first = mm(pieces[0], values)
         second = mm(pieces[1], xs_ref[CHUNK:, here])
         end = first * rows_ref[1:2, cols] + second * rows_ref[2:3, cols]
@@ -319,8 +336,10 @@
 
 
 def score_kernel(split, flag_ref, *refs):
-    edge_ref, idc_ref, idr_ref, g_ref, live_ref, carried_ref, ending_ref = refs[split:]
-    b_rows, c_rows = pick(flag_ref[0, 0], refs[:split], edge_ref)
+    idc_ref, idr_ref, g_ref, live_ref, carried_ref, ending_ref = refs[split:]
+    b_rows, c_rows = pick(flag_ref[0, 0], refs[:split])
+    rim = (iota((1, b_rows.shape[1]), 1) < 3) & (idr_ref[:1, :] == 0.0)
+    b_rows = jnp.where(rim, 0.0, b_rows)
     ending_ref[...] = ending(b_rows, idr_ref, 0)
     b_rows = b_rows.astype(BF16)
     c_cols = c_rows.T
@@ -338,14 +357,14 @@
     carried_ref[...] = jnp.where(ids == before, c_cols[CHUNK:, :], 0.0).astype(BF16)
 
 
-def local_kernel(low, xs_ref, edge_ref, g_ref, carried_ref, ending_ref, eps_ref, rows_ref, z_ref, y_ref, dec_ref):
+def local_kernel(low, xs_ref, g_ref, carried_ref, ending_ref, eps_ref, rows_ref, z_ref, y_ref, dec_ref):
     heads = eps_ref.shape[1] // 2
     for block in range(xs_ref.shape[1] // WIDE):
         start = low + block * WIDE
         here = slice(block * WIDE, (block + 1) * WIDE)
         cols = slice(start, start + WIDE)
         spread = spread_matrix(2, heads, start, WIDE)
-        values = opening(xs_ref, edge_ref, here, cols)
+        values = xs_ref[:CHUNK, here]
         middle = (mm(ending_ref[...], values) * rows_ref[0:1, cols]).astype(BF16)
         for j in range(2):
             span = slice(j * CHUNK, (j + 1) * CHUNK)
@@ -359,24 +378,28 @@
             dec_ref[span, here] = rows_ref[3 + j : 4 + j, cols] * gate
 
 
-def final_kernel(low, state_ref, y_ref, dec_ref, live_ref, gain_ref, *refs):
+def final_kernel(low, state_ref, edge_ref, y_ref, dec_ref, live_ref, gain_ref, *refs):
     out_ref, buffer, sem = refs[-3:]
     square = (WIDE, WIDE)
-    same = iota(square, 0) // HDIM == iota(square, 1) // HDIM
+    same = iota(square, 0) >> HDIM_BITS == iota(square, 1) >> HDIM_BITS
     mean_matrix = jnp.where(same, 1.0 / HDIM, 0.0).astype(BF16)
+    empty = jnp.zeros((DSTATE - EDGE, WIDE), BF16)
     copies = []
     for block in range(y_ref.shape[1] // WIDE):
         here = slice(block * WIDE, (block + 1) * WIDE)
         cols = slice(low + block * WIDE, low + (block + 1) * WIDE)
         gain = gain_ref[:, cols].astype(F32)
+        state = jnp.concatenate([state_ref[:DSTATE, here], edge_ref[:, cols], empty], axis=0)
         for j in range(2):
             span = slice(j * CHUNK, (j + 1) * CHUNK)
-            mixed = y_ref[span, here] + mm(live_ref[span, :], state_ref[:DSTATE, here]) * dec_ref[span, here]
+            mixed = y_ref[span, here] + mm(live_ref[span, :], state) * dec_ref[span, here]
             mean = mm((mixed * mixed).astype(BF16), mean_matrix)
             buffer[block, span, :] = (mixed * lax.rsqrt(mean + 1e-05) * gain).astype(BF16)
-        copy = pltpu.make_async_copy(buffer.at[block], out_ref.at[:, cols], sem.at[block])
-        copy.start()
-        copies.append(copy)
+            copy = pltpu.make_async_copy(
+                buffer.at[block, span], out_ref.at[span, cols], sem.at[block, j]
+            )
+            copy.start()
+            copies.append(copy)
     for copy in copies:
         copy.wait()
 
@@ -418,12 +441,13 @@
         in_hbm(conv_x),
     )
     shares = [own] + [crossed(own, "head", mask) for mask in range(1, split)]
-    fac, eps, table, ids_col, ids_row, x_near = call(
+    fac, eps, inv, table, ids_col, ids_row, x_near = call(
         prep_kernel,
         [spec] * 3 + [hbm],
         [
             shape((rows, 2 * heads), BF16),
             shape((rows, 2 * heads), BF16),
+            shape((EDGE, 2 * heads), BF16),
             shape((8, columns), F32),
             shape((rows, 128), F32),
             shape((8, rows), F32),
@@ -440,19 +464,29 @@
     gain = norm_gain.reshape(1, columns)
     extra = rim_rows(columns, split, widths[0])
 
+    score_shapes = [
+        shape((2, CHUNK, CHUNK), BF16),
+        shape((rows, DSTATE), BF16),
+        shape((CHUNK, DSTATE), BF16),
+        shape((DSTATE, CHUNK), BF16),
+    ]
+    scores, old, carried, ended = call(
+        functools.partial(score_kernel, split), [smem] + [spec] * (split + 2), score_shapes, (), "score"
+    )(flag, *shares, ids_col, ids_row)
+
     def fixed(rim):
-        return call(
-            fix_kernel,
-            [spec] * (5 + split),
-            [shape((2 * DSTATE, 128), BF16), shape((EDGE, columns), BF16)],
-            (),
-            "fix",
-        )(x_near, rim, taps, fac, ids_col, *shares)
+        shapes = [shape((rows, 2 * DSTATE), BF16), shape((EDGE, columns), BF16)]
+        if turns > 1:
+            shapes += [shape((2 * DSTATE, 128), BF16), shape((EDGE, columns), BF16)]
+        kernel = functools.partial(fix_kernel, split)
+        return call(kernel, [smem] + [spec] * (7 + split), shapes, (), "fix")(
+            flag, x_near, rim, taps, fac, inv, ids_col, old, *shares
+        )
 
     edges = []
     if turns > 1:
         tail = call(tail_kernel, [spec] * (2 + split), shape((extra, widths[0]), BF16), (), "tail")
-        edges = fixed(shifted(tail(x_near, starts, *shares), "ctx", 1))
+        live, edge, *edges = fixed(shifted(tail(x_near, starts, *shares), "ctx", 1))
 
     def relay(low, width, end):
         if turns == 1:
@@ -481,31 +515,20 @@
         )(flag, *shares, part, table, ids_row, *others)
         values.append(part)
         incoming.append(relay(low, width, end))
-    edge_bc, edge_x = edges or fixed(incoming[0])
-    scores, live, carried, ended = call(
-        functools.partial(score_kernel, split),
-        [smem] + [spec] * (split + 3),
-        [
-            shape((2, CHUNK, CHUNK), BF16),
-            shape((rows, DSTATE), BF16),
-            shape((CHUNK, DSTATE), BF16),
-            shape((DSTATE, CHUNK), BF16),
-        ],
-        (),
-        "score",
-    )(flag, *shares, edge_bc, ids_col, ids_row)
+    if turns == 1:
+        live, edge = fixed(incoming[0])
     out = None
     for group, (low, width) in enumerate(zip(lows, widths)):
         mixed, decay = call(
             functools.partial(local_kernel, low),
-            [spec] * 8,
+            [spec] * 7,
             [shape((rows, width), F32)] * 2,
             (),
             f"local{low}",
-        )(values[group], edge_x, scores, carried, ended, eps, table, z_in)
+        )(values[group], scores, carried, ended, eps, table, z_in)
         blocks = width // WIDE
-        args = [incoming[group], mixed, decay, live, gain]
-        in_specs = [spec] * 5
+        args = [incoming[group], edge, mixed, decay, live, gain]
+        in_specs = [spec] * 6
         if group > 0:
             args.append(out)
             in_specs.append(hbm)
@@ -513,10 +536,10 @@
             functools.partial(final_kernel, low),
             in_specs,
             shape((rows, columns), BF16),
-            [pltpu.VMEM((blocks, rows, WIDE), BF16), pltpu.SemaphoreType.DMA((blocks,))],
+            [pltpu.VMEM((blocks, rows, WIDE), BF16), pltpu.SemaphoreType.DMA((blocks, 2))],
             f"final{low}",
             hbm,
-            {5: 0} if group > 0 else {},
+            {6: 0} if group > 0 else {},
         )(*args)
     return out
 

time: 29.3 us -> 28.3 us (0.966)
  waiting for transfers between devices: 5.92 us -> 4.86 us
    ppermute x3, waiting for transfers between devices: 5.19 us -> 4.12 us  [shifted(): return lax.ppermute(value, axis, pairs)]
  transfers between devices with their start and end apart: 6 -> 6, of which waited for: 2 -> 4; matrix products, arithmetic and copies ran while one was open for 0% -> 0% of each run, Pallas kernels for 41% -> 42%
where the time goes in v5:
time: 28.3 us; the launch traced here: 28.1 us
  Pallas kernels  14.9 us (53%)
  starting transfers between devices  8.14 us (29%)
  waiting for transfers between devices  4.86 us (17%)
    ppermute x3, starting transfers between devices, shifted(): return lax.ppermute(value, axis, pairs)  4.99 us
    ppermute x3, waiting for transfers between devices, shifted(): return lax.ppermute(value, axis, pairs)  4.12 us
    pallas_call x3, Pallas kernels, on_device(): call(functools.partial(final_kernel, low), in_specs, shape((rows, columns...  4.11 us
    pallas_call x3, Pallas kernels, on_device(): call(functools.partial(conv_kernel, low), [spec] * 4, shape((rows, width)...  3.67 us
    ppermute x3, starting transfers between devices, crossed(): lax.ppermute(value, axis, [(source, source ^ mask) for source in range(co...  3.15 us
    pallas_call x3, Pallas kernels, on_device(): call(functools.partial(local_kernel, low), [spec] * 7, [shape((rows, widt...  2.62 us
    pallas_call x1, Pallas kernels, on_device(): call(prep_kernel, [spec] * 3 + [hbm], [shape((rows, 2 * heads), BF16), sh...  1.6 us
    pallas_call x1, Pallas kernels, on_device(): call(bc_kernel, [hbm] * 6, [shape((bc_width + 8, rows), BF16), shape((1,...  1.37 us
  transfers between devices with their start and end apart: 6, of which 4 were waited for; matrix products, arithmetic and copies ran while one was open for 0% of the time, Pallas kernels for 42%

profile of v5, /device:TPU:0, one launch (start us, length us, event | category | flops | bytes accessed | tf_op | source)
XLA Modules:
  0.0 28.1 jit_solution(1917305384502723969)
XLA Ops:
  0.0 1.4 %bc.1 = (bf16[72,512]{1,0:T(8,128)(2,1)S(1)}, s32[1,512]{1,0:T(1,128)S(1)}, f32[32,512]{1,0:T(8,128)S(1)}, f32[1,32]{1,0:T(1,128)S(1)}, bf16[4,2048]{1,0:T(4,128)(2,1)S(1)}) custom-call(bf16[64,512]{1,0:T(8,128)(2,1)} %bitcast.5, bf16[4,64]{1,0:T(4,128)(2,1)} %refs_1_.1, s32[1,512]{1,0:T(1,128)} %bitcast.7, f32[32,512]{1,0:T(8,128)} %bitcast.6, ...), custom_call_target="tpu_custom_call" | custom-call | tf_op jit(solution)/shard_map/bc/pallas_call | solution.py:419
  1.4 0.5 %collective-permute-start = (bf16[72,512]{1,0:T(8,128)(2,1)S(1)}, bf16[72,512]{1,0:T(8,128)(2,1)S(1)}, u32[]{:S(2)}, u32[]{:S(2)}) collective-permute-start(bf16[72,512]{1,0:T(8,128)(2,1)S(1)} %get-tuple-element.29.refs_0_), channel_id=1, source_target_pairs={{0,1},{1,0},{2,3},{3,2},{4,5},{5,4},{6,7},{7,6},{8,9},{9,8},{10,11... | collective-permute-start | bytes 221192 | tf_op jit(solution)/shard_map/ppermute | solution.py:30
  1.9 2.6 %collective-permute-start.1 = (bf16[72,512]{1,0:T(8,128)(2,1)S(1)}, bf16[72,512]{1,0:T(8,128)(2,1)S(1)}, u32[]{:S(2)}, u32[]{:S(2)}) collective-permute-start(bf16[72,512]{1,0:T(8,128)(2,1)S(1)} %get-tuple-element.29.refs_0_), channel_id=1, source_target_pairs={{0,2},{1,3},{2,0},{3,1},{4,6},{5,7},{6,4},{7,5},{8,10},{9,11},{10,... | collective-permute-start | bytes 221192 | tf_op jit(solution)/shard_map/ppermute | solution.py:30
  4.5 1.6 %prep.1 = (bf16[512,64]{1,0:T(8,128)(2,1)S(1)}, bf16[512,64]{1,0:T(8,128)(2,1)S(1)}, bf16[16,64]{1,0:T(8,128)(2,1)S(1)}, f32[8,2048]{1,0:T(8,128)S(1)}, f32[512,...) custom-call(f32[32,512]{1,0:T(8,128)S(1)} %get-tuple-element.30.dt_ref, ...), custom_call_target="tpu_custom_call" | custom-call | tf_op jit(solution)/shard_map/prep/pallas_call | solution.py:444
  6.1 1.8 %conv0.1.refs_4_.xs_ref = bf16[512,1024]{1,0:T(8,128)(2,1)S(1)} custom-call(bf16[512,2048]{1,0:T(8,128)(2,1)S(1)} %get-tuple-element.33.x_ref.refs_7_, bf16[4,2048]{1,0:T(4,128)(2,1)S(1)} %get-tuple-element.34.taps_ref, bf16[512,64]{1,0:T(8,128)(2,1)S(1)} %get-tuple-element.35.fac_ref, f32[512,128]{1,0:T(8,128)S(1)} %get-tuple-element.36.idc_ref.refs_4_), custom_call_target="tpu_custom_call" | custom-call | tf_op jit(solution)/shard_map/conv0/pallas_call | solution.py:500
  7.9 0.7 %collective-permute-done.2.refs_3_ = bf16[72,512]{1,0:T(8,128)(2,1)S(1)} collective-permute-done((bf16[72,512]{1,0:T(8,128)(2,1)S(1)}, bf16[72,512]{1,0:T(8,128)(2,1)S(1)}, u32[]{:S(2)}, u32[]{:S(2)}) %collective-permute-start.2) | collective-permute-done | bytes 73760 | tf_op jit(solution)/shard_map/ppermute | solution.py:30
  8.7 0.4 %state0.1 = bf16[144,1024]{1,0:T(8,128)(2,1)S(1)} custom-call(s32[1,1]{1,0:T(1,128)} %bitcast.flag_ref, bf16[72,512]{1,0:T(8,128)(2,1)S(1)} %get-tuple-element.29.refs_0_, bf16[72,512]{1,0:T(8,128)(2,1)S(1)} %collective-permute-done.refs_1_, bf16[72,512]{1,0:T(8,128)(2,1)S(1)} %collective-permute-done.1.refs_2_, ...), custom_call_target="tpu_custom_call" | custom-call | tf_op jit(solution)/shard_map/state0/pallas_call | solution.py:509
  9.0 1.8 %collective-permute-start.4 = (bf16[144,1024]{1,0:T(8,128)(2,1)S(1)}, bf16[144,1024]{1,0:T(8,128)(2,1)S(1)}, u32[]{:S(2)}, u32[]{:S(2)}) collective-permute-start(bf16[144,1024]{1,0:T(8,128)(2,1)S(1)} %state0.1), channel_id=1, source_target_pairs={{0,4},{4,8},{8,12},{12,16},{16,20},{20,24},{24,28},{28,0},{1,5},{5... | collective-permute-start | bytes 884744 | tf_op jit(solution)/shard_map/ppermute | solution.py:25
  10.9 0.9 %conv1024.1.refs_4_.xs_ref = bf16[512,512]{1,0:T(8,128)(2,1)S(1)} custom-call(bf16[512,2048]{1,0:T(8,128)(2,1)S(1)} %get-tuple-element.33.x_ref.refs_7_, bf16[4,2048]{1,0:T(4,128)(2,1)S(1)} %get-tuple-element.34.taps_ref, bf16[512,64]{1,0:T(8,128)(2,1)S(1)} %get-tuple-element.35.fac_ref, f32[512,128]{1,0:T(8,128)S(1)} %get-tuple-element.36.idc_ref.refs_4_), custom_call_target="tpu_custom_call" | custom-call | tf_op jit(solution)/shard_map/conv1024/pallas_call | solution.py:500
  11.8 0.3 state1024.1
  12.1 1.6 %collective-permute-start.5 = (bf16[128,512]{1,0:T(8,128)(2,1)S(1)}, bf16[128,512]{1,0:T(8,128)(2,1)S(1)}, u32[]{:S(2)}, u32[]{:S(2)}) collective-permute-start(bf16[128,512]{1,0:T(8,128)(2,1)S(1)} %state1024.1), channel_id=1, source_target_pairs={{0,4},{4,8},{8,12},{12,16},{16,20},{20,24},{24,28},{28,0},{1,5},{5... | collective-permute-start | bytes 393224 | tf_op jit(solution)/shard_map/ppermute | solution.py:25
  13.7 0.9 %conv1536.1.refs_4_.xs_ref = bf16[512,512]{1,0:T(8,128)(2,1)S(1)} custom-call(bf16[512,2048]{1,0:T(8,128)(2,1)S(1)} %get-tuple-element.33.x_ref.refs_7_, bf16[4,2048]{1,0:T(4,128)(2,1)S(1)} %get-tuple-element.34.taps_ref, bf16[512,64]{1,0:T(8,128)(2,1)S(1)} %get-tuple-element.35.fac_ref, f32[512,128]{1,0:T(8,128)S(1)} %get-tuple-element.36.idc_ref.refs_4_), custom_call_target="tpu_custom_call" | custom-call | tf_op jit(solution)/shard_map/conv1536/pallas_call | solution.py:500
  15.0 1.6 %collective-permute-start.3 = (bf16[128,512]{1,0:T(8,128)(2,1)S(1)}, bf16[128,512]{1,0:T(8,128)(2,1)S(1)}, u32[]{:S(2)}, u32[]{:S(2)}) collective-permute-start(bf16[128,512]{1,0:T(8,128)(2,1)S(1)} %state1536.1), channel_id=1, source_target_pairs={{0,4},{4,8},{8,12},{12,16},{16,20},{20,24},{24,28},{28,0},{1,5},{5... | collective-permute-start | bytes 393224 | tf_op jit(solution)/shard_map/ppermute | solution.py:25
  16.5 0.3 %score.1 = (bf16[2,256,256]{2,1,0:T(8,128)(2,1)S(1)}, bf16[512,128]{1,0:T(8,128)(2,1)S(1)}, bf16[256,128]{1,0:T(8,128)(2,1)S(1)}, bf16[128,256]{1,0:T(8,128)(2,1)S(1)}) custom-call(s32[1,1]{1,0:T(1,128)} %bitcast.flag_ref, bf16[72,512]{1,0:T(8,128)(2,1)S(1)} %get-tuple-element.29.refs_0_, bf16[72,512]{1,0:T(8,128)(2,1)S(1)} %collective-permute-done.refs_1_, ...), custom_call_target="tpu_custom_call" | custom-call | tf_op jit(solution)/shard_map/score/pallas_call | solution.py:473
  16.8 1.2 %local0.1 = (f32[512,1024]{1,0:T(8,128)S(1)}, f32[512,1024]{1,0:T(8,128)S(1)}) custom-call(bf16[512,1024]{1,0:T(8,128)(2,1)S(1)} %conv0.1.refs_4_.xs_ref, bf16[2,256,256]{2,1,0:T(8,128)(2,1)S(1)} %get-tuple-element.42.g_ref, bf16[256,128]{1,0:T(8,128)(2,1)S(1)} %get-tuple-element.43.carried_ref, bf16[128,256]{1,0:T(8,128)(2,1)S(1)} %get-tuple-element.44.ending_ref, ...), custom_call_target="tpu_custom_call" | custom-call | tf_op jit(solution)/shard_map/local0/pallas_call | solution.py:522
  18.0 0.7 %local1024.1 = (f32[512,512]{1,0:T(8,128)S(1)}, f32[512,512]{1,0:T(8,128)S(1)}) custom-call(bf16[512,512]{1,0:T(8,128)(2,1)S(1)} %conv1024.1.refs_4_.xs_ref, bf16[2,256,256]{2,1,0:T(8,128)(2,1)S(1)} %get-tuple-element.42.g_ref, bf16[256,128]{1,0:T(8,128)(2,1)S(1)} %get-tuple-element.43.carried_ref, bf16[128,256]{1,0:T(8,128)(2,1)S(1)} %get-tuple-element.44.ending_ref, ...), custom_call_target="tpu_custom_call" | custom-call | tf_op jit(solution)/shard_map/local1024/pallas_call | solution.py:522
  18.8 0.7 %local1536.1 = (f32[512,512]{1,0:T(8,128)S(1)}, f32[512,512]{1,0:T(8,128)S(1)}) custom-call(bf16[512,512]{1,0:T(8,128)(2,1)S(1)} %conv1536.1.refs_4_.xs_ref, bf16[2,256,256]{2,1,0:T(8,128)(2,1)S(1)} %get-tuple-element.42.g_ref, bf16[256,128]{1,0:T(8,128)(2,1)S(1)} %get-tuple-element.43.carried_ref, bf16[128,256]{1,0:T(8,128)(2,1)S(1)} %get-tuple-element.44.ending_ref, ...), custom_call_target="tpu_custom_call" | custom-call | tf_op jit(solution)/shard_map/local1536/pallas_call | solution.py:522
  19.5 2.2 %collective-permute-done.4.rim_ref.state_ref = bf16[144,1024]{1,0:T(8,128)(2,1)S(1)} collective-permute-done((bf16[144,1024]{1,0:T(8,128)(2,1)S(1)}, bf16[144,1024]{1,0:T(8,128)(2,1)S(1)}, u32[]{:S(2)}, u32[]{:S(2)}) %collective-permute-start.4) | collective-permute-done | bytes 294944 | tf_op jit(solution)/shard_map/ppermute | solution.py:25
  21.7 0.3 %fix.1 = (bf16[512,256]{1,0:T(8,128)(2,1)S(1)}, bf16[16,2048]{1,0:T(8,128)(2,1)S(1)}) custom-call(s32[1,1]{1,0:T(1,128)} %bitcast.flag_ref, bf16[512,2048]{1,0:T(8,128)(2,1)S(1)} %get-tuple-element.33.x_ref.refs_7_, bf16[144,1024]{1,0:T(8,128)(2,1)S(1)} %collective-permute-done.4.rim_ref.state_ref, bf16[4,2048]{1,0:T(4,128)(2,1)S(1)} %get-tuple-element.34.taps_ref, ...), custom_call_target="tpu_custom_call" | custom-call | tf_op jit(solution)/shard_map/fix/pallas_call | solution.py:482
  22.1 1.6 %final0.1.refs_0_ = bf16[512,2048]{1,0:T(8,128)(2,1)} custom-call(bf16[144,1024]{1,0:T(8,128)(2,1)S(1)} %collective-permute-done.4.rim_ref.state_ref, bf16[16,2048]{1,0:T(8,128)(2,1)S(1)} %get-tuple-element.41.edge_ref, f32[512,1024]{1,0:T(8,128)S(1)} %get-tuple-element.51.y_ref, f32[512,1024]{1,0:T(8,128)S(1)} %get-tuple-element.52.dec_ref, ...), custom_call_target="tpu_custom_call" | custom-call | tf_op jit(solution)/shard_map/final0/pallas_call | solution.py:535
  23.7 0.8 %collective-permute-done.5.state_ref = bf16[128,512]{1,0:T(8,128)(2,1)S(1)} collective-permute-done((bf16[128,512]{1,0:T(8,128)(2,1)S(1)}, bf16[128,512]{1,0:T(8,128)(2,1)S(1)}, u32[]{:S(2)}, u32[]{:S(2)}) %collective-permute-start.5) | collective-permute-done | bytes 131104 | tf_op jit(solution)/shard_map/ppermute | solution.py:25
  24.5 1.2 %final1024.1.refs_0_ = bf16[512,2048]{1,0:T(8,128)(2,1)} custom-call(bf16[128,512]{1,0:T(8,128)(2,1)S(1)} %collective-permute-done.5.state_ref, bf16[16,2048]{1,0:T(8,128)(2,1)S(1)} %get-tuple-element.41.edge_ref, f32[512,512]{1,0:T(8,128)S(1)} %get-tuple-element.49.y_ref, f32[512,512]{1,0:T(8,128)S(1)} %get-tuple-element.50.dec_ref, ...), custom_call_target="tpu_custom_call", output_to_operand_aliasing={{}: (6, {})} | custom-call | tf_op jit(solution)/shard_map/final1024/pallas_call | solution.py:535
  25.8 1.0 %collective-permute-done.3.state_ref = bf16[128,512]{1,0:T(8,128)(2,1)S(1)} collective-permute-done((bf16[128,512]{1,0:T(8,128)(2,1)S(1)}, bf16[128,512]{1,0:T(8,128)(2,1)S(1)}, u32[]{:S(2)}, u32[]{:S(2)}) %collective-permute-start.3) | collective-permute-done | bytes 131104 | tf_op jit(solution)/shard_map/ppermute | solution.py:25
  26.8 1.3 %final1536.1 = bf16[512,2048]{1,0:T(8,128)(2,1)} custom-call(bf16[128,512]{1,0:T(8,128)(2,1)S(1)} %collective-permute-done.3.state_ref, bf16[16,2048]{1,0:T(8,128)(2,1)S(1)} %get-tuple-element.41.edge_ref, f32[512,512]{1,0:T(8,128)S(1)} %get-tuple-element.46.y_ref, f32[512,512]{1,0:T(8,128)S(1)} %get-tuple-element.47.dec_ref, ...), custom_call_target="tpu_custom_call", output_to_operand_aliasing={{}: (6, {})} | custom-call | tf_op jit(solution)/shard_map/final1536/pallas_call | solution.py:535
  (9 shorter events, 0.4 us)
Async XLA Ops:
  1.4 6.6 %collective-permute-start = (bf16[72,512]{1,0:T(8,128)(2,1)S(1)}, bf16[72,512]{1,0:T(8,128)(2,1)S(1)}, u32[]{:S(2)}, u32[]{:S(2)}) collective-permute-start(bf16[72,512]{1,0:T(8,128)(2,1)S(1)} %get-tuple-element.29.refs_0_), channel_id=1, source_target_pairs={{0,1},{1,0},{2,3},{3,2},{4,5},{5,4},{6,7},{7,6},{8,9},{9,8},{10,11... | collective-permute-start | bytes 221192 | tf_op jit(solution)/shard_map/ppermute | solution.py:30
  1.9 6.0 %collective-permute-start.1 = (bf16[72,512]{1,0:T(8,128)(2,1)S(1)}, bf16[72,512]{1,0:T(8,128)(2,1)S(1)}, u32[]{:S(2)}, u32[]{:S(2)}) collective-permute-start(bf16[72,512]{1,0:T(8,128)(2,1)S(1)} %get-tuple-element.29.refs_0_), channel_id=1, source_target_pairs={{0,2},{1,3},{2,0},{3,1},{4,6},{5,7},{6,4},{7,5},{8,10},{9,11},{10,... | collective-permute-start | bytes 221192 | tf_op jit(solution)/shard_map/ppermute | solution.py:30
  4.5 4.2 %collective-permute-start.2 = (bf16[72,512]{1,0:T(8,128)(2,1)S(1)}, bf16[72,512]{1,0:T(8,128)(2,1)S(1)}, u32[]{:S(2)}, u32[]{:S(2)}) collective-permute-start(bf16[72,512]{1,0:T(8,128)(2,1)S(1)} %get-tuple-element.29.refs_0_), channel_id=1, source_target_pairs={{0,3},{1,2},{2,1},{3,0},{4,7},{5,6},{6,5},{7,4},{8,11},{9,10},{10,... | collective-permute-start | bytes 221192 | tf_op jit(solution)/shard_map/ppermute | solution.py:30
  9.0 12.7 %collective-permute-start.4 = (bf16[144,1024]{1,0:T(8,128)(2,1)S(1)}, bf16[144,1024]{1,0:T(8,128)(2,1)S(1)}, u32[]{:S(2)}, u32[]{:S(2)}) collective-permute-start(bf16[144,1024]{1,0:T(8,128)(2,1)S(1)} %state0.1), channel_id=1, source_target_pairs={{0,4},{4,8},{8,12},{12,16},{16,20},{20,24},{24,28},{28,0},{1,5},{5... | collective-permute-start | bytes 884744 | tf_op jit(solution)/shard_map/ppermute | solution.py:25
  12.1 4.4 %copy-start.1 = (bf16[2048]{0:T(1024)(128)(2,1)S(1)}, bf16[2048]{0:T(1024)(128)(2,1)}, u32[]{:S(2)}) copy-start(bf16[2048]{0:T(1024)(128)(2,1)} %param.16) | copy-start | bytes 12292
  12.1 4.7 %copy-start = (bf16[512,2048]{1,0:T(8,128)(2,1)S(1)}, bf16[512,2048]{1,0:T(8,128)(2,1)}, u32[]{:S(2)}) copy-start(bf16[512,2048]{1,0:T(8,128)(2,1)} %z_ref.5) | copy-start | bytes 6291460
  12.1 12.4 %collective-permute-start.5 = (bf16[128,512]{1,0:T(8,128)(2,1)S(1)}, bf16[128,512]{1,0:T(8,128)(2,1)S(1)}, u32[]{:S(2)}, u32[]{:S(2)}) collective-permute-start(bf16[128,512]{1,0:T(8,128)(2,1)S(1)} %state1024.1), channel_id=1, source_target_pairs={{0,4},{4,8},{8,12},{12,16},{16,20},{20,24},{24,28},{28,0},{1,5},{5... | collective-permute-start | bytes 393224 | tf_op jit(solution)/shard_map/ppermute | solution.py:25
  15.0 11.9 %collective-permute-start.3 = (bf16[128,512]{1,0:T(8,128)(2,1)S(1)}, bf16[128,512]{1,0:T(8,128)(2,1)S(1)}, u32[]{:S(2)}, u32[]{:S(2)}) collective-permute-start(bf16[128,512]{1,0:T(8,128)(2,1)S(1)} %state1536.1), channel_id=1, source_target_pairs={{0,4},{4,8},{8,12},{12,16},{16,20},{20,24},{24,28},{28,0},{1,5},{5... | collective-permute-start | bytes 393224 | tf_op jit(solution)/shard_map/ppermute | solution.py:25

commit v6 on v5

--- a/solution.py
+++ b/solution.py
@@ -13,7 +13,8 @@
 CONV = 4
 CHUNK = 256
 WIDE = 256
-SHARES = (4, 2, 2)
+PIECES = 4
+GROUPS = ((0, 1), (2,), (3,))
 EDGE = 16
 F32 = jnp.float32
 BF16 = jnp.bfloat16
@@ -69,6 +70,25 @@
         compiler_params=pltpu.CompilerParams(vmem_limit_bytes=limit << 20),
         name=name,
     )
+
+
+def order_of(split):
+    masks = [0]
+    mask = split // 2
+    while mask:
+        masks += [held | mask for held in masks]
+        mask //= 2
+    return masks
+
+
+def by_mask(refs, split):
+    size = refs[0].shape[0] * 2 // split
+    views = []
+    for place in range(split):
+        ref, row = refs[place * 2 // split], place % (split // 2) * size
+        views.append(ref.at[row : row + size, :])
+    order = order_of(split)
+    return [views[order.index(mask)] for mask in range(split)]
 
 
 def rim_rows(columns, split, width):
@@ -108,8 +128,9 @@
     return block.astype(BF16)
 
 
-def tail_kernel(x_ref, start_ref, *refs):
-    refs[-1][...] = rim_block(x_ref, start_ref, refs[:-1], refs[-1].shape[1])
+def tail_kernel(split, x_ref, start_ref, *refs):
+    shares = by_mask(refs[:2], split)
+    refs[-1][...] = rim_block(x_ref, start_ref, shares, refs[-1].shape[1])
 
 
 def prep_kernel(dt_ref, scale_ref, start_ref, x_hbm, *refs):
@@ -204,8 +225,8 @@
         copy.wait()
 
 
-def fix_kernel(split, flag_ref, x_ref, rim_ref, taps_ref, fac_ref, inv_ref, idc_ref, old_ref, *refs):
-    shares, (live_ref, xe_ref, *exact) = refs[:split], refs[split:]
+def fix_kernel(split, x_ref, rim_ref, taps_ref, fac_ref, inv_ref, idc_ref, old_ref, *refs):
+    shares, (live_ref, xe_ref, *exact) = by_mask(refs[:2], split), refs[2:]
     rows, columns = x_ref.shape
     heads = fac_ref.shape[1] // 2
     width = shares[0].shape[0] - 8
@@ -232,7 +253,7 @@
             exact[0][index * width : (index + 1) * width, :] = first.astype(BF16)
     near = jnp.concatenate(firsts[: split // 2], axis=1)
     far = jnp.concatenate(firsts[split // 2 :], axis=1)
-    own = flag_ref[0, 0] == 1
+    own = lax.axis_index("head") < split // 2
     b_edge, c_edge = jnp.where(own, near, far), jnp.where(own, far, near)
     b_edge = jnp.where((row < 3) & live, b_edge, 0.0)
     b_edge = jnp.concatenate([b_edge, jnp.zeros((120, DSTATE), F32)], axis=0).astype(BF16)
@@ -264,7 +285,11 @@
             exact[1][:, cols] = (value * mm(fac_ref[:EDGE, :], spread)).astype(BF16)
 
 
-def conv_kernel(low, x_ref, taps_ref, fac_ref, idc_ref, out_ref, ids_ref, mask_ref):
+def conv_kernel(low, x_ref, taps_ref, fac_ref, idc_ref, *refs):
+    out_ref, ids_ref, mask_ref = refs[-3:]
+    if len(refs) > 3:
+        out_ref = refs[1]
+        refs[2][...] = refs[0][...]
     rows = x_ref.shape[0]
     heads = fac_ref.shape[1] // 2
     ids_ref[:8, :] = jnp.zeros((8, 128), F32)
@@ -296,7 +321,7 @@
             out_ref[span, block * WIDE : (block + 1) * WIDE] = (value * factor[span]).astype(BF16)
 
 
-def pick(flag, refs, first=None):
+def pick(refs, first=None):
     half = len(refs) // 2
     width = refs[0].shape[0] - 8
     near = jnp.concatenate([ref[:width, :] for ref in refs[:half]], axis=0).astype(F32)
@@ -305,7 +330,7 @@
         edge = first[...].astype(F32)
         near = jnp.concatenate([edge[:DSTATE], near[:, 128:]], axis=1)
         far = jnp.concatenate([edge[DSTATE:], far[:, 128:]], axis=1)
-    own = flag == 1
+    own = lax.axis_index("head") < half
     return jnp.where(own, near, far), jnp.where(own, far, near)
 
 
@@ -315,29 +340,32 @@
     return jnp.where(idr_ref[:1, span] == end, b_rows[:, span], 0.0).astype(BF16)
 
 
-def state_kernel(low, split, carries, flag_ref, *refs):
-    xs_ref, rows_ref, idr_ref, *edges, end_ref = refs[split:]
+def state_kernel(low, split, count, carries, *refs):
+    xs_refs = refs[2 : 2 + count]
+    rows_ref, idr_ref, *edges, end_ref = refs[2 + count :]
     if carries:
         x_ref, start_ref = edges
         edges = []
-        end_ref[DSTATE:, :] = rim_block(x_ref, start_ref, refs[:split], end_ref.shape[1])
-    b_rows, _ = pick(flag_ref[0, 0], refs[:split], edges[0] if edges else None)
+        end_ref[DSTATE:, :] = rim_block(x_ref, start_ref, by_mask(refs[:2], split), end_ref.shape[1])
+    b_rows, _ = pick(by_mask(refs[:2], split), edges[0] if edges else None)
     pieces = [ending(b_rows, idr_ref, j) for j in range(2)]
-    for block in range(xs_ref.shape[1] // WIDE):
+    each = xs_refs[0].shape[1] // WIDE
+    for block in range(each * count):
+        xs_ref, part = xs_refs[block // each], slice(block % each * WIDE, (block % each + 1) * WIDE)
         here = slice(block * WIDE, (block + 1) * WIDE)
         cols = slice(low + block * WIDE, low + (block + 1) * WIDE)
-        values = xs_ref[:CHUNK, here]
+        values = xs_ref[:CHUNK, part]
         if edges:
             values = jnp.concatenate([edges[1][:, cols], values[EDGE:]], axis=0)
         first = mm(pieces[0], values)
-        second = mm(pieces[1], xs_ref[CHUNK:, here])
+        second = mm(pieces[1], xs_ref[CHUNK:, part])
         end = first * rows_ref[1:2, cols] + second * rows_ref[2:3, cols]
         end_ref[:DSTATE, here] = end.astype(end_ref.dtype)
 
 
-def score_kernel(split, flag_ref, *refs):
-    idc_ref, idr_ref, g_ref, live_ref, carried_ref, ending_ref = refs[split:]
-    b_rows, c_rows = pick(flag_ref[0, 0], refs[:split])
+def score_kernel(split, *refs):
+    idc_ref, idr_ref, g_ref, live_ref, carried_ref, ending_ref = refs[2:]
+    b_rows, c_rows = pick(by_mask(refs[:2], split))
     rim = (iota((1, b_rows.shape[1]), 1) < 3) & (idr_ref[:1, :] == 0.0)
     b_rows = jnp.where(rim, 0.0, b_rows)
     ending_ref[...] = ending(b_rows, idr_ref, 0)
@@ -357,21 +385,25 @@
     carried_ref[...] = jnp.where(ids == before, c_cols[CHUNK:, :], 0.0).astype(BF16)
 
 
-def local_kernel(low, xs_ref, g_ref, carried_ref, ending_ref, eps_ref, rows_ref, z_ref, y_ref, dec_ref):
+def local_kernel(low, *refs):
+    xs_refs = refs[:-8]
+    g_ref, carried_ref, ending_ref, eps_ref, rows_ref, z_ref, y_ref, dec_ref = refs[-8:]
     heads = eps_ref.shape[1] // 2
-    for block in range(xs_ref.shape[1] // WIDE):
+    each = xs_refs[0].shape[1] // WIDE
+    for block in range(each * len(xs_refs)):
+        xs_ref, part = xs_refs[block // each], slice(block % each * WIDE, (block % each + 1) * WIDE)
         start = low + block * WIDE
         here = slice(block * WIDE, (block + 1) * WIDE)
         cols = slice(start, start + WIDE)
         spread = spread_matrix(2, heads, start, WIDE)
-        values = xs_ref[:CHUNK, here]
+        values = xs_ref[:CHUNK, part]
         middle = (mm(ending_ref[...], values) * rows_ref[0:1, cols]).astype(BF16)
         for j in range(2):
             span = slice(j * CHUNK, (j + 1) * CHUNK)
             if j == 0:
                 y = mm(g_ref[0], values)
             else:
-                y = mm(g_ref[1], xs_ref[span, here]) + mm(carried_ref[...], middle)
+                y = mm(g_ref[1], xs_ref[span, part]) + mm(carried_ref[...], middle)
             half = 0.5 * z_ref[span, cols].astype(F32)
             gate = (half + half * jnp.tanh(half)) * mm(eps_ref[span, :], spread)
             y_ref[span, here] = y * gate
@@ -412,7 +444,6 @@
     split = lax.axis_size("head")
     starts = doc_start.reshape(1, rows)
     spec = pl.BlockSpec(memory_space=pltpu.VMEM)
-    smem = pl.BlockSpec(memory_space=pltpu.SMEM)
     hbm = pl.BlockSpec(memory_space=pltpu.HBM)
     shape = jax.ShapeDtypeStruct
     in_hbm = lambda value: pltpu.with_memory_space_constraint(value, pltpu.HBM)
@@ -440,7 +471,7 @@
         in_hbm(decay_scale.reshape(1, heads)),
         in_hbm(conv_x),
     )
-    shares = [own] + [crossed(own, "head", mask) for mask in range(1, split)]
+    far = crossed(own, "head", split // 2)
     fac, eps, inv, table, ids_col, ids_row, x_near = call(
         prep_kernel,
         [spec] * 3 + [hbm],
@@ -456,10 +487,26 @@
         [pltpu.SemaphoreType.DMA],
         "prep",
     )(steps, scale, starts, in_hbm(x_in))
-    flag = (lax.axis_index("head") < split // 2).astype(jnp.int32).reshape(1, 1)
-    total = sum(SHARES)
-    widths = [columns * share // total for share in SHARES]
-    lows = [sum(widths[:group]) for group in range(len(widths))]
+    width = columns // PIECES
+    values = []
+    for piece in range(PIECES):
+        kept = [own] if piece == 0 else []
+        part, *kept = call(
+            functools.partial(conv_kernel, piece * width),
+            [spec] * (4 + len(kept)),
+            [shape((rows, width), BF16)] + [shape(own.shape, BF16)] * len(kept),
+            [pltpu.VMEM((rows + 8, 128), F32), pltpu.VMEM((CONV - 1, rows, 128), F32)],
+            f"conv{piece}",
+        )(x_near, taps, fac, ids_col, *kept)
+        values.append(part)
+        if piece == 0:
+            ours, mask = jnp.concatenate([*kept, far], axis=0), split // 4
+    while mask > 1:
+        ours = jnp.concatenate([ours, crossed(ours, "head", mask)], axis=0)
+        mask //= 2
+    shares = [ours, crossed(ours, "head", 1)]
+    widths = [width * len(group) for group in GROUPS]
+    lows = [width * group[0] for group in GROUPS]
     state_type = BF16 if turns == 1 else F32
     gain = norm_gain.reshape(1, columns)
     extra = rim_rows(columns, split, widths[0])
@@ -471,21 +518,22 @@
         shape((DSTATE, CHUNK), BF16),
     ]
     scores, old, carried, ended = call(
-        functools.partial(score_kernel, split), [smem] + [spec] * (split + 2), score_shapes, (), "score"
-    )(flag, *shares, ids_col, ids_row)
+        functools.partial(score_kernel, split), [spec] * 4, score_shapes, (), "score"
+    )(*shares, ids_col, ids_row)
 
     def fixed(rim):
         shapes = [shape((rows, 2 * DSTATE), BF16), shape((EDGE, columns), BF16)]
         if turns > 1:
             shapes += [shape((2 * DSTATE, 128), BF16), shape((EDGE, columns), BF16)]
         kernel = functools.partial(fix_kernel, split)
-        return call(kernel, [smem] + [spec] * (7 + split), shapes, (), "fix")(
-            flag, x_near, rim, taps, fac, inv, ids_col, old, *shares
+        return call(kernel, [spec] * 9, shapes, (), "fix")(
+            x_near, rim, taps, fac, inv, ids_col, old, *shares
         )
 
     edges = []
     if turns > 1:
-        tail = call(tail_kernel, [spec] * (2 + split), shape((extra, widths[0]), BF16), (), "tail")
+        kernel = functools.partial(tail_kernel, split)
+        tail = call(kernel, [spec] * 4, shape((extra, widths[0]), BF16), (), "tail")
         live, edge, *edges = fixed(shifted(tail(x_near, starts, *shares), "ctx", 1))
 
     def relay(low, width, end):
@@ -495,37 +543,31 @@
         turn = lambda _, incoming: shifted(through * incoming + end, "ctx", 1)
         return lax.fori_loop(0, turns, turn, jnp.zeros_like(end)).astype(BF16)
 
-    values, incoming = [], []
-    for low, width in zip(lows, widths):
-        part = call(
-            functools.partial(conv_kernel, low),
-            [spec] * 4,
-            shape((rows, width), BF16),
-            [pltpu.VMEM((rows + 8, 128), F32), pltpu.VMEM((CONV - 1, rows, 128), F32)],
-            f"conv{low}",
-        )(x_near, taps, fac, ids_col)
+    incoming = []
+    for group, low, width in zip(GROUPS, lows, widths):
+        pieces = [values[piece] for piece in group]
         carries = turns == 1 and low == 0
         others = [x_near, starts] if carries else edges
         end = call(
-            functools.partial(state_kernel, low, split, carries),
-            [smem] + [spec] * (split + 3 + len(others)),
+            functools.partial(state_kernel, low, split, len(pieces), carries),
+            [spec] * (4 + len(pieces) + len(others)),
             shape((DSTATE + extra if carries else DSTATE, width), state_type),
             (),
             f"state{low}",
-        )(flag, *shares, part, table, ids_row, *others)
-        values.append(part)
+        )(*shares, *pieces, table, ids_row, *others)
         incoming.append(relay(low, width, end))
     if turns == 1:
         live, edge = fixed(incoming[0])
     out = None
     for group, (low, width) in enumerate(zip(lows, widths)):
+        pieces = [values[piece] for piece in GROUPS[group]]
         mixed, decay = call(
             functools.partial(local_kernel, low),
-            [spec] * 7,
+            [spec] * (6 + len(pieces)),
             [shape((rows, width), F32)] * 2,
             (),
             f"local{low}",
-        )(values[group], scores, carried, ended, eps, table, z_in)
+        )(*pieces, scores, carried, ended, eps, table, z_in)
         blocks = width // WIDE
         args = [incoming[group], edge, mixed, decay, live, gain]
         in_specs = [spec] * 6

time: 28.3 us -> 28 us (0.989)
    ppermute x3 -> x2, waiting for transfers between devices: 0.74 us -> 0.41 us  [crossed(): lax.ppermute(value, axis, [(source, source ^ mask) for source in range(co...]
    pallas_call x11 -> x12, Pallas kernels: 7.83 us -> 7.93 us  [the longest x4 3.78 us: on_device(): call(functools.partial(conv_kernel, piece * width), [spec] * (4 + len(kep...]
    ppermute x3 -> x2, starting transfers between devices: 3.15 us -> 3.07 us  [crossed(): lax.ppermute(value, axis, [(source, source ^ mask) for source in range(co...]
  transfers between devices with their start and end apart: 6 -> 5, of which waited for: 4 -> 4; matrix products, arithmetic and copies ran while one was open for 0% -> 0% of each run, Pallas kernels for 42% -> 43%
where the time goes in v6:
time: 28 us; the launch traced here: 27.8 us
  Pallas kernels  15 us (54%)
  starting transfers between devices  8.01 us (29%)
  waiting for transfers between devices  4.62 us (16%)
    ppermute x3, starting transfers between devices, shifted(): return lax.ppermute(value, axis, pairs)  4.93 us
    ppermute x3, waiting for transfers between devices, shifted(): return lax.ppermute(value, axis, pairs)  4.22 us
    pallas_call x3, Pallas kernels, on_device(): call(functools.partial(final_kernel, low), in_specs, shape((rows, columns...  4.06 us
    pallas_call x4, Pallas kernels, on_device(): call(functools.partial(conv_kernel, piece * width), [spec] * (4 + len(kep...  3.78 us
    ppermute x2, starting transfers between devices, crossed(): lax.ppermute(value, axis, [(source, source ^ mask) for source in range(co...  3.07 us
    pallas_call x3, Pallas kernels, on_device(): call(functools.partial(local_kernel, low), [spec] * (6 + len(pieces)), [s...  2.6 us
    pallas_call x1, Pallas kernels, on_device(): call(prep_kernel, [spec] * 3 + [hbm], [shape((rows, 2 * heads), BF16), sh...  1.6 us
    pallas_call x1, Pallas kernels, on_device(): call(bc_kernel, [hbm] * 6, [shape((bc_width + 8, rows), BF16), shape((1,...  1.37 us
  transfers between devices with their start and end apart: 5, of which 4 were waited for; matrix products, arithmetic and copies ran while one was open for 0% of the time, Pallas kernels for 43%

profile of v6, /device:TPU:0, one launch (start us, length us, event | category | flops | bytes accessed | tf_op | source)
XLA Modules:
  0.0 27.8 jit_solution(1946123154972441425)
XLA Ops:
  0.0 1.4 %bc.1 = (bf16[72,512]{1,0:T(8,128)(2,1)S(1)}, s32[1,512]{1,0:T(1,128)S(1)}, f32[32,512]{1,0:T(8,128)S(1)}, f32[1,32]{1,0:T(1,128)S(1)}, bf16[4,2048]{1,0:T(4,128)(2,1)S(1)}) custom-call(bf16[64,512]{1,0:T(8,128)(2,1)} %bitcast.4, bf16[4,64]{1,0:T(4,128)(2,1)} %refs_1_.1, s32[1,512]{1,0:T(1,128)} %bitcast.6, f32[32,512]{1,0:T(8,128)} %bitcast.5, ...), custom_call_target="tpu_custom_call" | custom-call | tf_op jit(solution)/shard_map/bc/pallas_call | solution.py:450
  1.4 3.0 %collective-permute-start = (bf16[72,512]{1,0:T(8,128)(2,1)S(1)}, bf16[72,512]{1,0:T(8,128)(2,1)S(1)}, u32[]{:S(2)}, u32[]{:S(2)}) collective-permute-start(bf16[72,512]{1,0:T(8,128)(2,1)S(1)} %get-tuple-element.38.refs_0_), channel_id=1, source_target_pairs={{0,2},{1,3},{2,0},{3,1},{4,6},{5,7},{6,4},{7,5},{8,10},{9,11},{10,... | collective-permute-start | bytes 221192 | tf_op jit(solution)/shard_map/ppermute | solution.py:31
  4.4 1.6 %prep.1 = (bf16[512,64]{1,0:T(8,128)(2,1)S(1)}, bf16[512,64]{1,0:T(8,128)(2,1)S(1)}, bf16[16,64]{1,0:T(8,128)(2,1)S(1)}, f32[8,2048]{1,0:T(8,128)S(1)}, f32[512,...) custom-call(f32[32,512]{1,0:T(8,128)S(1)} %get-tuple-element.31.dt_ref, ...), custom_call_target="tpu_custom_call" | custom-call | tf_op jit(solution)/shard_map/prep/pallas_call | solution.py:475
  6.0 0.9 %conv0.1 = (bf16[512,512]{1,0:T(8,128)(2,1)S(1)}, bf16[72,512]{1,0:T(8,128)(2,1)S(1)}) custom-call(bf16[512,2048]{1,0:T(8,128)(2,1)S(1)} %get-tuple-element.34.x_ref.refs_6_, bf16[4,2048]{1,0:T(4,128)(2,1)S(1)} %get-tuple-element.35.taps_ref, bf16[512,64]{1,0:T(8,128)(2,1)S(1)} %get-tuple-element.36.fac_ref, ...), custom_call_target="tpu_custom_call" | custom-call | tf_op jit(solution)/shard_map/conv0/pallas_call | solution.py:494
  7.1 0.9 %conv1.1.refs_3_.refs_1_ = bf16[512,512]{1,0:T(8,128)(2,1)S(1)} custom-call(bf16[512,2048]{1,0:T(8,128)(2,1)S(1)} %get-tuple-element.34.x_ref.refs_6_, bf16[4,2048]{1,0:T(4,128)(2,1)S(1)} %get-tuple-element.35.taps_ref, bf16[512,64]{1,0:T(8,128)(2,1)S(1)} %get-tuple-element.36.fac_ref, f32[512,128]{1,0:T(8,128)S(1)} %get-tuple-element.37.idc_ref.refs_2_), custom_call_target="tpu_custom_call" | custom-call | tf_op jit(solution)/shard_map/conv1/pallas_call | solution.py:494
  8.0 0.4 %collective-permute-done.1.refs_1_ = bf16[144,512]{1,0:T(8,128)(2,1)S(1)} collective-permute-done((bf16[144,512]{1,0:T(8,128)(2,1)S(1)}, bf16[144,512]{1,0:T(8,128)(2,1)S(1)}, u32[]{:S(2)}, u32[]{:S(2)}) %collective-permute-start.1) | collective-permute-done | bytes 147488 | tf_op jit(solution)/shard_map/ppermute | solution.py:31
  8.4 0.4 %state0.1 = bf16[144,1024]{1,0:T(8,128)(2,1)S(1)} custom-call(bf16[144,512]{1,0:T(8,128)(2,1)S(1)} %constant_dynamic-update-slice_fusion.refs_0_, bf16[144,512]{1,0:T(8,128)(2,1)S(1)} %collective-permute-done.1.refs_1_, bf16[512,512]{1,0:T(8,128)(2,1)S(1)} %get-tuple-element.42.refs_2_.refs_0_, bf16[512,512]{1,0:T(8,128)(2,1)S(1)} %conv1.1.refs_3_.refs_1_, ...), custom_call_target="tpu_custom_call" | custom-call | tf_op jit(solution)/shard_map/state0/pallas_call | solution.py:551
  8.8 1.8 %collective-permute-start.3 = (bf16[144,1024]{1,0:T(8,128)(2,1)S(1)}, bf16[144,1024]{1,0:T(8,128)(2,1)S(1)}, u32[]{:S(2)}, u32[]{:S(2)}) collective-permute-start(bf16[144,1024]{1,0:T(8,128)(2,1)S(1)} %state0.1), channel_id=1, source_target_pairs={{0,4},{4,8},{8,12},{12,16},{16,20},{20,24},{24,28},{28,0},{1,5},{5... | collective-permute-start | bytes 884744 | tf_op jit(solution)/shard_map/ppermute | solution.py:26
  10.6 0.9 %conv2.1.refs_2_.refs_0_ = bf16[512,512]{1,0:T(8,128)(2,1)S(1)} custom-call(bf16[512,2048]{1,0:T(8,128)(2,1)S(1)} %get-tuple-element.34.x_ref.refs_6_, bf16[4,2048]{1,0:T(4,128)(2,1)S(1)} %get-tuple-element.35.taps_ref, bf16[512,64]{1,0:T(8,128)(2,1)S(1)} %get-tuple-element.36.fac_ref, f32[512,128]{1,0:T(8,128)S(1)} %get-tuple-element.37.idc_ref.refs_2_), custom_call_target="tpu_custom_call" | custom-call | tf_op jit(solution)/shard_map/conv2/pallas_call | solution.py:494
  11.8 1.6 %collective-permute-start.4 = (bf16[128,512]{1,0:T(8,128)(2,1)S(1)}, bf16[128,512]{1,0:T(8,128)(2,1)S(1)}, u32[]{:S(2)}, u32[]{:S(2)}) collective-permute-start(bf16[128,512]{1,0:T(8,128)(2,1)S(1)} %state1024.1), channel_id=1, source_target_pairs={{0,4},{4,8},{8,12},{12,16},{16,20},{20,24},{24,28},{28,0},{1,5},{5... | collective-permute-start | bytes 393224 | tf_op jit(solution)/shard_map/ppermute | solution.py:26
  13.4 0.9 %conv3.1.refs_2_.refs_0_ = bf16[512,512]{1,0:T(8,128)(2,1)S(1)} custom-call(bf16[512,2048]{1,0:T(8,128)(2,1)S(1)} %get-tuple-element.34.x_ref.refs_6_, bf16[4,2048]{1,0:T(4,128)(2,1)S(1)} %get-tuple-element.35.taps_ref, bf16[512,64]{1,0:T(8,128)(2,1)S(1)} %get-tuple-element.36.fac_ref, f32[512,128]{1,0:T(8,128)S(1)} %get-tuple-element.37.idc_ref.refs_2_), custom_call_target="tpu_custom_call" | custom-call | tf_op jit(solution)/shard_map/conv3/pallas_call | solution.py:494
  14.3 0.3 %state1536.1 = bf16[128,512]{1,0:T(8,128)(2,1)S(1)} custom-call(bf16[144,512]{1,0:T(8,128)(2,1)S(1)} %constant_dynamic-update-slice_fusion.refs_0_, bf16[144,512]{1,0:T(8,128)(2,1)S(1)} %collective-permute-done.1.refs_1_, bf16[512,512]{1,0:T(8,128)(2,1)S(1)} %conv3.1.refs_2_.refs_0_, f32[8,2048]{1,0:T(8,128)S(1)} %get-tuple-element.40.refs_3_.refs_4_.refs_5_.refs_6_, ...), custom_call_target="tpu_custom_call" | custom-call | tf_op jit(solution)/shard_map/state1536/pallas_call | solution.py:551
  14.6 1.6 %collective-permute-start.2 = (bf16[128,512]{1,0:T(8,128)(2,1)S(1)}, bf16[128,512]{1,0:T(8,128)(2,1)S(1)}, u32[]{:S(2)}, u32[]{:S(2)}) collective-permute-start(bf16[128,512]{1,0:T(8,128)(2,1)S(1)} %state1536.1), channel_id=1, source_target_pairs={{0,4},{4,8},{8,12},{12,16},{16,20},{20,24},{24,28},{28,0},{1,5},{5... | collective-permute-start | bytes 393224 | tf_op jit(solution)/shard_map/ppermute | solution.py:26
  16.2 0.3 %score.1 = (bf16[2,256,256]{2,1,0:T(8,128)(2,1)S(1)}, bf16[512,128]{1,0:T(8,128)(2,1)S(1)}, bf16[256,128]{1,0:T(8,128)(2,1)S(1)}, bf16[128,256]{1,0:T(8,128)(2,1)S(1)}) custom-call(bf16[144,512]{1,0:T(8,128)(2,1)S(1)} %constant_dynamic-update-slice_fusion.refs_0_, bf16[144,512]{1,0:T(8,128)(2,1)S(1)} %collective-permute-done.1.refs_1_, ...), custom_call_target="tpu_custom_call" | custom-call | tf_op jit(solution)/shard_map/score/pallas_call | solution.py:520
  16.5 1.1 %local0.1 = (f32[512,1024]{1,0:T(8,128)S(1)}, f32[512,1024]{1,0:T(8,128)S(1)}) custom-call(bf16[512,512]{1,0:T(8,128)(2,1)S(1)} %get-tuple-element.42.refs_2_.refs_0_, bf16[512,512]{1,0:T(8,128)(2,1)S(1)} %conv1.1.refs_3_.refs_1_, bf16[2,256,256]{2,1,0:T(8,128)(2,1)S(1)} %get-tuple-element.46.refs_1_.refs_2_, ...), custom_call_target="tpu_custom_call" | custom-call | tf_op jit(solution)/shard_map/local0/pallas_call | solution.py:564
  17.7 0.7 %local1024.1 = (f32[512,512]{1,0:T(8,128)S(1)}, f32[512,512]{1,0:T(8,128)S(1)}) custom-call(bf16[512,512]{1,0:T(8,128)(2,1)S(1)} %conv2.1.refs_2_.refs_0_, bf16[2,256,256]{2,1,0:T(8,128)(2,1)S(1)} %get-tuple-element.46.refs_1_.refs_2_, bf16[256,128]{1,0:T(8,128)(2,1)S(1)} %get-tuple-element.47.refs_2_.refs_3_, ...), custom_call_target="tpu_custom_call" | custom-call | tf_op jit(solution)/shard_map/local1024/pallas_call | solution.py:564
  18.4 0.7 %local1536.1 = (f32[512,512]{1,0:T(8,128)S(1)}, f32[512,512]{1,0:T(8,128)S(1)}) custom-call(bf16[512,512]{1,0:T(8,128)(2,1)S(1)} %conv3.1.refs_2_.refs_0_, bf16[2,256,256]{2,1,0:T(8,128)(2,1)S(1)} %get-tuple-element.46.refs_1_.refs_2_, bf16[256,128]{1,0:T(8,128)(2,1)S(1)} %get-tuple-element.47.refs_2_.refs_3_, ...), custom_call_target="tpu_custom_call" | custom-call | tf_op jit(solution)/shard_map/local1536/pallas_call | solution.py:564
  19.1 2.3 %collective-permute-done.3.rim_ref.state_ref = bf16[144,1024]{1,0:T(8,128)(2,1)S(1)} collective-permute-done((bf16[144,1024]{1,0:T(8,128)(2,1)S(1)}, bf16[144,1024]{1,0:T(8,128)(2,1)S(1)}, u32[]{:S(2)}, u32[]{:S(2)}) %collective-permute-start.3) | collective-permute-done | bytes 294944 | tf_op jit(solution)/shard_map/ppermute | solution.py:26
  21.4 0.3 %fix.1 = (bf16[512,256]{1,0:T(8,128)(2,1)S(1)}, bf16[16,2048]{1,0:T(8,128)(2,1)S(1)}) custom-call(bf16[512,2048]{1,0:T(8,128)(2,1)S(1)} %get-tuple-element.34.x_ref.refs_6_, bf16[144,1024]{1,0:T(8,128)(2,1)S(1)} %collective-permute-done.3.rim_ref.state_ref, bf16[4,2048]{1,0:T(4,128)(2,1)S(1)} %get-tuple-element.35.taps_ref, ...), custom_call_target="tpu_custom_call" | custom-call | tf_op jit(solution)/shard_map/fix/pallas_call | solution.py:529
  21.8 1.6 %final0.1.refs_0_ = bf16[512,2048]{1,0:T(8,128)(2,1)} custom-call(bf16[144,1024]{1,0:T(8,128)(2,1)S(1)} %collective-permute-done.3.rim_ref.state_ref, bf16[16,2048]{1,0:T(8,128)(2,1)S(1)} %get-tuple-element.45.edge_ref, f32[512,1024]{1,0:T(8,128)S(1)} %get-tuple-element.55.y_ref, f32[512,1024]{1,0:T(8,128)S(1)} %get-tuple-element.56.dec_ref, ...), custom_call_target="tpu_custom_call" | custom-call | tf_op jit(solution)/shard_map/final0/pallas_call | solution.py:577
  23.3 0.9 %collective-permute-done.4.state_ref = bf16[128,512]{1,0:T(8,128)(2,1)S(1)} collective-permute-done((bf16[128,512]{1,0:T(8,128)(2,1)S(1)}, bf16[128,512]{1,0:T(8,128)(2,1)S(1)}, u32[]{:S(2)}, u32[]{:S(2)}) %collective-permute-start.4) | collective-permute-done | bytes 131104 | tf_op jit(solution)/shard_map/ppermute | solution.py:26
  24.2 1.2 %final1024.1.refs_0_ = bf16[512,2048]{1,0:T(8,128)(2,1)} custom-call(bf16[128,512]{1,0:T(8,128)(2,1)S(1)} %collective-permute-done.4.state_ref, bf16[16,2048]{1,0:T(8,128)(2,1)S(1)} %get-tuple-element.45.edge_ref, f32[512,512]{1,0:T(8,128)S(1)} %get-tuple-element.53.y_ref, f32[512,512]{1,0:T(8,128)S(1)} %get-tuple-element.54.dec_ref, ...), custom_call_target="tpu_custom_call", output_to_operand_aliasing={{}: (6, {})} | custom-call | tf_op jit(solution)/shard_map/final1024/pallas_call | solution.py:577
  25.4 1.1 %collective-permute-done.2.state_ref = bf16[128,512]{1,0:T(8,128)(2,1)S(1)} collective-permute-done((bf16[128,512]{1,0:T(8,128)(2,1)S(1)}, bf16[128,512]{1,0:T(8,128)(2,1)S(1)}, u32[]{:S(2)}, u32[]{:S(2)}) %collective-permute-start.2) | collective-permute-done | bytes 131104 | tf_op jit(solution)/shard_map/ppermute | solution.py:26
  26.5 1.3 %final1536.1 = bf16[512,2048]{1,0:T(8,128)(2,1)} custom-call(bf16[128,512]{1,0:T(8,128)(2,1)S(1)} %collective-permute-done.2.state_ref, bf16[16,2048]{1,0:T(8,128)(2,1)S(1)} %get-tuple-element.45.edge_ref, f32[512,512]{1,0:T(8,128)S(1)} %get-tuple-element.50.y_ref, f32[512,512]{1,0:T(8,128)S(1)} %get-tuple-element.51.dec_ref, ...), custom_call_target="tpu_custom_call", output_to_operand_aliasing={{}: (6, {})} | custom-call | tf_op jit(solution)/shard_map/final1536/pallas_call | solution.py:577
  (10 shorter events, 0.4 us)
Async XLA Ops:
  1.4 5.6 %collective-permute-start = (bf16[72,512]{1,0:T(8,128)(2,1)S(1)}, bf16[72,512]{1,0:T(8,128)(2,1)S(1)}, u32[]{:S(2)}, u32[]{:S(2)}) collective-permute-start(bf16[72,512]{1,0:T(8,128)(2,1)S(1)} %get-tuple-element.38.refs_0_), channel_id=1, source_target_pairs={{0,2},{1,3},{2,0},{3,1},{4,6},{5,7},{6,4},{7,5},{8,10},{9,11},{10,... | collective-permute-start | bytes 221192 | tf_op jit(solution)/shard_map/ppermute | solution.py:31
  7.0 1.4 %collective-permute-start.1 = (bf16[144,512]{1,0:T(8,128)(2,1)S(1)}, bf16[144,512]{1,0:T(8,128)(2,1)S(1)}, u32[]{:S(2)}, u32[]{:S(2)}) collective-permute-start(bf16[144,512]{1,0:T(8,128)(2,1)S(1)} %constant_dynamic-update-slice_fusion.refs_0_), channel_id=1, source_target_pairs={{0,1},{1,0},{2,3},{3,2},{4,5},{5,4},{6,7},{7,6},{8,9},{9,8},{10,11... | collective-permute-start | bytes 442376 | tf_op jit(solution)/shard_map/ppermute | solution.py:31
  8.8 12.6 %collective-permute-start.3 = (bf16[144,1024]{1,0:T(8,128)(2,1)S(1)}, bf16[144,1024]{1,0:T(8,128)(2,1)S(1)}, u32[]{:S(2)}, u32[]{:S(2)}) collective-permute-start(bf16[144,1024]{1,0:T(8,128)(2,1)S(1)} %state0.1), channel_id=1, source_target_pairs={{0,4},{4,8},{8,12},{12,16},{16,20},{20,24},{24,28},{28,0},{1,5},{5... | collective-permute-start | bytes 884744 | tf_op jit(solution)/shard_map/ppermute | solution.py:26
  11.8 4.4 %copy-start.1 = (bf16[2048]{0:T(1024)(128)(2,1)S(1)}, bf16[2048]{0:T(1024)(128)(2,1)}, u32[]{:S(2)}) copy-start(bf16[2048]{0:T(1024)(128)(2,1)} %param.16) | copy-start | bytes 12292
  11.8 4.7 %copy-start = (bf16[512,2048]{1,0:T(8,128)(2,1)S(1)}, bf16[512,2048]{1,0:T(8,128)(2,1)}, u32[]{:S(2)}) copy-start(bf16[512,2048]{1,0:T(8,128)(2,1)} %refs_7_.1) | copy-start | bytes 6291460
  11.8 12.4 %collective-permute-start.4 = (bf16[128,512]{1,0:T(8,128)(2,1)S(1)}, bf16[128,512]{1,0:T(8,128)(2,1)S(1)}, u32[]{:S(2)}, u32[]{:S(2)}) collective-permute-start(bf16[128,512]{1,0:T(8,128)(2,1)S(1)} %state1024.1), channel_id=1, source_target_pairs={{0,4},{4,8},{8,12},{12,16},{16,20},{20,24},{24,28},{28,0},{1,5},{5... | collective-permute-start | bytes 393224 | tf_op jit(solution)/shard_map/ppermute | solution.py:26
  14.6 11.9 %collective-permute-start.2 = (bf16[128,512]{1,0:T(8,128)(2,1)S(1)}, bf16[128,512]{1,0:T(8,128)(2,1)S(1)}, u32[]{:S(2)}, u32[]{:S(2)}) collective-permute-start(bf16[128,512]{1,0:T(8,128)(2,1)S(1)} %state1536.1), channel_id=1, source_target_pairs={{0,4},{4,8},{8,12},{12,16},{16,20},{20,24},{24,28},{28,0},{1,5},{5... | collective-permute-start | bytes 393224 | tf_op jit(solution)/shard_map/ppermute | solution.py:26

commit v7 on v6

--- a/solution.py
+++ b/solution.py
@@ -13,7 +13,6 @@
 CONV = 4
 CHUNK = 256
 WIDE = 256
-PIECES = 4
 GROUPS = ((0, 1), (2,), (3,))
 EDGE = 16
 F32 = jnp.float32
@@ -92,13 +91,18 @@
 
 
 def rim_rows(columns, split, width):
-    slots = columns // width + -(-128 * split // width)
-    return -(-3 * slots // 16) * 16
+    return -(-3 * (columns + 128 * split) // width // 8) * 8
+
+
+def rim_place(columns, split, width, row, index):
+    lane = row * 128 * split + index * 128
+    return 3 * columns // width + lane // width, lane % width
 
 
 def rim_block(x_ref, start_ref, shares, width):
     rows, columns = x_ref.shape
-    total = rim_rows(columns, len(shares), width)
+    split = len(shares)
+    total = rim_rows(columns, split, width)
     starts = start_ref[:, rows - 128 :].astype(F32)
     last = starts[:, 127:128]
     before = jnp.maximum(last, starts[:, 126:127])
@@ -106,25 +110,28 @@
     kept = jnp.where(row == 5, 1.0 - before, jnp.where(row == 6, 1.0 - last, 1.0))
     kept = jnp.where(row >= 5, kept, 0.0)
     kept = jnp.concatenate([kept] * (width // 128), axis=1)
-    row = iota((8, width), 0)
+
+    def placed(piece, shift, left=0):
+        right = width - left - piece.shape[1]
+        sides = [jnp.zeros((8, left), F32)] if left else []
+        sides += [piece] + ([jnp.zeros((8, right), F32)] if right else [])
+        piece = jnp.concatenate(sides, axis=1)
+        if total > 8:
+            piece = jnp.concatenate([piece, jnp.zeros((total - 8, width), F32)], axis=0)
+        return pltpu.roll(piece, shift % total, 0) if shift % total else piece
+
     block = jnp.zeros((total, width), F32)
-    below = jnp.zeros((total - 8, width), F32)
-    slot = 0
-    for low in range(0, columns, width):
+    for slot, low in enumerate(range(0, columns, width)):
         piece = x_ref[rows - 8 :, low : low + width].astype(F32) * kept
-        piece = jnp.concatenate([piece, below], axis=0)
-        block = block + pltpu.roll(piece, (slot - 5) % total, 0)
-        slot += 3
-    count = width // 128
-    for index in range(0, len(shares), count):
-        piece = [share[share.shape[0] - 8 :, :128] for share in shares[index : index + count]]
-        gap = width - 128 * len(piece)
-        piece += [jnp.zeros((8, gap), BF16)] if gap else []
+        block = block + placed(piece, 3 * slot - 5)
+    count = min(width // 128, split)
+    for first in range(0, split, count):
+        piece = [share[share.shape[0] - 8 :, :128] for share in shares[first : first + count]]
         piece = jnp.concatenate(piece, axis=1).astype(F32)
-        piece = jnp.where((row >= 3) & (row < 6), piece, 0.0)
-        piece = jnp.concatenate([piece, below], axis=0)
-        block = block + pltpu.roll(piece, (slot - 3) % total, 0)
-        slot += 3
+        for each in range(3):
+            own = jnp.where(iota(piece.shape, 0) == 3 + each, piece, 0.0)
+            down, left = rim_place(columns, split, width, each, first)
+            block = block + placed(own, down - 3 - each, left)
     return block.astype(BF16)
 
 
@@ -205,7 +212,8 @@
             kept = kept * pltpu.roll(open_, back - 1, 1)
         piece = pltpu.roll(values, back, 1)[:, 128:] * kept[:1, 128:]
         total = total + piece * taps[:, CONV - 1 - back : CONV - back]
-    out_ref[:width, :] = (total / (1.0 + jnp.exp(-total))).astype(BF16)
+    half = 0.5 * total
+    out_ref[:width, :] = (half + half * jnp.tanh(half)).astype(BF16)
     lane = iota((1, 128), 1)
     last = open_[:1, rows:]
     near, far = last[:, 127:128], last[:, 126:127]
@@ -233,17 +241,20 @@
     depth = rim_rows(columns, split, rim_ref.shape[1])
     base = rim_ref.shape[0] - depth
 
-    def rim(low, size, row):
-        slot, lane = low // rim_ref.shape[1], low % rim_ref.shape[1]
+    def moved(lane, size, shift):
         block = rim_ref[base:, lane : lane + size].astype(F32)
-        return pltpu.roll(block, (row - 3 * slot) % depth, 0)[:8]
+        return (pltpu.roll(block, shift % depth, 0) if shift % depth else block)[:8]
 
     live = idc_ref[:8, :] == 0.0
     row, lane = iota((8, 128), 0), iota((width, 128), 1)
     firsts = []
     for index, share in enumerate(shares):
         own = share[width:, :128].astype(F32)
-        total = own + jnp.where(live, rim(columns + index * 128, 128, 0), 0.0)
+        after = jnp.zeros((8, 128), F32)
+        for each in range(3):
+            down, left = rim_place(columns, split, rim_ref.shape[1], each, index)
+            after = jnp.where(row == each, moved(left, 128, each - down), after)
+        total = own + jnp.where(live, after, 0.0)
         total = total + pltpu.roll(total, 64, 1)
         value = total / (1.0 + jnp.exp(-total))
         firsts.append(value[:, :width])
@@ -272,7 +283,9 @@
     for low in range(0, columns, WIDE):
         cols = slice(low, low + WIDE)
         taps = 0.5 * taps_ref[:, cols].astype(F32)
-        padded = jnp.concatenate([rim(low, WIDE, 5), x_ref[:EDGE, cols].astype(F32)], axis=0)
+        slot, left = low // rim_ref.shape[1], low % rim_ref.shape[1]
+        above = moved(left, WIDE, 5 - 3 * slot)
+        padded = jnp.concatenate([above, x_ref[:EDGE, cols].astype(F32)], axis=0)
         half = padded[8:] * taps[CONV - 1 : CONV, :]
         for back in range(1, CONV):
             piece = pltpu.roll(padded, back, 0)[8:] * masks[back - 1]
@@ -487,12 +500,15 @@
         [pltpu.SemaphoreType.DMA],
         "prep",
     )(steps, scale, starts, in_hbm(x_in))
-    width = columns // PIECES
+    units = columns // WIDE
+    sizes = [units // 4] * 4
+    sizes = [WIDE * size for size in sizes]
+    places = [sum(sizes[:piece]) for piece in range(len(sizes))]
     values = []
-    for piece in range(PIECES):
+    for piece, (place, width) in enumerate(zip(places, sizes)):
         kept = [own] if piece == 0 else []
         part, *kept = call(
-            functools.partial(conv_kernel, piece * width),
+            functools.partial(conv_kernel, place),
             [spec] * (4 + len(kept)),
             [shape((rows, width), BF16)] + [shape(own.shape, BF16)] * len(kept),
             [pltpu.VMEM((rows + 8, 128), F32), pltpu.VMEM((CONV - 1, rows, 128), F32)],
@@ -505,8 +521,8 @@
         ours = jnp.concatenate([ours, crossed(ours, "head", mask)], axis=0)
         mask //= 2
     shares = [ours, crossed(ours, "head", 1)]
-    widths = [width * len(group) for group in GROUPS]
-    lows = [width * group[0] for group in GROUPS]
+    widths = [sum(sizes[piece] for piece in group) for group in GROUPS]
+    lows = [places[group[0]] for group in GROUPS]
     state_type = BF16 if turns == 1 else F32
     gain = norm_gain.reshape(1, columns)
     extra = rim_rows(columns, split, widths[0])

time: 28 us -> 27.6 us (0.986)
  waiting for transfers between devices: 4.62 us -> 4.27 us
    ppermute x3, waiting for transfers between devices: 4.22 us -> 3.86 us  [shifted(): return lax.ppermute(value, axis, pairs)]
  transfers between devices with their start and end apart: 5 -> 5, of which waited for: 4 -> 4; matrix products, arithmetic and copies ran while one was open for 0% -> 0% of each run, Pallas kernels for 43% -> 44%
where the time goes in v7:
time: 27.6 us; the launch traced here: 27.4 us
  Pallas kernels  15 us (54%)
  starting transfers between devices  8 us (29%)
  waiting for transfers between devices  4.27 us (15%)
    ppermute x3, starting transfers between devices, shifted(): return lax.ppermute(value, axis, pairs)  4.92 us
    pallas_call x3, Pallas kernels, on_device(): call(functools.partial(final_kernel, low), in_specs, shape((rows, columns...  4.06 us
    ppermute x3, waiting for transfers between devices, shifted(): return lax.ppermute(value, axis, pairs)  3.86 us
    pallas_call x4, Pallas kernels, on_device(): call(functools.partial(conv_kernel, place), [spec] * (4 + len(kept)), [sh...  3.79 us
    ppermute x2, starting transfers between devices, crossed(): lax.ppermute(value, axis, [(source, source ^ mask) for source in range(co...  3.07 us
    pallas_call x3, Pallas kernels, on_device(): call(functools.partial(local_kernel, low), [spec] * (6 + len(pieces)), [s...  2.6 us
    pallas_call x1, Pallas kernels, on_device(): call(prep_kernel, [spec] * 3 + [hbm], [shape((rows, 2 * heads), BF16), sh...  1.6 us
    pallas_call x1, Pallas kernels, on_device(): call(bc_kernel, [hbm] * 6, [shape((bc_width + 8, rows), BF16), shape((1,...  1.37 us
  transfers between devices with their start and end apart: 5, of which 4 were waited for; matrix products, arithmetic and copies ran while one was open for 0% of the time, Pallas kernels for 44%

profile of v7, /device:TPU:0, one launch (start us, length us, event | category | flops | bytes accessed | tf_op | source)
XLA Modules:
  0.0 27.4 jit_solution(15162740462926581073)
XLA Ops:
  0.0 1.4 %bc.1 = (bf16[72,512]{1,0:T(8,128)(2,1)S(1)}, s32[1,512]{1,0:T(1,128)S(1)}, f32[32,512]{1,0:T(8,128)S(1)}, f32[1,32]{1,0:T(1,128)S(1)}, bf16[4,2048]{1,0:T(4,128)(2,1)S(1)}) custom-call(bf16[64,512]{1,0:T(8,128)(2,1)} %bitcast.4, bf16[4,64]{1,0:T(4,128)(2,1)} %refs_1_.1, s32[1,512]{1,0:T(1,128)} %bitcast.6, f32[32,512]{1,0:T(8,128)} %bitcast.5, ...), custom_call_target="tpu_custom_call" | custom-call | tf_op jit(solution)/shard_map/bc/pallas_call | solution.py:463
  1.4 3.0 %collective-permute-start = (bf16[72,512]{1,0:T(8,128)(2,1)S(1)}, bf16[72,512]{1,0:T(8,128)(2,1)S(1)}, u32[]{:S(2)}, u32[]{:S(2)}) collective-permute-start(bf16[72,512]{1,0:T(8,128)(2,1)S(1)} %get-tuple-element.38.refs_0_), channel_id=1, source_target_pairs={{0,2},{1,3},{2,0},{3,1},{4,6},{5,7},{6,4},{7,5},{8,10},{9,11},{10,... | collective-permute-start | bytes 221192 | tf_op jit(solution)/shard_map/ppermute | solution.py:30
  4.4 1.6 %prep.1 = (bf16[512,64]{1,0:T(8,128)(2,1)S(1)}, bf16[512,64]{1,0:T(8,128)(2,1)S(1)}, bf16[16,64]{1,0:T(8,128)(2,1)S(1)}, f32[8,2048]{1,0:T(8,128)S(1)}, f32[512,...) custom-call(f32[32,512]{1,0:T(8,128)S(1)} %get-tuple-element.31.dt_ref, ...), custom_call_target="tpu_custom_call" | custom-call | tf_op jit(solution)/shard_map/prep/pallas_call | solution.py:488
  6.0 0.9 %conv0.1 = (bf16[512,512]{1,0:T(8,128)(2,1)S(1)}, bf16[72,512]{1,0:T(8,128)(2,1)S(1)}) custom-call(bf16[512,2048]{1,0:T(8,128)(2,1)S(1)} %get-tuple-element.34.x_ref.refs_6_, bf16[4,2048]{1,0:T(4,128)(2,1)S(1)} %get-tuple-element.35.taps_ref, bf16[512,64]{1,0:T(8,128)(2,1)S(1)} %get-tuple-element.36.fac_ref, ...), custom_call_target="tpu_custom_call" | custom-call | tf_op jit(solution)/shard_map/conv0/pallas_call | solution.py:510
  7.1 0.9 %conv1.1.refs_3_.refs_1_ = bf16[512,512]{1,0:T(8,128)(2,1)S(1)} custom-call(bf16[512,2048]{1,0:T(8,128)(2,1)S(1)} %get-tuple-element.34.x_ref.refs_6_, bf16[4,2048]{1,0:T(4,128)(2,1)S(1)} %get-tuple-element.35.taps_ref, bf16[512,64]{1,0:T(8,128)(2,1)S(1)} %get-tuple-element.36.fac_ref, f32[512,128]{1,0:T(8,128)S(1)} %get-tuple-element.37.idc_ref.refs_2_), custom_call_target="tpu_custom_call" | custom-call | tf_op jit(solution)/shard_map/conv1/pallas_call | solution.py:510
  8.0 0.4 %collective-permute-done.1.refs_1_ = bf16[144,512]{1,0:T(8,128)(2,1)S(1)} collective-permute-done((bf16[144,512]{1,0:T(8,128)(2,1)S(1)}, bf16[144,512]{1,0:T(8,128)(2,1)S(1)}, u32[]{:S(2)}, u32[]{:S(2)}) %collective-permute-start.1) | collective-permute-done | bytes 147488 | tf_op jit(solution)/shard_map/ppermute | solution.py:30
  8.4 0.4 %state0.1 = bf16[136,1024]{1,0:T(8,128)(2,1)S(1)} custom-call(bf16[144,512]{1,0:T(8,128)(2,1)S(1)} %constant_dynamic-update-slice_fusion.refs_0_, bf16[144,512]{1,0:T(8,128)(2,1)S(1)} %collective-permute-done.1.refs_1_, bf16[512,512]{1,0:T(8,128)(2,1)S(1)} %get-tuple-element.42.refs_2_.refs_0_, bf16[512,512]{1,0:T(8,128)(2,1)S(1)} %conv1.1.refs_3_.refs_1_, ...), custom_call_target="tpu_custom_call" | custom-call | tf_op jit(solution)/shard_map/state0/pallas_call | solution.py:567
  8.8 1.8 %collective-permute-start.3 = (bf16[136,1024]{1,0:T(8,128)(2,1)S(1)}, bf16[136,1024]{1,0:T(8,128)(2,1)S(1)}, u32[]{:S(2)}, u32[]{:S(2)}) collective-permute-start(bf16[136,1024]{1,0:T(8,128)(2,1)S(1)} %state0.1), channel_id=1, source_target_pairs={{0,4},{4,8},{8,12},{12,16},{16,20},{20,24},{24,28},{28,0},{1,5},{5... | collective-permute-start | bytes 835592 | tf_op jit(solution)/shard_map/ppermute | solution.py:25
  10.6 0.9 %conv2.1.refs_2_.refs_0_ = bf16[512,512]{1,0:T(8,128)(2,1)S(1)} custom-call(bf16[512,2048]{1,0:T(8,128)(2,1)S(1)} %get-tuple-element.34.x_ref.refs_6_, bf16[4,2048]{1,0:T(4,128)(2,1)S(1)} %get-tuple-element.35.taps_ref, bf16[512,64]{1,0:T(8,128)(2,1)S(1)} %get-tuple-element.36.fac_ref, f32[512,128]{1,0:T(8,128)S(1)} %get-tuple-element.37.idc_ref.refs_2_), custom_call_target="tpu_custom_call" | custom-call | tf_op jit(solution)/shard_map/conv2/pallas_call | solution.py:510
  11.8 1.6 %collective-permute-start.4 = (bf16[128,512]{1,0:T(8,128)(2,1)S(1)}, bf16[128,512]{1,0:T(8,128)(2,1)S(1)}, u32[]{:S(2)}, u32[]{:S(2)}) collective-permute-start(bf16[128,512]{1,0:T(8,128)(2,1)S(1)} %state1024.1), channel_id=1, source_target_pairs={{0,4},{4,8},{8,12},{12,16},{16,20},{20,24},{24,28},{28,0},{1,5},{5... | collective-permute-start | bytes 393224 | tf_op jit(solution)/shard_map/ppermute | solution.py:25
  13.4 0.9 %conv3.1.refs_2_.refs_0_ = bf16[512,512]{1,0:T(8,128)(2,1)S(1)} custom-call(bf16[512,2048]{1,0:T(8,128)(2,1)S(1)} %get-tuple-element.34.x_ref.refs_6_, bf16[4,2048]{1,0:T(4,128)(2,1)S(1)} %get-tuple-element.35.taps_ref, bf16[512,64]{1,0:T(8,128)(2,1)S(1)} %get-tuple-element.36.fac_ref, f32[512,128]{1,0:T(8,128)S(1)} %get-tuple-element.37.idc_ref.refs_2_), custom_call_target="tpu_custom_call" | custom-call | tf_op jit(solution)/shard_map/conv3/pallas_call | solution.py:510
  14.3 0.3 %state1536.1 = bf16[128,512]{1,0:T(8,128)(2,1)S(1)} custom-call(bf16[144,512]{1,0:T(8,128)(2,1)S(1)} %constant_dynamic-update-slice_fusion.refs_0_, bf16[144,512]{1,0:T(8,128)(2,1)S(1)} %collective-permute-done.1.refs_1_, bf16[512,512]{1,0:T(8,128)(2,1)S(1)} %conv3.1.refs_2_.refs_0_, f32[8,2048]{1,0:T(8,128)S(1)} %get-tuple-element.40.refs_3_.refs_4_.refs_5_.refs_6_, ...), custom_call_target="tpu_custom_call" | custom-call | tf_op jit(solution)/shard_map/state1536/pallas_call | solution.py:567
  14.6 1.6 %collective-permute-start.2 = (bf16[128,512]{1,0:T(8,128)(2,1)S(1)}, bf16[128,512]{1,0:T(8,128)(2,1)S(1)}, u32[]{:S(2)}, u32[]{:S(2)}) collective-permute-start(bf16[128,512]{1,0:T(8,128)(2,1)S(1)} %state1536.1), channel_id=1, source_target_pairs={{0,4},{4,8},{8,12},{12,16},{16,20},{20,24},{24,28},{28,0},{1,5},{5... | collective-permute-start | bytes 393224 | tf_op jit(solution)/shard_map/ppermute | solution.py:25
  16.2 0.3 %score.1 = (bf16[2,256,256]{2,1,0:T(8,128)(2,1)S(1)}, bf16[512,128]{1,0:T(8,128)(2,1)S(1)}, bf16[256,128]{1,0:T(8,128)(2,1)S(1)}, bf16[128,256]{1,0:T(8,128)(2,1)S(1)}) custom-call(bf16[144,512]{1,0:T(8,128)(2,1)S(1)} %constant_dynamic-update-slice_fusion.refs_0_, bf16[144,512]{1,0:T(8,128)(2,1)S(1)} %collective-permute-done.1.refs_1_, ...), custom_call_target="tpu_custom_call" | custom-call | tf_op jit(solution)/shard_map/score/pallas_call | solution.py:536
  16.5 1.1 %local0.1 = (f32[512,1024]{1,0:T(8,128)S(1)}, f32[512,1024]{1,0:T(8,128)S(1)}) custom-call(bf16[512,512]{1,0:T(8,128)(2,1)S(1)} %get-tuple-element.42.refs_2_.refs_0_, bf16[512,512]{1,0:T(8,128)(2,1)S(1)} %conv1.1.refs_3_.refs_1_, bf16[2,256,256]{2,1,0:T(8,128)(2,1)S(1)} %get-tuple-element.46.refs_1_.refs_2_, ...), custom_call_target="tpu_custom_call" | custom-call | tf_op jit(solution)/shard_map/local0/pallas_call | solution.py:580
  17.7 0.7 %local1024.1 = (f32[512,512]{1,0:T(8,128)S(1)}, f32[512,512]{1,0:T(8,128)S(1)}) custom-call(bf16[512,512]{1,0:T(8,128)(2,1)S(1)} %conv2.1.refs_2_.refs_0_, bf16[2,256,256]{2,1,0:T(8,128)(2,1)S(1)} %get-tuple-element.46.refs_1_.refs_2_, bf16[256,128]{1,0:T(8,128)(2,1)S(1)} %get-tuple-element.47.refs_2_.refs_3_, ...), custom_call_target="tpu_custom_call" | custom-call | tf_op jit(solution)/shard_map/local1024/pallas_call | solution.py:580
  18.4 0.7 %local1536.1 = (f32[512,512]{1,0:T(8,128)S(1)}, f32[512,512]{1,0:T(8,128)S(1)}) custom-call(bf16[512,512]{1,0:T(8,128)(2,1)S(1)} %conv3.1.refs_2_.refs_0_, bf16[2,256,256]{2,1,0:T(8,128)(2,1)S(1)} %get-tuple-element.46.refs_1_.refs_2_, bf16[256,128]{1,0:T(8,128)(2,1)S(1)} %get-tuple-element.47.refs_2_.refs_3_, ...), custom_call_target="tpu_custom_call" | custom-call | tf_op jit(solution)/shard_map/local1536/pallas_call | solution.py:580
  19.1 1.9 %collective-permute-done.3.rim_ref.state_ref = bf16[136,1024]{1,0:T(8,128)(2,1)S(1)} collective-permute-done((bf16[136,1024]{1,0:T(8,128)(2,1)S(1)}, bf16[136,1024]{1,0:T(8,128)(2,1)S(1)}, u32[]{:S(2)}, u32[]{:S(2)}) %collective-permute-start.3) | collective-permute-done | bytes 278560 | tf_op jit(solution)/shard_map/ppermute | solution.py:25
  21.0 0.3 %fix.1 = (bf16[512,256]{1,0:T(8,128)(2,1)S(1)}, bf16[16,2048]{1,0:T(8,128)(2,1)S(1)}) custom-call(bf16[512,2048]{1,0:T(8,128)(2,1)S(1)} %get-tuple-element.34.x_ref.refs_6_, bf16[136,1024]{1,0:T(8,128)(2,1)S(1)} %collective-permute-done.3.rim_ref.state_ref, bf16[4,2048]{1,0:T(4,128)(2,1)S(1)} %get-tuple-element.35.taps_ref, ...), custom_call_target="tpu_custom_call" | custom-call | tf_op jit(solution)/shard_map/fix/pallas_call | solution.py:545
  21.4 1.6 %final0.1.refs_0_ = bf16[512,2048]{1,0:T(8,128)(2,1)} custom-call(bf16[136,1024]{1,0:T(8,128)(2,1)S(1)} %collective-permute-done.3.rim_ref.state_ref, bf16[16,2048]{1,0:T(8,128)(2,1)S(1)} %get-tuple-element.45.edge_ref, f32[512,1024]{1,0:T(8,128)S(1)} %get-tuple-element.55.y_ref, f32[512,1024]{1,0:T(8,128)S(1)} %get-tuple-element.56.dec_ref, ...), custom_call_target="tpu_custom_call" | custom-call | tf_op jit(solution)/shard_map/final0/pallas_call | solution.py:593
  23.0 0.9 %collective-permute-done.4.state_ref = bf16[128,512]{1,0:T(8,128)(2,1)S(1)} collective-permute-done((bf16[128,512]{1,0:T(8,128)(2,1)S(1)}, bf16[128,512]{1,0:T(8,128)(2,1)S(1)}, u32[]{:S(2)}, u32[]{:S(2)}) %collective-permute-start.4) | collective-permute-done | bytes 131104 | tf_op jit(solution)/shard_map/ppermute | solution.py:25
  23.8 1.2 %final1024.1.refs_0_ = bf16[512,2048]{1,0:T(8,128)(2,1)} custom-call(bf16[128,512]{1,0:T(8,128)(2,1)S(1)} %collective-permute-done.4.state_ref, bf16[16,2048]{1,0:T(8,128)(2,1)S(1)} %get-tuple-element.45.edge_ref, f32[512,512]{1,0:T(8,128)S(1)} %get-tuple-element.53.y_ref, f32[512,512]{1,0:T(8,128)S(1)} %get-tuple-element.54.dec_ref, ...), custom_call_target="tpu_custom_call", output_to_operand_aliasing={{}: (6, {})} | custom-call | tf_op jit(solution)/shard_map/final1024/pallas_call | solution.py:593
  25.1 1.1 %collective-permute-done.2.state_ref = bf16[128,512]{1,0:T(8,128)(2,1)S(1)} collective-permute-done((bf16[128,512]{1,0:T(8,128)(2,1)S(1)}, bf16[128,512]{1,0:T(8,128)(2,1)S(1)}, u32[]{:S(2)}, u32[]{:S(2)}) %collective-permute-start.2) | collective-permute-done | bytes 131104 | tf_op jit(solution)/shard_map/ppermute | solution.py:25
  26.2 1.3 %final1536.1 = bf16[512,2048]{1,0:T(8,128)(2,1)} custom-call(bf16[128,512]{1,0:T(8,128)(2,1)S(1)} %collective-permute-done.2.state_ref, bf16[16,2048]{1,0:T(8,128)(2,1)S(1)} %get-tuple-element.45.edge_ref, f32[512,512]{1,0:T(8,128)S(1)} %get-tuple-element.50.y_ref, f32[512,512]{1,0:T(8,128)S(1)} %get-tuple-element.51.dec_ref, ...), custom_call_target="tpu_custom_call", output_to_operand_aliasing={{}: (6, {})} | custom-call | tf_op jit(solution)/shard_map/final1536/pallas_call | solution.py:593
  (10 shorter events, 0.4 us)
Async XLA Ops:
  1.4 5.6 %collective-permute-start = (bf16[72,512]{1,0:T(8,128)(2,1)S(1)}, bf16[72,512]{1,0:T(8,128)(2,1)S(1)}, u32[]{:S(2)}, u32[]{:S(2)}) collective-permute-start(bf16[72,512]{1,0:T(8,128)(2,1)S(1)} %get-tuple-element.38.refs_0_), channel_id=1, source_target_pairs={{0,2},{1,3},{2,0},{3,1},{4,6},{5,7},{6,4},{7,5},{8,10},{9,11},{10,... | collective-permute-start | bytes 221192 | tf_op jit(solution)/shard_map/ppermute | solution.py:30
  7.0 1.4 %collective-permute-start.1 = (bf16[144,512]{1,0:T(8,128)(2,1)S(1)}, bf16[144,512]{1,0:T(8,128)(2,1)S(1)}, u32[]{:S(2)}, u32[]{:S(2)}) collective-permute-start(bf16[144,512]{1,0:T(8,128)(2,1)S(1)} %constant_dynamic-update-slice_fusion.refs_0_), channel_id=1, source_target_pairs={{0,1},{1,0},{2,3},{3,2},{4,5},{5,4},{6,7},{7,6},{8,9},{9,8},{10,11... | collective-permute-start | bytes 442376 | tf_op jit(solution)/shard_map/ppermute | solution.py:30
  8.8 12.3 %collective-permute-start.3 = (bf16[136,1024]{1,0:T(8,128)(2,1)S(1)}, bf16[136,1024]{1,0:T(8,128)(2,1)S(1)}, u32[]{:S(2)}, u32[]{:S(2)}) collective-permute-start(bf16[136,1024]{1,0:T(8,128)(2,1)S(1)} %state0.1), channel_id=1, source_target_pairs={{0,4},{4,8},{8,12},{12,16},{16,20},{20,24},{24,28},{28,0},{1,5},{5... | collective-permute-start | bytes 835592 | tf_op jit(solution)/shard_map/ppermute | solution.py:25
  11.8 4.4 %copy-start.1 = (bf16[2048]{0:T(1024)(128)(2,1)S(1)}, bf16[2048]{0:T(1024)(128)(2,1)}, u32[]{:S(2)}) copy-start(bf16[2048]{0:T(1024)(128)(2,1)} %param.16) | copy-start | bytes 12292
  11.8 4.7 %copy-start = (bf16[512,2048]{1,0:T(8,128)(2,1)S(1)}, bf16[512,2048]{1,0:T(8,128)(2,1)}, u32[]{:S(2)}) copy-start(bf16[512,2048]{1,0:T(8,128)(2,1)} %refs_7_.1) | copy-start | bytes 6291460
  11.8 12.0 %collective-permute-start.4 = (bf16[128,512]{1,0:T(8,128)(2,1)S(1)}, bf16[128,512]{1,0:T(8,128)(2,1)S(1)}, u32[]{:S(2)}, u32[]{:S(2)}) collective-permute-start(bf16[128,512]{1,0:T(8,128)(2,1)S(1)} %state1024.1), channel_id=1, source_target_pairs={{0,4},{4,8},{8,12},{12,16},{16,20},{20,24},{24,28},{28,0},{1,5},{5... | collective-permute-start | bytes 393224 | tf_op jit(solution)/shard_map/ppermute | solution.py:25
  14.6 11.6 %collective-permute-start.2 = (bf16[128,512]{1,0:T(8,128)(2,1)S(1)}, bf16[128,512]{1,0:T(8,128)(2,1)S(1)}, u32[]{:S(2)}, u32[]{:S(2)}) collective-permute-start(bf16[128,512]{1,0:T(8,128)(2,1)S(1)} %state1536.1), channel_id=1, source_target_pairs={{0,4},{4,8},{8,12},{12,16},{16,20},{20,24},{24,28},{28,0},{1,5},{5... | collective-permute-start | bytes 393224 | tf_op jit(solution)/shard_map/ppermute | solution.py:25

commit v8 on v7

--- a/solution.py
+++ b/solution.py
@@ -174,13 +174,13 @@
     first, second = mids
     table = jnp.concatenate(
         [
-            jnp.exp(first + second),
-            jnp.exp(first + 2.0 * second) * keep,
+            jnp.exp(first),
             jnp.exp(second),
-            jnp.exp(first),
-            jnp.exp(2.0 * first + second),
+            jnp.exp(2.0 * first),
+            jnp.exp(2.0 * second) * keep,
             jnp.exp(2.0 * (first + second)) * whole,
             first,
+            second,
             second,
         ],
         axis=0,
@@ -372,7 +372,8 @@
             values = jnp.concatenate([edges[1][:, cols], values[EDGE:]], axis=0)
         first = mm(pieces[0], values)
         second = mm(pieces[1], xs_ref[CHUNK:, part])
-        end = first * rows_ref[1:2, cols] + second * rows_ref[2:3, cols]
+        first = first * rows_ref[0:1, cols] * rows_ref[3:4, cols]
+        end = first + second * rows_ref[1:2, cols]
         end_ref[:DSTATE, here] = end.astype(end_ref.dtype)
 
 
@@ -410,7 +411,8 @@
         cols = slice(start, start + WIDE)
         spread = spread_matrix(2, heads, start, WIDE)
         values = xs_ref[:CHUNK, part]
-        middle = (mm(ending_ref[...], values) * rows_ref[0:1, cols]).astype(BF16)
+        middle = mm(ending_ref[...], values) * rows_ref[0:1, cols]
+        middle = (middle * rows_ref[1:2, cols]).astype(BF16)
         for j in range(2):
             span = slice(j * CHUNK, (j + 1) * CHUNK)
             if j == 0:
@@ -420,7 +422,8 @@
             half = 0.5 * z_ref[span, cols].astype(F32)
             gate = (half + half * jnp.tanh(half)) * mm(eps_ref[span, :], spread)
             y_ref[span, here] = y * gate
-            dec_ref[span, here] = rows_ref[3 + j : 4 + j, cols] * gate
+            decay = gate * rows_ref[j : j + 1, cols]
+            dec_ref[span, here] = decay * rows_ref[2:3, cols] if j else decay
 
 
 def final_kernel(low, state_ref, edge_ref, y_ref, dec_ref, live_ref, gain_ref, *refs):
@@ -555,7 +558,7 @@
     def relay(low, width, end):
         if turns == 1:
             return shifted(end, "ctx", 1)
-        through = table[5:6, low : low + width]
+        through = table[4:5, low : low + width]
         turn = lambda _, incoming: shifted(through * incoming + end, "ctx", 1)
         return lax.fori_loop(0, turns, turn, jnp.zeros_like(end)).astype(BF16)
 

time: 27.6 us -> 27.6 us (level)
  no operation moved by 1% of the time
where the time goes in v8:
time: 27.6 us; the launch traced here: 27.4 us
  Pallas kernels  15 us (54%)
  starting transfers between devices  8 us (29%)
  waiting for transfers between devices  4.25 us (15%)
    ppermute x3, starting transfers between devices, shifted(): return lax.ppermute(value, axis, pairs)  4.92 us
    pallas_call x3, Pallas kernels, on_device(): call(functools.partial(final_kernel, low), in_specs, shape((rows, columns...  4.06 us
    ppermute x3, waiting for transfers between devices, shifted(): return lax.ppermute(value, axis, pairs)  3.84 us
    pallas_call x4, Pallas kernels, on_device(): call(functools.partial(conv_kernel, place), [spec] * (4 + len(kept)), [sh...  3.79 us
    ppermute x2, starting transfers between devices, crossed(): lax.ppermute(value, axis, [(source, source ^ mask) for source in range(co...  3.07 us
    pallas_call x3, Pallas kernels, on_device(): call(functools.partial(local_kernel, low), [spec] * (6 + len(pieces)), [s...  2.62 us
    pallas_call x1, Pallas kernels, on_device(): call(prep_kernel, [spec] * 3 + [hbm], [shape((rows, 2 * heads), BF16), sh...  1.6 us
    pallas_call x1, Pallas kernels, on_device(): call(bc_kernel, [hbm] * 6, [shape((bc_width + 8, rows), BF16), shape((1,...  1.37 us
  transfers between devices with their start and end apart: 5, of which 4 were waited for; matrix products, arithmetic and copies ran while one was open for 0% of the time, Pallas kernels for 44%

profile of v8, /device:TPU:0, one launch (start us, length us, event | category | flops | bytes accessed | tf_op | source)
XLA Modules:
  0.0 27.4 jit_solution(4700175949678461326)
XLA Ops:
  0.0 1.4 %bc.1 = (bf16[72,512]{1,0:T(8,128)(2,1)S(1)}, s32[1,512]{1,0:T(1,128)S(1)}, f32[32,512]{1,0:T(8,128)S(1)}, f32[1,32]{1,0:T(1,128)S(1)}, bf16[4,2048]{1,0:T(4,128)(2,1)S(1)}) custom-call(bf16[64,512]{1,0:T(8,128)(2,1)} %bitcast.4, bf16[4,64]{1,0:T(4,128)(2,1)} %refs_1_.1, s32[1,512]{1,0:T(1,128)} %bitcast.6, f32[32,512]{1,0:T(8,128)} %bitcast.5, ...), custom_call_target="tpu_custom_call" | custom-call | tf_op jit(solution)/shard_map/bc/pallas_call | solution.py:466
  1.4 3.0 %collective-permute-start = (bf16[72,512]{1,0:T(8,128)(2,1)S(1)}, bf16[72,512]{1,0:T(8,128)(2,1)S(1)}, u32[]{:S(2)}, u32[]{:S(2)}) collective-permute-start(bf16[72,512]{1,0:T(8,128)(2,1)S(1)} %get-tuple-element.38.refs_0_), channel_id=1, source_target_pairs={{0,2},{1,3},{2,0},{3,1},{4,6},{5,7},{6,4},{7,5},{8,10},{9,11},{10,... | collective-permute-start | bytes 221192 | tf_op jit(solution)/shard_map/ppermute | solution.py:30
  4.4 1.6 %prep.1 = (bf16[512,64]{1,0:T(8,128)(2,1)S(1)}, bf16[512,64]{1,0:T(8,128)(2,1)S(1)}, bf16[16,64]{1,0:T(8,128)(2,1)S(1)}, f32[8,2048]{1,0:T(8,128)S(1)}, f32[512,...) custom-call(f32[32,512]{1,0:T(8,128)S(1)} %get-tuple-element.31.dt_ref, ...), custom_call_target="tpu_custom_call" | custom-call | tf_op jit(solution)/shard_map/prep/pallas_call | solution.py:491
  6.0 0.9 %conv0.1 = (bf16[512,512]{1,0:T(8,128)(2,1)S(1)}, bf16[72,512]{1,0:T(8,128)(2,1)S(1)}) custom-call(bf16[512,2048]{1,0:T(8,128)(2,1)S(1)} %get-tuple-element.34.x_ref.refs_6_, bf16[4,2048]{1,0:T(4,128)(2,1)S(1)} %get-tuple-element.35.taps_ref, bf16[512,64]{1,0:T(8,128)(2,1)S(1)} %get-tuple-element.36.fac_ref, ...), custom_call_target="tpu_custom_call" | custom-call | tf_op jit(solution)/shard_map/conv0/pallas_call | solution.py:513
  7.1 0.9 %conv1.1.refs_3_.refs_1_ = bf16[512,512]{1,0:T(8,128)(2,1)S(1)} custom-call(bf16[512,2048]{1,0:T(8,128)(2,1)S(1)} %get-tuple-element.34.x_ref.refs_6_, bf16[4,2048]{1,0:T(4,128)(2,1)S(1)} %get-tuple-element.35.taps_ref, bf16[512,64]{1,0:T(8,128)(2,1)S(1)} %get-tuple-element.36.fac_ref, f32[512,128]{1,0:T(8,128)S(1)} %get-tuple-element.37.idc_ref.refs_2_), custom_call_target="tpu_custom_call" | custom-call | tf_op jit(solution)/shard_map/conv1/pallas_call | solution.py:513
  8.0 0.4 %collective-permute-done.1.refs_1_ = bf16[144,512]{1,0:T(8,128)(2,1)S(1)} collective-permute-done((bf16[144,512]{1,0:T(8,128)(2,1)S(1)}, bf16[144,512]{1,0:T(8,128)(2,1)S(1)}, u32[]{:S(2)}, u32[]{:S(2)}) %collective-permute-start.1) | collective-permute-done | bytes 147488 | tf_op jit(solution)/shard_map/ppermute | solution.py:30
  8.4 0.4 %state0.1 = bf16[136,1024]{1,0:T(8,128)(2,1)S(1)} custom-call(bf16[144,512]{1,0:T(8,128)(2,1)S(1)} %constant_dynamic-update-slice_fusion.refs_0_, bf16[144,512]{1,0:T(8,128)(2,1)S(1)} %collective-permute-done.1.refs_1_, bf16[512,512]{1,0:T(8,128)(2,1)S(1)} %get-tuple-element.42.refs_2_.refs_0_, bf16[512,512]{1,0:T(8,128)(2,1)S(1)} %conv1.1.refs_3_.refs_1_, ...), custom_call_target="tpu_custom_call" | custom-call | tf_op jit(solution)/shard_map/state0/pallas_call | solution.py:570
  8.8 1.8 %collective-permute-start.3 = (bf16[136,1024]{1,0:T(8,128)(2,1)S(1)}, bf16[136,1024]{1,0:T(8,128)(2,1)S(1)}, u32[]{:S(2)}, u32[]{:S(2)}) collective-permute-start(bf16[136,1024]{1,0:T(8,128)(2,1)S(1)} %state0.1), channel_id=1, source_target_pairs={{0,4},{4,8},{8,12},{12,16},{16,20},{20,24},{24,28},{28,0},{1,5},{5... | collective-permute-start | bytes 835592 | tf_op jit(solution)/shard_map/ppermute | solution.py:25
  10.6 0.9 %conv2.1.refs_2_.refs_0_ = bf16[512,512]{1,0:T(8,128)(2,1)S(1)} custom-call(bf16[512,2048]{1,0:T(8,128)(2,1)S(1)} %get-tuple-element.34.x_ref.refs_6_, bf16[4,2048]{1,0:T(4,128)(2,1)S(1)} %get-tuple-element.35.taps_ref, bf16[512,64]{1,0:T(8,128)(2,1)S(1)} %get-tuple-element.36.fac_ref, f32[512,128]{1,0:T(8,128)S(1)} %get-tuple-element.37.idc_ref.refs_2_), custom_call_target="tpu_custom_call" | custom-call | tf_op jit(solution)/shard_map/conv2/pallas_call | solution.py:513
  11.8 1.6 %collective-permute-start.4 = (bf16[128,512]{1,0:T(8,128)(2,1)S(1)}, bf16[128,512]{1,0:T(8,128)(2,1)S(1)}, u32[]{:S(2)}, u32[]{:S(2)}) collective-permute-start(bf16[128,512]{1,0:T(8,128)(2,1)S(1)} %state1024.1), channel_id=1, source_target_pairs={{0,4},{4,8},{8,12},{12,16},{16,20},{20,24},{24,28},{28,0},{1,5},{5... | collective-permute-start | bytes 393224 | tf_op jit(solution)/shard_map/ppermute | solution.py:25
  13.4 0.9 %conv3.1.refs_2_.refs_0_ = bf16[512,512]{1,0:T(8,128)(2,1)S(1)} custom-call(bf16[512,2048]{1,0:T(8,128)(2,1)S(1)} %get-tuple-element.34.x_ref.refs_6_, bf16[4,2048]{1,0:T(4,128)(2,1)S(1)} %get-tuple-element.35.taps_ref, bf16[512,64]{1,0:T(8,128)(2,1)S(1)} %get-tuple-element.36.fac_ref, f32[512,128]{1,0:T(8,128)S(1)} %get-tuple-element.37.idc_ref.refs_2_), custom_call_target="tpu_custom_call" | custom-call | tf_op jit(solution)/shard_map/conv3/pallas_call | solution.py:513
  14.3 0.3 %state1536.1 = bf16[128,512]{1,0:T(8,128)(2,1)S(1)} custom-call(bf16[144,512]{1,0:T(8,128)(2,1)S(1)} %constant_dynamic-update-slice_fusion.refs_0_, bf16[144,512]{1,0:T(8,128)(2,1)S(1)} %collective-permute-done.1.refs_1_, bf16[512,512]{1,0:T(8,128)(2,1)S(1)} %conv3.1.refs_2_.refs_0_, f32[8,2048]{1,0:T(8,128)S(1)} %get-tuple-element.40.refs_3_.refs_4_.refs_5_.refs_6_, ...), custom_call_target="tpu_custom_call" | custom-call | tf_op jit(solution)/shard_map/state1536/pallas_call | solution.py:570
  14.6 1.6 %collective-permute-start.2 = (bf16[128,512]{1,0:T(8,128)(2,1)S(1)}, bf16[128,512]{1,0:T(8,128)(2,1)S(1)}, u32[]{:S(2)}, u32[]{:S(2)}) collective-permute-start(bf16[128,512]{1,0:T(8,128)(2,1)S(1)} %state1536.1), channel_id=1, source_target_pairs={{0,4},{4,8},{8,12},{12,16},{16,20},{20,24},{24,28},{28,0},{1,5},{5... | collective-permute-start | bytes 393224 | tf_op jit(solution)/shard_map/ppermute | solution.py:25
  16.2 0.3 %score.1 = (bf16[2,256,256]{2,1,0:T(8,128)(2,1)S(1)}, bf16[512,128]{1,0:T(8,128)(2,1)S(1)}, bf16[256,128]{1,0:T(8,128)(2,1)S(1)}, bf16[128,256]{1,0:T(8,128)(2,1)S(1)}) custom-call(bf16[144,512]{1,0:T(8,128)(2,1)S(1)} %constant_dynamic-update-slice_fusion.refs_0_, bf16[144,512]{1,0:T(8,128)(2,1)S(1)} %collective-permute-done.1.refs_1_, ...), custom_call_target="tpu_custom_call" | custom-call | tf_op jit(solution)/shard_map/score/pallas_call | solution.py:539
  16.5 1.2 %local0.1 = (f32[512,1024]{1,0:T(8,128)S(1)}, f32[512,1024]{1,0:T(8,128)S(1)}) custom-call(bf16[512,512]{1,0:T(8,128)(2,1)S(1)} %get-tuple-element.42.refs_2_.refs_0_, bf16[512,512]{1,0:T(8,128)(2,1)S(1)} %conv1.1.refs_3_.refs_1_, bf16[2,256,256]{2,1,0:T(8,128)(2,1)S(1)} %get-tuple-element.46.refs_1_.refs_2_, ...), custom_call_target="tpu_custom_call" | custom-call | tf_op jit(solution)/shard_map/local0/pallas_call | solution.py:583
  17.7 0.7 %local1024.1 = (f32[512,512]{1,0:T(8,128)S(1)}, f32[512,512]{1,0:T(8,128)S(1)}) custom-call(bf16[512,512]{1,0:T(8,128)(2,1)S(1)} %conv2.1.refs_2_.refs_0_, bf16[2,256,256]{2,1,0:T(8,128)(2,1)S(1)} %get-tuple-element.46.refs_1_.refs_2_, bf16[256,128]{1,0:T(8,128)(2,1)S(1)} %get-tuple-element.47.refs_2_.refs_3_, ...), custom_call_target="tpu_custom_call" | custom-call | tf_op jit(solution)/shard_map/local1024/pallas_call | solution.py:583
  18.4 0.7 %local1536.1 = (f32[512,512]{1,0:T(8,128)S(1)}, f32[512,512]{1,0:T(8,128)S(1)}) custom-call(bf16[512,512]{1,0:T(8,128)(2,1)S(1)} %conv3.1.refs_2_.refs_0_, bf16[2,256,256]{2,1,0:T(8,128)(2,1)S(1)} %get-tuple-element.46.refs_1_.refs_2_, bf16[256,128]{1,0:T(8,128)(2,1)S(1)} %get-tuple-element.47.refs_2_.refs_3_, ...), custom_call_target="tpu_custom_call" | custom-call | tf_op jit(solution)/shard_map/local1536/pallas_call | solution.py:583
  19.2 1.9 %collective-permute-done.3.rim_ref.state_ref = bf16[136,1024]{1,0:T(8,128)(2,1)S(1)} collective-permute-done((bf16[136,1024]{1,0:T(8,128)(2,1)S(1)}, bf16[136,1024]{1,0:T(8,128)(2,1)S(1)}, u32[]{:S(2)}, u32[]{:S(2)}) %collective-permute-start.3) | collective-permute-done | bytes 278560 | tf_op jit(solution)/shard_map/ppermute | solution.py:25
  21.0 0.3 %fix.1 = (bf16[512,256]{1,0:T(8,128)(2,1)S(1)}, bf16[16,2048]{1,0:T(8,128)(2,1)S(1)}) custom-call(bf16[512,2048]{1,0:T(8,128)(2,1)S(1)} %get-tuple-element.34.x_ref.refs_6_, bf16[136,1024]{1,0:T(8,128)(2,1)S(1)} %collective-permute-done.3.rim_ref.state_ref, bf16[4,2048]{1,0:T(4,128)(2,1)S(1)} %get-tuple-element.35.taps_ref, ...), custom_call_target="tpu_custom_call" | custom-call | tf_op jit(solution)/shard_map/fix/pallas_call | solution.py:548
  21.4 1.6 %final0.1.refs_0_ = bf16[512,2048]{1,0:T(8,128)(2,1)} custom-call(bf16[136,1024]{1,0:T(8,128)(2,1)S(1)} %collective-permute-done.3.rim_ref.state_ref, bf16[16,2048]{1,0:T(8,128)(2,1)S(1)} %get-tuple-element.45.edge_ref, f32[512,1024]{1,0:T(8,128)S(1)} %get-tuple-element.55.y_ref, f32[512,1024]{1,0:T(8,128)S(1)} %get-tuple-element.56.dec_ref, ...), custom_call_target="tpu_custom_call" | custom-call | tf_op jit(solution)/shard_map/final0/pallas_call | solution.py:596
  23.0 0.9 %collective-permute-done.4.state_ref = bf16[128,512]{1,0:T(8,128)(2,1)S(1)} collective-permute-done((bf16[128,512]{1,0:T(8,128)(2,1)S(1)}, bf16[128,512]{1,0:T(8,128)(2,1)S(1)}, u32[]{:S(2)}, u32[]{:S(2)}) %collective-permute-start.4) | collective-permute-done | bytes 131104 | tf_op jit(solution)/shard_map/ppermute | solution.py:25
  23.8 1.2 %final1024.1.refs_0_ = bf16[512,2048]{1,0:T(8,128)(2,1)} custom-call(bf16[128,512]{1,0:T(8,128)(2,1)S(1)} %collective-permute-done.4.state_ref, bf16[16,2048]{1,0:T(8,128)(2,1)S(1)} %get-tuple-element.45.edge_ref, f32[512,512]{1,0:T(8,128)S(1)} %get-tuple-element.53.y_ref, f32[512,512]{1,0:T(8,128)S(1)} %get-tuple-element.54.dec_ref, ...), custom_call_target="tpu_custom_call", output_to_operand_aliasing={{}: (6, {})} | custom-call | tf_op jit(solution)/shard_map/final1024/pallas_call | solution.py:596
  25.1 1.1 %collective-permute-done.2.state_ref = bf16[128,512]{1,0:T(8,128)(2,1)S(1)} collective-permute-done((bf16[128,512]{1,0:T(8,128)(2,1)S(1)}, bf16[128,512]{1,0:T(8,128)(2,1)S(1)}, u32[]{:S(2)}, u32[]{:S(2)}) %collective-permute-start.2) | collective-permute-done | bytes 131104 | tf_op jit(solution)/shard_map/ppermute | solution.py:25
  26.2 1.3 %final1536.1 = bf16[512,2048]{1,0:T(8,128)(2,1)} custom-call(bf16[128,512]{1,0:T(8,128)(2,1)S(1)} %collective-permute-done.2.state_ref, bf16[16,2048]{1,0:T(8,128)(2,1)S(1)} %get-tuple-element.45.edge_ref, f32[512,512]{1,0:T(8,128)S(1)} %get-tuple-element.50.y_ref, f32[512,512]{1,0:T(8,128)S(1)} %get-tuple-element.51.dec_ref, ...), custom_call_target="tpu_custom_call", output_to_operand_aliasing={{}: (6, {})} | custom-call | tf_op jit(solution)/shard_map/final1536/pallas_call | solution.py:596
  (10 shorter events, 0.4 us)
Async XLA Ops:
  1.4 5.6 %collective-permute-start = (bf16[72,512]{1,0:T(8,128)(2,1)S(1)}, bf16[72,512]{1,0:T(8,128)(2,1)S(1)}, u32[]{:S(2)}, u32[]{:S(2)}) collective-permute-start(bf16[72,512]{1,0:T(8,128)(2,1)S(1)} %get-tuple-element.38.refs_0_), channel_id=1, source_target_pairs={{0,2},{1,3},{2,0},{3,1},{4,6},{5,7},{6,4},{7,5},{8,10},{9,11},{10,... | collective-permute-start | bytes 221192 | tf_op jit(solution)/shard_map/ppermute | solution.py:30
  7.0 1.4 %collective-permute-start.1 = (bf16[144,512]{1,0:T(8,128)(2,1)S(1)}, bf16[144,512]{1,0:T(8,128)(2,1)S(1)}, u32[]{:S(2)}, u32[]{:S(2)}) collective-permute-start(bf16[144,512]{1,0:T(8,128)(2,1)S(1)} %constant_dynamic-update-slice_fusion.refs_0_), channel_id=1, source_target_pairs={{0,1},{1,0},{2,3},{3,2},{4,5},{5,4},{6,7},{7,6},{8,9},{9,8},{10,11... | collective-permute-start | bytes 442376 | tf_op jit(solution)/shard_map/ppermute | solution.py:30
  8.8 12.3 %collective-permute-start.3 = (bf16[136,1024]{1,0:T(8,128)(2,1)S(1)}, bf16[136,1024]{1,0:T(8,128)(2,1)S(1)}, u32[]{:S(2)}, u32[]{:S(2)}) collective-permute-start(bf16[136,1024]{1,0:T(8,128)(2,1)S(1)} %state0.1), channel_id=1, source_target_pairs={{0,4},{4,8},{8,12},{12,16},{16,20},{20,24},{24,28},{28,0},{1,5},{5... | collective-permute-start | bytes 835592 | tf_op jit(solution)/shard_map/ppermute | solution.py:25
  11.8 4.4 %copy-start.1 = (bf16[2048]{0:T(1024)(128)(2,1)S(1)}, bf16[2048]{0:T(1024)(128)(2,1)}, u32[]{:S(2)}) copy-start(bf16[2048]{0:T(1024)(128)(2,1)} %param.16) | copy-start | bytes 12292
  11.8 4.7 %copy-start = (bf16[512,2048]{1,0:T(8,128)(2,1)S(1)}, bf16[512,2048]{1,0:T(8,128)(2,1)}, u32[]{:S(2)}) copy-start(bf16[512,2048]{1,0:T(8,128)(2,1)} %refs_7_.1) | copy-start | bytes 6291460
  11.8 12.0 %collective-permute-start.4 = (bf16[128,512]{1,0:T(8,128)(2,1)S(1)}, bf16[128,512]{1,0:T(8,128)(2,1)S(1)}, u32[]{:S(2)}, u32[]{:S(2)}) collective-permute-start(bf16[128,512]{1,0:T(8,128)(2,1)S(1)} %state1024.1), channel_id=1, source_target_pairs={{0,4},{4,8},{8,12},{12,16},{16,20},{20,24},{24,28},{28,0},{1,5},{5... | collective-permute-start | bytes 393224 | tf_op jit(solution)/shard_map/ppermute | solution.py:25
  14.6 11.6 %collective-permute-start.2 = (bf16[128,512]{1,0:T(8,128)(2,1)S(1)}, bf16[128,512]{1,0:T(8,128)(2,1)S(1)}, u32[]{:S(2)}, u32[]{:S(2)}) collective-permute-start(bf16[128,512]{1,0:T(8,128)(2,1)S(1)} %state1536.1), channel_id=1, source_target_pairs={{0,4},{4,8},{8,12},{12,16},{16,20},{20,24},{24,28},{28,0},{1,5},{5... | collective-permute-start | bytes 393224 | tf_op jit(solution)/shard_map/ppermute | solution.py:25

commit v9 on v8

--- a/solution.py
+++ b/solution.py
@@ -199,12 +199,13 @@
     ]
     for copy in copies:
         copy.start()
-    for copy in copies[:3]:
-        copy.wait()
-    values = jnp.concatenate([jnp.zeros((width, 128), F32), bc_ref[...].astype(F32)], axis=1)
+    copies[1].wait()
+    copies[2].wait()
     starts = jnp.broadcast_to(start_ref[...].astype(F32), (8, rows))
     open_ = jnp.concatenate([jnp.ones((8, 128), F32), 1.0 - starts], axis=1)
     taps = jnp.concatenate([taps_ref[...].astype(F32)] * 2, axis=0).T
+    copies[0].wait()
+    values = jnp.concatenate([jnp.zeros((width, 128), F32), bc_ref[...].astype(F32)], axis=1)
     total = values[:, 128:] * taps[:, CONV - 1 : CONV]
     kept = open_
     for back in range(1, CONV):

time: 27.6 us -> 27.6 us (level)
  no operation moved by 1% of the time
where the time goes in v9:
time: 27.6 us; the launch traced here: 27.4 us
  Pallas kernels  15 us (54%)
  starting transfers between devices  8 us (29%)
  waiting for transfers between devices  4.25 us (15%)
    ppermute x3, starting transfers between devices, shifted(): return lax.ppermute(value, axis, pairs)  4.93 us
    pallas_call x3, Pallas kernels, on_device(): call(functools.partial(final_kernel, low), in_specs, shape((rows, columns...  4.06 us
    ppermute x3, waiting for transfers between devices, shifted(): return lax.ppermute(value, axis, pairs)  3.84 us
    pallas_call x4, Pallas kernels, on_device(): call(functools.partial(conv_kernel, place), [spec] * (4 + len(kept)), [sh...  3.78 us
    ppermute x2, starting transfers between devices, crossed(): lax.ppermute(value, axis, [(source, source ^ mask) for source in range(co...  3.07 us
    pallas_call x3, Pallas kernels, on_device(): call(functools.partial(local_kernel, low), [spec] * (6 + len(pieces)), [s...  2.62 us
    pallas_call x1, Pallas kernels, on_device(): call(prep_kernel, [spec] * 3 + [hbm], [shape((rows, 2 * heads), BF16), sh...  1.6 us
    pallas_call x1, Pallas kernels, on_device(): call(bc_kernel, [hbm] * 6, [shape((bc_width + 8, rows), BF16), shape((1,...  1.35 us
  transfers between devices with their start and end apart: 5, of which 4 were waited for; matrix products, arithmetic and copies ran while one was open for 0% of the time, Pallas kernels for 44%

profile of v9, /device:TPU:0, one launch (start us, length us, event | category | flops | bytes accessed | tf_op | source)
XLA Modules:
  0.0 27.4 jit_solution(609187201583126398)
XLA Ops:
  0.0 1.4 %bc.1 = (bf16[72,512]{1,0:T(8,128)(2,1)S(1)}, s32[1,512]{1,0:T(1,128)S(1)}, f32[32,512]{1,0:T(8,128)S(1)}, f32[1,32]{1,0:T(1,128)S(1)}, bf16[4,2048]{1,0:T(4,128)(2,1)S(1)}) custom-call(bf16[64,512]{1,0:T(8,128)(2,1)} %bitcast.4, bf16[4,64]{1,0:T(4,128)(2,1)} %refs_1_.1, s32[1,512]{1,0:T(1,128)} %bitcast.6, f32[32,512]{1,0:T(8,128)} %bitcast.5, ...), custom_call_target="tpu_custom_call" | custom-call | tf_op jit(solution)/shard_map/bc/pallas_call | solution.py:467
  1.4 3.0 %collective-permute-start = (bf16[72,512]{1,0:T(8,128)(2,1)S(1)}, bf16[72,512]{1,0:T(8,128)(2,1)S(1)}, u32[]{:S(2)}, u32[]{:S(2)}) collective-permute-start(bf16[72,512]{1,0:T(8,128)(2,1)S(1)} %get-tuple-element.38.refs_0_), channel_id=1, source_target_pairs={{0,2},{1,3},{2,0},{3,1},{4,6},{5,7},{6,4},{7,5},{8,10},{9,11},{10,... | collective-permute-start | bytes 221192 | tf_op jit(solution)/shard_map/ppermute | solution.py:30
  4.4 1.6 %prep.1 = (bf16[512,64]{1,0:T(8,128)(2,1)S(1)}, bf16[512,64]{1,0:T(8,128)(2,1)S(1)}, bf16[16,64]{1,0:T(8,128)(2,1)S(1)}, f32[8,2048]{1,0:T(8,128)S(1)}, f32[512,...) custom-call(f32[32,512]{1,0:T(8,128)S(1)} %get-tuple-element.31.dt_ref, ...), custom_call_target="tpu_custom_call" | custom-call | tf_op jit(solution)/shard_map/prep/pallas_call | solution.py:492
  6.0 0.9 %conv0.1 = (bf16[512,512]{1,0:T(8,128)(2,1)S(1)}, bf16[72,512]{1,0:T(8,128)(2,1)S(1)}) custom-call(bf16[512,2048]{1,0:T(8,128)(2,1)S(1)} %get-tuple-element.34.x_ref.refs_6_, bf16[4,2048]{1,0:T(4,128)(2,1)S(1)} %get-tuple-element.35.taps_ref, bf16[512,64]{1,0:T(8,128)(2,1)S(1)} %get-tuple-element.36.fac_ref, ...), custom_call_target="tpu_custom_call" | custom-call | tf_op jit(solution)/shard_map/conv0/pallas_call | solution.py:514
  7.0 0.9 %conv1.1.refs_3_.refs_1_ = bf16[512,512]{1,0:T(8,128)(2,1)S(1)} custom-call(bf16[512,2048]{1,0:T(8,128)(2,1)S(1)} %get-tuple-element.34.x_ref.refs_6_, bf16[4,2048]{1,0:T(4,128)(2,1)S(1)} %get-tuple-element.35.taps_ref, bf16[512,64]{1,0:T(8,128)(2,1)S(1)} %get-tuple-element.36.fac_ref, f32[512,128]{1,0:T(8,128)S(1)} %get-tuple-element.37.idc_ref.refs_2_), custom_call_target="tpu_custom_call" | custom-call | tf_op jit(solution)/shard_map/conv1/pallas_call | solution.py:514
  8.0 0.4 %collective-permute-done.1.refs_1_ = bf16[144,512]{1,0:T(8,128)(2,1)S(1)} collective-permute-done((bf16[144,512]{1,0:T(8,128)(2,1)S(1)}, bf16[144,512]{1,0:T(8,128)(2,1)S(1)}, u32[]{:S(2)}, u32[]{:S(2)}) %collective-permute-start.1) | collective-permute-done | bytes 147488 | tf_op jit(solution)/shard_map/ppermute | solution.py:30
  8.4 0.4 %state0.1 = bf16[136,1024]{1,0:T(8,128)(2,1)S(1)} custom-call(bf16[144,512]{1,0:T(8,128)(2,1)S(1)} %constant_dynamic-update-slice_fusion.refs_0_, bf16[144,512]{1,0:T(8,128)(2,1)S(1)} %collective-permute-done.1.refs_1_, bf16[512,512]{1,0:T(8,128)(2,1)S(1)} %get-tuple-element.42.refs_2_.refs_0_, bf16[512,512]{1,0:T(8,128)(2,1)S(1)} %conv1.1.refs_3_.refs_1_, ...), custom_call_target="tpu_custom_call" | custom-call | tf_op jit(solution)/shard_map/state0/pallas_call | solution.py:571
  8.8 1.8 %collective-permute-start.3 = (bf16[136,1024]{1,0:T(8,128)(2,1)S(1)}, bf16[136,1024]{1,0:T(8,128)(2,1)S(1)}, u32[]{:S(2)}, u32[]{:S(2)}) collective-permute-start(bf16[136,1024]{1,0:T(8,128)(2,1)S(1)} %state0.1), channel_id=1, source_target_pairs={{0,4},{4,8},{8,12},{12,16},{16,20},{20,24},{24,28},{28,0},{1,5},{5... | collective-permute-start | bytes 835592 | tf_op jit(solution)/shard_map/ppermute | solution.py:25
  10.5 0.9 %conv2.1.refs_2_.refs_0_ = bf16[512,512]{1,0:T(8,128)(2,1)S(1)} custom-call(bf16[512,2048]{1,0:T(8,128)(2,1)S(1)} %get-tuple-element.34.x_ref.refs_6_, bf16[4,2048]{1,0:T(4,128)(2,1)S(1)} %get-tuple-element.35.taps_ref, bf16[512,64]{1,0:T(8,128)(2,1)S(1)} %get-tuple-element.36.fac_ref, f32[512,128]{1,0:T(8,128)S(1)} %get-tuple-element.37.idc_ref.refs_2_), custom_call_target="tpu_custom_call" | custom-call | tf_op jit(solution)/shard_map/conv2/pallas_call | solution.py:514
  11.8 1.6 %collective-permute-start.4 = (bf16[128,512]{1,0:T(8,128)(2,1)S(1)}, bf16[128,512]{1,0:T(8,128)(2,1)S(1)}, u32[]{:S(2)}, u32[]{:S(2)}) collective-permute-start(bf16[128,512]{1,0:T(8,128)(2,1)S(1)} %state1024.1), channel_id=1, source_target_pairs={{0,4},{4,8},{8,12},{12,16},{16,20},{20,24},{24,28},{28,0},{1,5},{5... | collective-permute-start | bytes 393224 | tf_op jit(solution)/shard_map/ppermute | solution.py:25
  13.4 0.9 %conv3.1.refs_2_.refs_0_ = bf16[512,512]{1,0:T(8,128)(2,1)S(1)} custom-call(bf16[512,2048]{1,0:T(8,128)(2,1)S(1)} %get-tuple-element.34.x_ref.refs_6_, bf16[4,2048]{1,0:T(4,128)(2,1)S(1)} %get-tuple-element.35.taps_ref, bf16[512,64]{1,0:T(8,128)(2,1)S(1)} %get-tuple-element.36.fac_ref, f32[512,128]{1,0:T(8,128)S(1)} %get-tuple-element.37.idc_ref.refs_2_), custom_call_target="tpu_custom_call" | custom-call | tf_op jit(solution)/shard_map/conv3/pallas_call | solution.py:514
  14.3 0.3 %state1536.1 = bf16[128,512]{1,0:T(8,128)(2,1)S(1)} custom-call(bf16[144,512]{1,0:T(8,128)(2,1)S(1)} %constant_dynamic-update-slice_fusion.refs_0_, bf16[144,512]{1,0:T(8,128)(2,1)S(1)} %collective-permute-done.1.refs_1_, bf16[512,512]{1,0:T(8,128)(2,1)S(1)} %conv3.1.refs_2_.refs_0_, f32[8,2048]{1,0:T(8,128)S(1)} %get-tuple-element.40.refs_3_.refs_4_.refs_5_.refs_6_, ...), custom_call_target="tpu_custom_call" | custom-call | tf_op jit(solution)/shard_map/state1536/pallas_call | solution.py:571
  14.6 1.6 %collective-permute-start.2 = (bf16[128,512]{1,0:T(8,128)(2,1)S(1)}, bf16[128,512]{1,0:T(8,128)(2,1)S(1)}, u32[]{:S(2)}, u32[]{:S(2)}) collective-permute-start(bf16[128,512]{1,0:T(8,128)(2,1)S(1)} %state1536.1), channel_id=1, source_target_pairs={{0,4},{4,8},{8,12},{12,16},{16,20},{20,24},{24,28},{28,0},{1,5},{5... | collective-permute-start | bytes 393224 | tf_op jit(solution)/shard_map/ppermute | solution.py:25
  16.2 0.3 %score.1 = (bf16[2,256,256]{2,1,0:T(8,128)(2,1)S(1)}, bf16[512,128]{1,0:T(8,128)(2,1)S(1)}, bf16[256,128]{1,0:T(8,128)(2,1)S(1)}, bf16[128,256]{1,0:T(8,128)(2,1)S(1)}) custom-call(bf16[144,512]{1,0:T(8,128)(2,1)S(1)} %constant_dynamic-update-slice_fusion.refs_0_, bf16[144,512]{1,0:T(8,128)(2,1)S(1)} %collective-permute-done.1.refs_1_, ...), custom_call_target="tpu_custom_call" | custom-call | tf_op jit(solution)/shard_map/score/pallas_call | solution.py:540
  16.5 1.2 %local0.1 = (f32[512,1024]{1,0:T(8,128)S(1)}, f32[512,1024]{1,0:T(8,128)S(1)}) custom-call(bf16[512,512]{1,0:T(8,128)(2,1)S(1)} %get-tuple-element.42.refs_2_.refs_0_, bf16[512,512]{1,0:T(8,128)(2,1)S(1)} %conv1.1.refs_3_.refs_1_, bf16[2,256,256]{2,1,0:T(8,128)(2,1)S(1)} %get-tuple-element.46.refs_1_.refs_2_, ...), custom_call_target="tpu_custom_call" | custom-call | tf_op jit(solution)/shard_map/local0/pallas_call | solution.py:584
  17.7 0.7 %local1024.1 = (f32[512,512]{1,0:T(8,128)S(1)}, f32[512,512]{1,0:T(8,128)S(1)}) custom-call(bf16[512,512]{1,0:T(8,128)(2,1)S(1)} %conv2.1.refs_2_.refs_0_, bf16[2,256,256]{2,1,0:T(8,128)(2,1)S(1)} %get-tuple-element.46.refs_1_.refs_2_, bf16[256,128]{1,0:T(8,128)(2,1)S(1)} %get-tuple-element.47.refs_2_.refs_3_, ...), custom_call_target="tpu_custom_call" | custom-call | tf_op jit(solution)/shard_map/local1024/pallas_call | solution.py:584
  18.4 0.7 %local1536.1 = (f32[512,512]{1,0:T(8,128)S(1)}, f32[512,512]{1,0:T(8,128)S(1)}) custom-call(bf16[512,512]{1,0:T(8,128)(2,1)S(1)} %conv3.1.refs_2_.refs_0_, bf16[2,256,256]{2,1,0:T(8,128)(2,1)S(1)} %get-tuple-element.46.refs_1_.refs_2_, bf16[256,128]{1,0:T(8,128)(2,1)S(1)} %get-tuple-element.47.refs_2_.refs_3_, ...), custom_call_target="tpu_custom_call" | custom-call | tf_op jit(solution)/shard_map/local1536/pallas_call | solution.py:584
  19.1 1.9 %collective-permute-done.3.rim_ref.state_ref = bf16[136,1024]{1,0:T(8,128)(2,1)S(1)} collective-permute-done((bf16[136,1024]{1,0:T(8,128)(2,1)S(1)}, bf16[136,1024]{1,0:T(8,128)(2,1)S(1)}, u32[]{:S(2)}, u32[]{:S(2)}) %collective-permute-start.3) | collective-permute-done | bytes 278560 | tf_op jit(solution)/shard_map/ppermute | solution.py:25
  21.0 0.3 %fix.1 = (bf16[512,256]{1,0:T(8,128)(2,1)S(1)}, bf16[16,2048]{1,0:T(8,128)(2,1)S(1)}) custom-call(bf16[512,2048]{1,0:T(8,128)(2,1)S(1)} %get-tuple-element.34.x_ref.refs_6_, bf16[136,1024]{1,0:T(8,128)(2,1)S(1)} %collective-permute-done.3.rim_ref.state_ref, bf16[4,2048]{1,0:T(4,128)(2,1)S(1)} %get-tuple-element.35.taps_ref, ...), custom_call_target="tpu_custom_call" | custom-call | tf_op jit(solution)/shard_map/fix/pallas_call | solution.py:549
  21.4 1.6 %final0.1.refs_0_ = bf16[512,2048]{1,0:T(8,128)(2,1)} custom-call(bf16[136,1024]{1,0:T(8,128)(2,1)S(1)} %collective-permute-done.3.rim_ref.state_ref, bf16[16,2048]{1,0:T(8,128)(2,1)S(1)} %get-tuple-element.45.edge_ref, f32[512,1024]{1,0:T(8,128)S(1)} %get-tuple-element.55.y_ref, f32[512,1024]{1,0:T(8,128)S(1)} %get-tuple-element.56.dec_ref, ...), custom_call_target="tpu_custom_call" | custom-call | tf_op jit(solution)/shard_map/final0/pallas_call | solution.py:597
  22.9 0.9 %collective-permute-done.4.state_ref = bf16[128,512]{1,0:T(8,128)(2,1)S(1)} collective-permute-done((bf16[128,512]{1,0:T(8,128)(2,1)S(1)}, bf16[128,512]{1,0:T(8,128)(2,1)S(1)}, u32[]{:S(2)}, u32[]{:S(2)}) %collective-permute-start.4) | collective-permute-done | bytes 131104 | tf_op jit(solution)/shard_map/ppermute | solution.py:25
  23.8 1.2 %final1024.1.refs_0_ = bf16[512,2048]{1,0:T(8,128)(2,1)} custom-call(bf16[128,512]{1,0:T(8,128)(2,1)S(1)} %collective-permute-done.4.state_ref, bf16[16,2048]{1,0:T(8,128)(2,1)S(1)} %get-tuple-element.45.edge_ref, f32[512,512]{1,0:T(8,128)S(1)} %get-tuple-element.53.y_ref, f32[512,512]{1,0:T(8,128)S(1)} %get-tuple-element.54.dec_ref, ...), custom_call_target="tpu_custom_call", output_to_operand_aliasing={{}: (6, {})} | custom-call | tf_op jit(solution)/shard_map/final1024/pallas_call | solution.py:597
  25.1 1.1 %collective-permute-done.2.state_ref = bf16[128,512]{1,0:T(8,128)(2,1)S(1)} collective-permute-done((bf16[128,512]{1,0:T(8,128)(2,1)S(1)}, bf16[128,512]{1,0:T(8,128)(2,1)S(1)}, u32[]{:S(2)}, u32[]{:S(2)}) %collective-permute-start.2) | collective-permute-done | bytes 131104 | tf_op jit(solution)/shard_map/ppermute | solution.py:25
  26.2 1.3 %final1536.1 = bf16[512,2048]{1,0:T(8,128)(2,1)} custom-call(bf16[128,512]{1,0:T(8,128)(2,1)S(1)} %collective-permute-done.2.state_ref, bf16[16,2048]{1,0:T(8,128)(2,1)S(1)} %get-tuple-element.45.edge_ref, f32[512,512]{1,0:T(8,128)S(1)} %get-tuple-element.50.y_ref, f32[512,512]{1,0:T(8,128)S(1)} %get-tuple-element.51.dec_ref, ...), custom_call_target="tpu_custom_call", output_to_operand_aliasing={{}: (6, {})} | custom-call | tf_op jit(solution)/shard_map/final1536/pallas_call | solution.py:597
  (10 shorter events, 0.4 us)
Async XLA Ops:
  1.4 5.6 %collective-permute-start = (bf16[72,512]{1,0:T(8,128)(2,1)S(1)}, bf16[72,512]{1,0:T(8,128)(2,1)S(1)}, u32[]{:S(2)}, u32[]{:S(2)}) collective-permute-start(bf16[72,512]{1,0:T(8,128)(2,1)S(1)} %get-tuple-element.38.refs_0_), channel_id=1, source_target_pairs={{0,2},{1,3},{2,0},{3,1},{4,6},{5,7},{6,4},{7,5},{8,10},{9,11},{10,... | collective-permute-start | bytes 221192 | tf_op jit(solution)/shard_map/ppermute | solution.py:30
  7.0 1.4 %collective-permute-start.1 = (bf16[144,512]{1,0:T(8,128)(2,1)S(1)}, bf16[144,512]{1,0:T(8,128)(2,1)S(1)}, u32[]{:S(2)}, u32[]{:S(2)}) collective-permute-start(bf16[144,512]{1,0:T(8,128)(2,1)S(1)} %constant_dynamic-update-slice_fusion.refs_0_), channel_id=1, source_target_pairs={{0,1},{1,0},{2,3},{3,2},{4,5},{5,4},{6,7},{7,6},{8,9},{9,8},{10,11... | collective-permute-start | bytes 442376 | tf_op jit(solution)/shard_map/ppermute | solution.py:30
  8.8 12.3 %collective-permute-start.3 = (bf16[136,1024]{1,0:T(8,128)(2,1)S(1)}, bf16[136,1024]{1,0:T(8,128)(2,1)S(1)}, u32[]{:S(2)}, u32[]{:S(2)}) collective-permute-start(bf16[136,1024]{1,0:T(8,128)(2,1)S(1)} %state0.1), channel_id=1, source_target_pairs={{0,4},{4,8},{8,12},{12,16},{16,20},{20,24},{24,28},{28,0},{1,5},{5... | collective-permute-start | bytes 835592 | tf_op jit(solution)/shard_map/ppermute | solution.py:25
  11.8 4.4 %copy-start.1 = (bf16[2048]{0:T(1024)(128)(2,1)S(1)}, bf16[2048]{0:T(1024)(128)(2,1)}, u32[]{:S(2)}) copy-start(bf16[2048]{0:T(1024)(128)(2,1)} %param.16) | copy-start | bytes 12292
  11.8 4.7 %copy-start = (bf16[512,2048]{1,0:T(8,128)(2,1)S(1)}, bf16[512,2048]{1,0:T(8,128)(2,1)}, u32[]{:S(2)}) copy-start(bf16[512,2048]{1,0:T(8,128)(2,1)} %refs_7_.1) | copy-start | bytes 6291460
  11.8 12.0 %collective-permute-start.4 = (bf16[128,512]{1,0:T(8,128)(2,1)S(1)}, bf16[128,512]{1,0:T(8,128)(2,1)S(1)}, u32[]{:S(2)}, u32[]{:S(2)}) collective-permute-start(bf16[128,512]{1,0:T(8,128)(2,1)S(1)} %state1024.1), channel_id=1, source_target_pairs={{0,4},{4,8},{8,12},{12,16},{16,20},{20,24},{24,28},{28,0},{1,5},{5... | collective-permute-start | bytes 393224 | tf_op jit(solution)/shard_map/ppermute | solution.py:25
  14.6 11.6 %collective-permute-start.2 = (bf16[128,512]{1,0:T(8,128)(2,1)S(1)}, bf16[128,512]{1,0:T(8,128)(2,1)S(1)}, u32[]{:S(2)}, u32[]{:S(2)}) collective-permute-start(bf16[128,512]{1,0:T(8,128)(2,1)S(1)} %state1536.1), channel_id=1, source_target_pairs={{0,4},{4,8},{8,12},{12,16},{16,20},{20,24},{24,28},{28,0},{1,5},{5... | collective-permute-start | bytes 393224 | tf_op jit(solution)/shard_map/ppermute | solution.py:25
